TPU v7x, 32 devices: a whole 2x2x4 slice. The times are simulated.
32 devices in a mesh: dp: 4 (over y, x), fsdp: 8 (over z, core).
Axes of the slice: x: 2, y: 2, z: 4, core: 2. Of those that a mesh axis runs over, the one named last changes fastest.
Arguments:
- triplane: bfloat16 [8, 1024, 1024], P('dp', 'fsdp'), may hold values from -6 to 6
- image_tokens: bfloat16 [8, 4096, 1024], P('dp', 'fsdp'), may hold values from -6 to 6
- camera: float32 [8, 16], P('dp'), may hold values from -4 to 4
- view_tokens: int32 [8], P('dp'), may hold values from 1024 to 4096, as said below
- master: float32 [16, 1024, 1024], P('dp', 'fsdp'), may hold values from -0.1875 to 0.1875
- moment1: float32 [16, 1024, 1024], P('dp', 'fsdp'), may hold values from -162.9174 to 162.9174
- moment2: float32 [16, 1024, 1024], P('dp', 'fsdp'), may hold values from 819.2 to 3276.8
- tile_slots: int32 [16], replicated, may hold values from 0 to 15, each once
- modulation: float32 [17, 9216], P(None, ('dp', 'fsdp')), may hold values from -0.9 to 0.9
- mod_moment1: float32 [17, 9216], P(None, ('dp', 'fsdp')), may hold values from -162.9174 to 162.9174
- mod_moment2: float32 [17, 9216], P(None, ('dp', 'fsdp')), may hold values from 819.2 to 3276.8
- cotangent: bfloat16 [8, 1024, 1024], P('dp', 'fsdp'), may hold values from -6 to 6
Outputs:
- block_output: bfloat16 [8, 1024, 1024], P('dp', 'fsdp')
- grad_triplane: float32 [8, 1024, 1024], P('dp', 'fsdp')
- grad_image: float32 [8, 4096, 1024], P('dp', 'fsdp')
- new_master: float32 [16, 1024, 1024], P('dp', 'fsdp')
- new_moment1: float32 [16, 1024, 1024], P('dp', 'fsdp')
- new_moment2: float32 [16, 1024, 1024], P('dp', 'fsdp')
- master_copy: bfloat16 [16, 1024, 1024], P('dp', 'fsdp')
- new_modulation: float32 [17, 9216], P(None, ('dp', 'fsdp'))
- new_mod_moment1: float32 [17, 9216], P(None, ('dp', 'fsdp'))
- new_mod_moment2: float32 [17, 9216], P(None, ('dp', 'fsdp'))
Inputs may be any that keep to these rules, and one draw needn't show every extreme that they name: `view_tokens`: each is a whole multiple of 1024. `tile_slots`: every slot is named by exactly one tile.
All inputs are finite; a program needn't handle non-finite values.
Results may differ from a plain program's by a relative error of at most 0.035.
The roundings to bfloat16 on the way count: a program that leaves them out, or rounds other values in their place, can miss the bound.
Values may be sent and summed in bfloat16 or wider, within the bound.
A program may use at most 384 MiB of HBM per device.

v0:
```python
import jax
import jax.numpy as jnp
from jax import lax
from jax.sharding import PartitionSpec as P

HD = 64
STEP = 5


HIGHEST = lax.Precision.HIGHEST
NEGATIVE = -1e30
BETA_ONE = 0.5
BETA_TWO = 0.5
EPSILON = 1e-08
WEIGHT_DECAY = 0.01
RATE_TILES = 0.03
RATE_MODULATION = 0.15


def contract(form, left, right):
    return jnp.einsum(form, left, right, preferred_element_type=jnp.float32)


def layer_norm(values):
    center = values - jnp.mean(values, axis=-1, keepdims=True)
    spread = jnp.mean(center * center, axis=-1, keepdims=True)
    return center * lax.rsqrt(spread + 1e-06)


def modulate(values, shift, scale):
    return layer_norm(values) * (1.0 + scale) + shift


def modulate_back(values, shift, scale, grad_normed):
    unused, pull = jax.vjp(modulate, values, shift, scale)
    return pull(grad_normed)


def gelu_tanh(values):
    return jax.nn.gelu(values, approximate=True)


def fetch_weights(master, modulation):
    narrow = master.astype(jnp.bfloat16)
    mod_narrow = modulation.astype(jnp.bfloat16)
    mod_narrow = mod_narrow.reshape(mod_narrow.shape[0], 1, 1, mod_narrow.shape[1])
    row_blocks, mod_blocks = (
        lax.all_gather(narrow, "fsdp", axis=1, tiled=True),
        lax.all_gather(mod_narrow, "fsdp", axis=2, tiled=True),
    )
    gathered, mod_all = (
        lax.all_gather(row_blocks, "dp", axis=0, tiled=True),
        lax.all_gather(mod_blocks, "dp", axis=1, tiled=True),
    )
    return (gathered, mod_all.reshape(mod_all.shape[0], -1))


def pick_tiles(gathered, tile_slots, start_tile, amount):
    return jnp.stack(
        [
            lax.dynamic_index_in_dim(gathered, tile_slots[start_tile + offset], 0, keepdims=False)
            for offset in range(amount)
        ]
    )


def tile_groups(gathered, tile_slots):
    return (
        pick_tiles(gathered, tile_slots, 0, 3),
        pick_tiles(gathered, tile_slots, 3, 1)[0],
        pick_tiles(gathered, tile_slots, 4, 1)[0],
        pick_tiles(gathered, tile_slots, 5, 2),
        pick_tiles(gathered, tile_slots, 7, 1)[0],
        pick_tiles(gathered, tile_slots, 8, 4),
        pick_tiles(gathered, tile_slots, 12, 4),
    )


def split_heads(pieces):
    return lax.all_to_all(pieces, "fsdp", split_axis=3, concat_axis=1, tiled=True)


def merge_heads(pieces):
    return lax.all_to_all(pieces, "fsdp", split_axis=1, concat_axis=3, tiled=True)


def masked_scores(queries, key_rows, key_mask):
    scores = contract("lhe,she->hls", queries, key_rows) * 0.125
    return jnp.where(key_mask[None, None, :], scores, NEGATIVE)


def attend_forward(pieces):
    queries, key_rows, value_rows, key_mask = pieces
    scores = masked_scores(queries, key_rows, key_mask)
    highest = jnp.max(scores, axis=-1, keepdims=True)
    weights_exp = jnp.exp(scores - highest)
    totals = jnp.sum(weights_exp, axis=-1, keepdims=True)
    probs_low = (weights_exp / totals).astype(jnp.bfloat16)
    result = contract("hls,she->lhe", probs_low, value_rows)
    return (result.astype(jnp.bfloat16), (highest + jnp.log(totals))[..., 0])


def attend_backward(pieces):
    queries, key_rows, value_rows, key_mask, logsum, grad_result = pieces
    scores = masked_scores(queries, key_rows, key_mask)
    probs = jnp.exp(scores - logsum[..., None])
    grad_probs = contract("lhe,she->hls", grad_result, value_rows)
    row_terms = jnp.sum(grad_probs * probs, axis=-1, keepdims=True)
    grad_scores = (probs * (grad_probs - row_terms)).astype(jnp.bfloat16)
    grad_queries = contract("hls,she->lhe", grad_scores, key_rows) * 0.125
    grad_keys = contract("hls,lhe->she", grad_scores, queries) * 0.125
    grad_values = contract("hls,lhe->she", probs.astype(jnp.bfloat16), grad_result)
    return (
        grad_queries.astype(jnp.bfloat16),
        grad_keys.astype(jnp.bfloat16),
        grad_values.astype(jnp.bfloat16),
    )


def adamw(weights, grads, first, second, rate):
    first_new = BETA_ONE * first + (1.0 - BETA_ONE) * grads
    second_new = BETA_TWO * second + (1.0 - BETA_TWO) * grads * grads
    first_hat = first_new / (1.0 - BETA_ONE**STEP)
    second_hat = second_new / (1.0 - BETA_TWO**STEP)
    weights_new = weights - rate * (
        first_hat / (jnp.sqrt(second_hat) + EPSILON) + WEIGHT_DECAY * weights
    )
    return (weights_new, first_new, second_new)


def shards(
    triplane,
    image_tokens,
    camera,
    view_tokens,
    master,
    moment1,
    moment2,
    tile_slots,
    modulation,
    mod_moment1,
    mod_moment2,
    cotangent,
):
    objects, tri_local, model_width = triplane.shape
    img_local = image_tokens.shape[1]
    groups = lax.axis_size("fsdp")
    owners = lax.axis_size("dp")
    tri_total = tri_local * groups
    img_total = img_local * groups
    head_width = model_width // groups
    heads_here = head_width // HD
    tile_count = master.shape[0] * owners
    gathered, mod_all = fetch_weights(master, modulation)
    mod_full = mod_all.astype(jnp.float32)
    modulations = (
        jnp.dot(camera, mod_full[:-1], precision=HIGHEST, preferred_element_type=jnp.float32)
        + mod_full[-1]
    )
    blocks = [
        modulations[:, position * model_width : (position + 1) * model_width][:, None, :]
        for position in range(9)
    ]
    tiles_qkv, tile_out_one, tile_query_two, tiles_pair, tile_out_two, tiles_up, tiles_down = (
        tile_groups(gathered, tile_slots)
    )
    residual_in = triplane.astype(jnp.float32)
    normed_one = modulate(residual_in, blocks[0], blocks[1]).astype(jnp.bfloat16)
    triples = contract("otd,kde->otke", normed_one, tiles_qkv).astype(jnp.bfloat16)
    triple_heads = split_heads(triples.reshape(objects, tri_local, 3, groups, head_width))
    self_query = triple_heads[:, :, 0, 0].reshape(objects, tri_total, heads_here, HD)
    self_keys = triple_heads[:, :, 1, 0].reshape(objects, tri_total, heads_here, HD)
    self_values = triple_heads[:, :, 2, 0].reshape(objects, tri_total, heads_here, HD)
    every_key = jnp.ones((objects, tri_total), dtype=bool)
    self_result, self_logsum = lax.map(
        attend_forward, (self_query, self_keys, self_values, every_key)
    )
    merged_one = merge_heads(self_result.reshape(objects, tri_total, 1, 1, head_width)).reshape(
        objects, tri_local, model_width
    )
    branch_one = contract("otd,de->ote", merged_one, tile_out_one)
    residual_mid = residual_in + blocks[2] * branch_one
    normed_two = modulate(residual_mid, blocks[3], blocks[4]).astype(jnp.bfloat16)
    cross_query = contract("otd,de->ote", normed_two, tile_query_two).astype(jnp.bfloat16)
    image_pairs = contract("oid,kde->oike", image_tokens, tiles_pair).astype(jnp.bfloat16)
    query_heads, pair_heads = (
        lax.all_to_all(
            cross_query.reshape(objects, tri_local, 1, groups, head_width),
            "fsdp",
            split_axis=3,
            concat_axis=1,
            tiled=True,
        ),
        lax.all_to_all(
            image_pairs.reshape(objects, img_local, 2, groups, head_width),
            "fsdp",
            split_axis=3,
            concat_axis=1,
            tiled=True,
        ),
    )
    cross_queries = query_heads[:, :, 0, 0].reshape(objects, tri_total, heads_here, HD)
    cross_keys = pair_heads[:, :, 0, 0].reshape(objects, img_total, heads_here, HD)
    cross_values = pair_heads[:, :, 1, 0].reshape(objects, img_total, heads_here, HD)
    live_mask = lax.broadcasted_iota(jnp.int32, (objects, img_total), 1) < view_tokens[:, None]
    cross_result, cross_logsum = lax.map(
        attend_forward, (cross_queries, cross_keys, cross_values, live_mask)
    )
    merged_two = merge_heads(cross_result.reshape(objects, tri_total, 1, 1, head_width)).reshape(
        objects, tri_local, model_width
    )
    branch_two = contract("otd,de->ote", merged_two, tile_out_two)
    residual_late = residual_mid + blocks[5] * branch_two
    normed_three = modulate(residual_late, blocks[6], blocks[7]).astype(jnp.bfloat16)
    hidden_pre = contract("otd,kde->otke", normed_three, tiles_up)
    hidden = gelu_tanh(hidden_pre).astype(jnp.bfloat16)
    branch_three = contract("otkd,kde->ote", hidden, tiles_down)
    block_output = (residual_late + blocks[8] * branch_three).astype(jnp.bfloat16)
    gathered_back, unused_mod = fetch_weights(master, modulation)
    back_qkv, back_out_one, back_query_two, back_pair, back_out_two, back_up, back_down = (
        tile_groups(gathered_back, tile_slots)
    )
    grad_final = cotangent.astype(jnp.float32)
    grad_gate_three = jnp.sum(grad_final * branch_three, axis=1)
    grad_branch_three = (blocks[8] * grad_final).astype(jnp.bfloat16)
    grad_down = contract("otkd,ote->kde", hidden, grad_branch_three)
    grad_hidden = contract("ote,kde->otkd", grad_branch_three, back_down)
    unused_gelu, gelu_pull = jax.vjp(gelu_tanh, hidden_pre)
    grad_pre = gelu_pull(grad_hidden)[0].astype(jnp.bfloat16)
    grad_up = contract("otd,otke->kde", normed_three, grad_pre)
    grad_normed_three = contract("otke,kde->otd", grad_pre, back_up)
    grad_late_norm, grad_shift_three, grad_scale_three = modulate_back(
        residual_late, blocks[6], blocks[7], grad_normed_three
    )
    grad_late = grad_final + grad_late_norm
    grad_gate_two = jnp.sum(grad_late * branch_two, axis=1)
    grad_branch_two = (blocks[5] * grad_late).astype(jnp.bfloat16)
    grad_out_two = contract("otd,ote->de", merged_two, grad_branch_two)
    grad_merged_two = contract("ote,de->otd", grad_branch_two, back_out_two).astype(jnp.bfloat16)
    grad_cross_heads = split_heads(
        grad_merged_two.reshape(objects, tri_local, 1, groups, head_width)
    )
    grad_cross_heads = grad_cross_heads.reshape(objects, tri_total, heads_here, HD)
    cross_grad_query, cross_grad_keys, cross_grad_values = lax.map(
        attend_backward,
        (cross_queries, cross_keys, cross_values, live_mask, cross_logsum, grad_cross_heads),
    )
    grad_pair_heads = jnp.stack([cross_grad_keys, cross_grad_values], axis=2).reshape(
        objects, img_total, 2, 1, head_width
    )
    grad_query_two, grad_pairs = (
        lax.all_to_all(
            cross_grad_query.reshape(objects, tri_total, 1, 1, head_width),
            "fsdp",
            split_axis=1,
            concat_axis=3,
            tiled=True,
        ),
        lax.all_to_all(grad_pair_heads, "fsdp", split_axis=1, concat_axis=3, tiled=True),
    )
    grad_query_two = grad_query_two.reshape(objects, tri_local, model_width)
    grad_pairs = grad_pairs.reshape(objects, img_local, 2, model_width)
    grad_tile_query = contract("otd,ote->de", normed_two, grad_query_two)
    grad_tiles_pair = contract("oid,oike->kde", image_tokens, grad_pairs)
    grad_image = contract("oike,kde->oid", grad_pairs, back_pair)
    grad_normed_two = contract("ote,de->otd", grad_query_two, back_query_two)
    grad_mid_norm, grad_shift_two, grad_scale_two = modulate_back(
        residual_mid, blocks[3], blocks[4], grad_normed_two
    )
    grad_mid = grad_late + grad_mid_norm
    grad_gate_one = jnp.sum(grad_mid * branch_one, axis=1)
    grad_branch_one = (blocks[2] * grad_mid).astype(jnp.bfloat16)
    grad_out_one = contract("otd,ote->de", merged_one, grad_branch_one)
    grad_merged_one = contract("ote,de->otd", grad_branch_one, back_out_one).astype(jnp.bfloat16)
    grad_self_heads = split_heads(
        grad_merged_one.reshape(objects, tri_local, 1, groups, head_width)
    )
    grad_self_heads = grad_self_heads.reshape(objects, tri_total, heads_here, HD)
    self_grad_query, self_grad_keys, self_grad_values = lax.map(
        attend_backward,
        (self_query, self_keys, self_values, every_key, self_logsum, grad_self_heads),
    )
    grad_triple_heads = jnp.stack([self_grad_query, self_grad_keys, self_grad_values], axis=2)
    grad_triples = merge_heads(grad_triple_heads.reshape(objects, tri_total, 3, 1, head_width))
    grad_triples = grad_triples.reshape(objects, tri_local, 3, model_width)
    grad_qkv = contract("otd,otke->kde", normed_one, grad_triples)
    grad_normed_one = contract("otke,kde->otd", grad_triples, back_qkv)
    grad_in_norm, grad_shift_one, grad_scale_one = modulate_back(
        residual_in, blocks[0], blocks[1], grad_normed_one
    )
    grad_triplane = grad_mid + grad_in_norm
    grad_mods = jnp.concatenate(
        [
            grad_shift_one[:, 0],
            grad_scale_one[:, 0],
            grad_gate_one,
            grad_shift_two[:, 0],
            grad_scale_two[:, 0],
            grad_gate_two,
            grad_shift_three[:, 0],
            grad_scale_three[:, 0],
            grad_gate_three,
        ],
        axis=-1,
    )
    grad_mod_rows = jnp.dot(
        camera.T, grad_mods, precision=HIGHEST, preferred_element_type=jnp.float32
    )
    grad_modulation = jnp.concatenate(
        [grad_mod_rows, jnp.sum(grad_mods, axis=0, keepdims=True)], axis=0
    )
    mod_columns = modulation.shape[1]
    grad_mod_blocks = grad_modulation.reshape(grad_modulation.shape[0], owners, groups, mod_columns)
    logical = [
        grad_qkv[0],
        grad_qkv[1],
        grad_qkv[2],
        grad_out_one,
        grad_tile_query,
        grad_tiles_pair[0],
        grad_tiles_pair[1],
        grad_out_two,
        grad_up[0],
        grad_up[1],
        grad_up[2],
        grad_up[3],
        grad_down[0],
        grad_down[1],
        grad_down[2],
        grad_down[3],
    ]
    slot_grads = jnp.zeros((tile_count, model_width, model_width), jnp.float32)
    for position in range(tile_count):
        slot_grads = lax.dynamic_update_index_in_dim(
            slot_grads, logical[position], tile_slots[position], 0
        )
    row_sums, mod_row_sums = (
        lax.psum_scatter(
            slot_grads.astype(jnp.bfloat16), "fsdp", scatter_dimension=1, tiled=True
        ).astype(jnp.float32),
        lax.psum_scatter(
            grad_mod_blocks.astype(jnp.bfloat16), "fsdp", scatter_dimension=2, tiled=True
        ).astype(jnp.float32),
    )
    tile_grad, mod_grad = (
        lax.psum_scatter(
            row_sums.astype(jnp.bfloat16), "dp", scatter_dimension=0, tiled=True
        ).astype(jnp.float32),
        lax.psum_scatter(
            mod_row_sums.astype(jnp.bfloat16), "dp", scatter_dimension=1, tiled=True
        ).astype(jnp.float32),
    )
    mod_grad = mod_grad.reshape(mod_grad.shape[0], mod_columns)
    new_master, new_moment1, new_moment2 = adamw(master, tile_grad, moment1, moment2, RATE_TILES)
    new_modulation, new_mod_moment1, new_mod_moment2 = adamw(
        modulation, mod_grad, mod_moment1, mod_moment2, RATE_MODULATION
    )
    return (
        block_output,
        grad_triplane,
        grad_image,
        new_master,
        new_moment1,
        new_moment2,
        new_master.astype(jnp.bfloat16),
        new_modulation,
        new_mod_moment1,
        new_mod_moment2,
    )


def solution(mesh):
    in_specs = (
        P("dp", "fsdp", None),
        P("dp", "fsdp", None),
        P("dp", None),
        P("dp"),
        P("dp", "fsdp", None),
        P("dp", "fsdp", None),
        P("dp", "fsdp", None),
        P(),
        P(None, ("dp", "fsdp")),
        P(None, ("dp", "fsdp")),
        P(None, ("dp", "fsdp")),
        P("dp", "fsdp", None),
    )
    out_specs = (
        P("dp", "fsdp", None),
        P("dp", "fsdp", None),
        P("dp", "fsdp", None),
        P("dp", "fsdp", None),
        P("dp", "fsdp", None),
        P("dp", "fsdp", None),
        P("dp", "fsdp", None),
        P(None, ("dp", "fsdp")),
        P(None, ("dp", "fsdp")),
        P(None, ("dp", "fsdp")),
    )
    return jax.shard_map(shards, mesh=mesh, in_specs=in_specs, out_specs=out_specs, check_vma=False)
```

profile of v0, /device:TPU:0, one launch (start us, length us, event | category | flops | bytes accessed | tf_op | source)
XLA Modules:
  0.0 1725.0 jit_solution(6739558012118976788)
XLA Ops:
  10.2 84.9 %all-gather.5.cloned.1.call-done = bf16[4,1024,1024]{2,1,0:T(8,128)(2,1)} async-done(((bf16[4,128,1024]{2,1,0:T(8,128)(2,1)}), bf16[4,1024,1024]{2,1,0:T(8,128)(2,1)}) %all-gather.5.cloned.1.call-update) | async-done | bytes 8388624 | tf_op jit(solution)/shard_map/all_gather | solution.py:48
  113.4 14.0 all-gather.1
  127.7 16.4 all_gather.15
  156.3 239.5 %all-gather.7.cloned.1.call-done = bf16[16,1024,1024]{2,1,0:T(8,128)(2,1)} async-done(((bf16[4,1024,1024]{2,1,0:T(8,128)(2,1)}), bf16[16,1024,1024]{2,1,0:T(8,128)(2,1)}) %all-gather.7.cloned.1.call-update) | async-done | bytes 33554448 | tf_op jit(solution)/shard_map/all_gather | solution.py:52
  395.8 18.4 %constant_dynamic-slice_fusion.7 = (bf16[1,1024,1024]{2,1,0:T(8,128)(2,1)}, bf16[1,1024,1024]{2,1,0:T(8,128)(2,1)}, bf16[1,1024,1024]{2,1,0:T(8,128)(2,1)}, bf16...) fusion(bf16[16,1024,1024]{2,1,0:T(8,128)(2,1)} %all-gather.7.cl, ...), kind=kLoop, calls=%fused_computation.279 | loop fusion | bytes 54526004 | tf_op jit(solution)/shard_map/jit(dynamic_index_in_dim)/dynamic_slice | solution.py:61
  414.3 4.8 fusion.164
  420.7 4.9 all-to-all-start
  425.5 37.8 %all-to-all-done = bf16[2,128,3,8,128]{4,1,2,0,3:T(8,128)(2,1)} async-done(((bf16[2,128,3,8,128]{4,1,2,0,3:T(8,128)(2,1)}), bf16[2,128,3,8,128]{4,1,2,0,3:T(8,128)(2,1)}, u32[]{:S(2)}, u32[]{:S(2)}) %all-to-all-start) | async-done | bytes 1572896 | tf_op jit(solution)/shard_map/all_to_all | solution.py:80
  469.1 10.4 while.52
  481.9 4.1 all-to-all-start.1
  489.7 11.6 all-to-all-done.1
  525.0 8.3 fusion.132
  533.3 6.4 copy.274
  539.8 5.6 all-to-all-start.2
  546.0 93.4 %all-to-all-done.2 = bf16[2,512,2,8,128]{4,1,2,0,3:T(8,128)(2,1)} async-done(((bf16[2,512,2,8,128]{4,1,2,0,3:T(8,128)(2,1)}), bf16[2,512,2,8,128]{4,1,2,0,3:T(8,128)(2,1)}, u32[]{:S(2)}, u32[]{:S(2)}) %all-to-all-start.2) | async-done | bytes 4194336 | tf_op jit(solution)/shard_map/all_to_all | solution.py:194
  644.1 4.1 copy.276
  652.4 89.1 %while.53 = (s32[]{:T(128)}, bf16[2,1024,2,64]{1,3,2,0:T(8,128)(2,1)S(1)}, f32[2,2,1024]{2,1,0:T(2,128)S(1)}, bf16[2,4096,2,64]{1,3,2,0:T(8,128)(2,1)}, pred[2,4...) while((s32[]{:T(128)}, ...), condition=%wide.region_11.12_spmd, body=%wide.region_8.11_spmd.sunk | while | flops 2248275968 | bytes 103372888 | solution.py:206
  652.5 14.8 fusion.285
  667.3 14.7 fusion.286
  682.0 14.9 fusion.287
  697.0 14.8 fusion.285
  711.9 14.7 fusion.286
  726.6 14.9 fusion.287
  748.2 13.3 all-to-all-done.4
  768.5 4.2 fusion.129
  772.8 5.2 fusion.121
  790.0 15.2 all-to-all-done.5
  808.5 204.9 %while.54 = (s32[]{:T(128)}, bf16[2,1024,2,64]{1,3,2,0:T(8,128)(2,1)}, bf16[2,4096,2,64]{1,3,2,0:T(8,128)(2,1)}, bf16[2,4096,2,64]{1,3,2,0:T(8,128)(2,1)}, bf16[...) while((s32[]{:T(128)}, ...), condition=%wide.region_18.19_spmd, body=%wide.region_16.18_spmd.sunk | while | flops 5496371200 | bytes 266683536 | solution.py:244
  808.9 14.6 fusion.296
  823.6 22.9 %multiply_reduce_fusion.15 = (f32[2,1024]{1,0:T(2,128)S(1)}, f32[2,1024,4096]{2,1,0:T(8,128)}) fusion(f32[2,1024,4096]{2,1,0:T(8,128)} %fusion.296, f32[2,1024]{1,0:T(2,128)S(1)} %dynamic-slice_bitcast_fusion.4, pred[4096]{0:T(1024)(128)(4,1)S(1)} %dynamic-slice_reduce_fusion.5, bf16[2,4096,2,64]{1,3,2,0:T(8,128)(2,1)S(1)} %copy-done.8, ...), kind=kOutput, calls=%fused_computation.81.clone.1 | convolution fusion | flops 1115682816 | bytes 68441088 | tf_op jit(solution)/shard_map/while/body/eval_jaxpr/lhe,she->hls/dot_general | solution.py:21
  846.5 27.6 %multiply_convert_fusion.11 = bf16[2,1024,4096]{2,1,0:T(8,128)(2,1)} fusion(f32[2,1024,4096]{2,1,0:T(8,128)} %get-tuple-element.585, f32[2,1024,4096]{2,1,0:T(8,128)} %fusion.296, f32[2,1024]{1,0:T(2,128)S(1)} %get-tuple-element.586, f32[2,1024]{1,0:T(2,128)S(1)} %dynamic-slice_bitcast_fusion.4, pred[4096]{0:T(1024)(128)(4,1)S(1)} %dynamic-slice_reduce_fusion.5), kind=kLoop, calls=%fused_computation.80.clone.1 | loop fusion | flops 50331648 | bytes 83906560 | tf_op jit(solution)/shard_map/while/body/eval_jaxpr/convert_element_type | solution.py:109
  874.0 9.8 fusion.298
  883.8 12.0 fusion.297
  895.8 15.3 fusion.299
  911.1 14.6 fusion.296
  925.7 22.9 %multiply_reduce_fusion.15 = (f32[2,1024]{1,0:T(2,128)S(1)}, f32[2,1024,4096]{2,1,0:T(8,128)}) fusion(f32[2,1024,4096]{2,1,0:T(8,128)} %fusion.296, f32[2,1024]{1,0:T(2,128)S(1)} %dynamic-slice_bitcast_fusion.4, pred[4096]{0:T(1024)(128)(4,1)S(1)} %dynamic-slice_reduce_fusion.5, bf16[2,4096,2,64]{1,3,2,0:T(8,128)(2,1)S(1)} %copy-done.8, ...), kind=kOutput, calls=%fused_computation.81.clone.1 | convolution fusion | flops 1115682816 | bytes 68441088 | tf_op jit(solution)/shard_map/while/body/eval_jaxpr/lhe,she->hls/dot_general | solution.py:21
  948.7 27.6 %multiply_convert_fusion.11 = bf16[2,1024,4096]{2,1,0:T(8,128)(2,1)} fusion(f32[2,1024,4096]{2,1,0:T(8,128)} %get-tuple-element.585, f32[2,1024,4096]{2,1,0:T(8,128)} %fusion.296, f32[2,1024]{1,0:T(2,128)S(1)} %get-tuple-element.586, f32[2,1024]{1,0:T(2,128)S(1)} %dynamic-slice_bitcast_fusion.4, pred[4096]{0:T(1024)(128)(4,1)S(1)} %dynamic-slice_reduce_fusion.5), kind=kLoop, calls=%fused_computation.80.clone.1 | loop fusion | flops 50331648 | bytes 83906560 | tf_op jit(solution)/shard_map/while/body/eval_jaxpr/convert_element_type | solution.py:109
  976.2 9.8 fusion.298
  986.0 12.0 fusion.297
  998.0 15.2 fusion.299
  1015.5 18.7 %all_to_all.156 = bf16[2,1024,1,1,128]{4,0,3,2,1:T(2,128)(2,1)S(1)} all-to-all(bf16[2,1024,1,1,128]{4,0,3,2,1:T(2,128)(2,1)} %copy.285), channel_id=1, replica_groups=mesh['dp'=4,'fsdp'=8] {'fsdp'}, dimensions={1} | all-to-all | bytes 1048576 | tf_op jit(solution)/shard_map/all_to_all | solution.py:252
  1041.2 8.3 fusion.185
  1053.1 18.5 %all_to_all.157 = bf16[2,128,1,8,128]{4,1,0,2,3:T(8,128)(2,1)} all-to-all(bf16[2,128,1,8,128]{4,1,0,2,3:T(8,128)(2,1)S(1)} %copy.288), channel_id=1, replica_groups=mesh['dp'=4,'fsdp'=8] {'fsdp'}, dimensions={3} | all-to-all | bytes 1048576 | tf_op jit(solution)/shard_map/all_to_all | solution.py:80
  1078.5 22.6 %while.55 = (s32[]{:T(128)}, bf16[2,1024,2,64]{1,3,2,0:T(8,128)(2,1)}, bf16[2,1024,2,64]{1,3,2,0:T(8,128)(2,1)}, bf16[2,1024,2,64]{1,3,2,0:T(8,128)(2,1)}, bf16[...) while((s32[]{:T(128)}, ...), condition=%wide.region_23.24_spmd, body=%wide.region_21.23_spmd.sunk | while | flops 1367996416 | bytes 78181648 | solution.py:279
  1103.7 5.0 copy.290
  1108.7 4.3 all-to-all-start.8
  1113.0 4.6 pad_maximum_fusion.1
  1117.6 11.1 copy.293
  1128.8 22.1 %all-to-all-done.8 = bf16[2,1024,3,1,128]{4,0,3,2,1:T(2,128)(2,1)} async-done(((bf16[2,1024,3,1,128]{4,0,3,2,1:T(2,128)(2,1)}), bf16[2,1024,3,1,128]{4,0,3,2,1:T(2,128)(2,1)}, u32[]{:S(2)}, u32[]{:S(2)}) %all-to-all-start.8) | async-done | bytes 1572896 | tf_op jit(solution)/shard_map/all_to_all | solution.py:84
  1150.8 4.6 all-to-all-start.9
  1155.5 4.1 convolution_bitcast_fusion.1
  1179.3 8.7 convolution_bitcast_fusion
  1195.6 4.9 fusion.183
  1223.4 11.0 broadcast_in_dim.152
  1244.3 9.4 all-to-all-done.9
  1256.4 4.7 copy.295
  1261.2 7.3 reshape.261
  1268.4 7.0 convolution_bitcast_fusion.3
  1281.8 4.1 copy.305
  1310.0 320.0 %reduce-scatter.6.cloned.1.call-done = bf16[16,128,1024]{2,1,0:T(8,128)(2,1)} async-done(((bf16[16,1024,1024]{2,1,0:T(8,128)(2,1)}), bf16[16,128,1024]{2,1,0:T(8,128)(2,1)}) %reduce-scatter.6.cloned.1.call-update) | async-done | bytes 4194320 | tf_op jit(solution)/shard_map/reduce_scatter | solution.py:338
  1632.9 22.2 %reduce-scatter.10.cloned.1.call-done = bf16[17,1,1,288]{3,0,2,1:T(8,128)(2,1)} async-done(((bf16[17,4,1,288]{3,0,2,1:T(8,128)(2,1)}), bf16[17,1,1,288]{3,0,2,1:T(8,128)(2,1)}) %reduce-scatter.10.cloned.1.call-update) | async-done | bytes 9808
  1656.5 9.9 fusion.135
  1666.4 44.1 %reduce-scatter.8.cloned.1.call-done = bf16[4,128,1024]{2,1,0:T(8,128)(2,1)} async-done(((bf16[16,128,1024]{2,1,0:T(8,128)(2,1)}), bf16[4,128,1024]{2,1,0:T(8,128)(2,1)}) %reduce-scatter.8.cloned.1.call-update) | async-done | bytes 1048592 | tf_op jit(solution)/shard_map/reduce_scatter | solution.py:346
  1710.6 7.3 fusion.216
  (421 shorter events, 229.8 us)
Async XLA Ops:
  7.2 517.8 %copy-start = (bf16[2,512,1024]{2,1,0:T(8,128)(2,1)S(1)}, bf16[2,512,1024]{2,1,0:T(8,128)(2,1)}, u32[]{:S(2)}) copy-start(bf16[2,512,1024]{2,1,0:T(8,128)(2,1)} %param.21) | copy-start | bytes 6291460
  7.2 87.8 %all-gather.5.cloned.1.call-start = ((), (), s32[]{:S(2)}) async-start(), calls=%async_computation.13 | async-start | bytes 9437184 | tf_op jit(solution)/shard_map/all_gather | solution.py:48
  10.1 385.7 %all-gather.7.cloned.1.call-start = ((), (), s32[]{:S(2)}) async-start(), calls=%async_computation.14 | async-start | bytes 41943040 | tf_op jit(solution)/shard_map/all_gather | solution.py:52
  95.0 18.3 %copy-start.59 = (f32[17,288]{1,0:T(8,128)S(1)}, f32[17,288]{1,0:T(8,128)}, u32[]{:S(2)}) copy-start(f32[17,288]{1,0:T(8,128)} %param.28) | copy-start | bytes 58756
  95.0 58.9 %copy-start.13 = (bf16[2,128,1024]{2,1,0:T(8,128)(2,1)S(1)}, bf16[2,128,1024]{2,1,0:T(8,128)(2,1)}, u32[]{:S(2)}) copy-start(bf16[2,128,1024]{2,1,0:T(8,128)(2,1)} %param.20) | copy-start | bytes 1572868
  95.1 59.3 %copy-start.100 = (f32[2,16]{1,0:T(2,128)S(1)}, f32[2,16]{1,0:T(2,128)}, u32[]{:S(2)}) copy-start(f32[2,16]{1,0:T(2,128)} %param.22) | copy-start | bytes 388
  154.1 260.2 %copy-start.81 = (f32[2,128]{1,0:T(2,128)}, f32[2,128]{1,0:T(2,128)S(1)}, u32[]{:S(2)}) copy-start(f32[2,128]{1,0:T(2,128)S(1)} %broadcast_multiply_fusion.2) | copy-start | bytes 3076
  154.4 259.9 %copy-start.83 = (f32[2,128]{1,0:T(2,128)}, f32[2,128]{1,0:T(2,128)S(1)}, u32[]{:S(2)}) copy-start(f32[2,128]{1,0:T(2,128)S(1)} %fusion.202) | copy-start | bytes 3076
  156.3 258.0 %copy-start.66 = (f32[2,1024]{1,0:T(2,128)}, f32[2,1024]{1,0:T(2,128)S(1)}, u32[]{:S(2)}) copy-start(f32[2,1024]{1,0:T(2,128)S(1)} %get-tuple-element.361) | copy-start | bytes 24580
  156.3 258.0 %copy-start.77 = (f32[2,1024]{1,0:T(2,128)}, f32[2,1024]{1,0:T(2,128)S(1)}, u32[]{:S(2)}) copy-start(f32[2,1024]{1,0:T(2,128)S(1)} %get-tuple-element.360) | copy-start | bytes 24580
  156.3 349.4 %copy-start.61 = (f32[2,1024]{1,0:T(2,128)}, f32[2,1024]{1,0:T(2,128)S(1)}, u32[]{:S(2)}) copy-start(f32[2,1024]{1,0:T(2,128)S(1)} %get-tuple-element.362) | copy-start | bytes 24580
  156.3 353.3 %copy-start.54 = (f32[2,1024]{1,0:T(2,128)}, f32[2,1024]{1,0:T(2,128)S(1)}, u32[]{:S(2)}) copy-start(f32[2,1024]{1,0:T(2,128)S(1)} %get-tuple-element.358) | copy-start | bytes 24580
  156.3 353.3 %copy-start.75 = (f32[2,1024]{1,0:T(2,128)}, f32[2,1024]{1,0:T(2,128)S(1)}, u32[]{:S(2)}) copy-start(f32[2,1024]{1,0:T(2,128)S(1)} %get-tuple-element.357) | copy-start | bytes 24580
  420.7 42.7 %all-to-all-start = ((bf16[2,128,3,8,128]{4,1,2,0,3:T(8,128)(2,1)}), bf16[2,128,3,8,128]{4,1,2,0,3:T(8,128)(2,1)}, u32[]{:S(2)}, u32[]{:S(2)}) async-start(bf16[2,128,3,8,128]{4,1,2,0,3:T(8,128)(2,1)} %bitcast.501), calls=%async_computation | async-start | bytes 3145728 | tf_op jit(solution)/shard_map/all_to_all | solution.py:80
  479.6 29.6 %copy-start.1 = (bf16[2,1024,2,64]{1,3,2,0:T(8,128)(2,1)}, bf16[2,1024,2,64]{1,3,2,0:T(8,128)(2,1)S(1)}, u32[]{:S(2)}) copy-start(bf16[2,1024,2,64]{1,3,2,0:T(8,128)(2,1)S(1)} %get-tuple-element.716) | copy-start | bytes 1572868
  479.6 29.6 %copy-start.3 = (bf16[2,1024,2,64]{1,3,2,0:T(8,128)(2,1)}, bf16[2,1024,2,64]{1,3,2,0:T(8,128)(2,1)S(1)}, u32[]{:S(2)}) copy-start(bf16[2,1024,2,64]{1,3,2,0:T(8,128)(2,1)S(1)} %get-tuple-element.717) | copy-start | bytes 1572868
  479.6 29.6 %copy-start.57 = (f32[2,2,1024]{2,1,0:T(2,128)}, f32[2,2,1024]{2,1,0:T(2,128)S(1)}, u32[]{:S(2)}) copy-start(f32[2,2,1024]{2,1,0:T(2,128)S(1)} %get-tuple-element.682) | copy-start | bytes 49156
  481.9 19.5 %all-to-all-start.1 = ((bf16[2,1024,1,1,128]{4,0,3,2,1:T(2,128)(2,1)}), bf16[2,1024,1,1,128]{4,0,3,2,1:T(2,128)(2,1)}, u32[]{:S(2)}, u32[]{:S(2)}) async-start(bf16[2,1024,1,1,128]{4,0,3,2,1:T(2,128)(2,1)} %copy.269), calls=%async_computation.1 | async-start | bytes 1048576 | tf_op jit(solution)/shard_map/all_to_all | solution.py:84
  509.5 11.5 copy-start.89
  509.5 11.5 copy-start.91
  513.6 26.2 %all-to-all-start.3 = ((bf16[2,128,1,8,128]{4,1,0,2,3:T(8,128)(2,1)}), bf16[2,128,1,8,128]{4,1,0,2,3:T(8,128)(2,1)S(1)}, u32[]{:S(2)}, u32[]{:S(2)}) async-start(bf16[2,128,1,8,128]{4,1,0,2,3:T(8,128)(2,1)} %copy.277), calls=%async_computation.3 | async-start | bytes 1048576 | tf_op jit(solution)/shard_map/all_to_all | solution.py:187
  539.8 99.6 %all-to-all-start.2 = ((bf16[2,512,2,8,128]{4,1,2,0,3:T(8,128)(2,1)}), bf16[2,512,2,8,128]{4,1,2,0,3:T(8,128)(2,1)}, u32[]{:S(2)}, u32[]{:S(2)}) async-start(bf16[2,512,2,8,128]{4,1,2,0,3:T(8,128)(2,1)} %copy.274), calls=%async_computation.2 | async-start | bytes 8388608 | tf_op jit(solution)/shard_map/all_to_all | solution.py:194
  741.5 22.6 %copy-start.64 = (f32[2,1024]{1,0:T(2,128)S(1)}, f32[2,1024]{1,0:T(2,128)}, u32[]{:S(2)}) copy-start(f32[2,1024]{1,0:T(2,128)} %get-tuple-element.359) | copy-start | bytes 24580
  742.7 18.9 %all-to-all-start.4 = ((bf16[2,1024,1,1,128]{4,0,3,2,1:T(2,128)(2,1)}), bf16[2,1024,1,1,128]{4,0,3,2,1:T(2,128)(2,1)S(1)}, u32[]{:S(2)}, u32[]{:S(2)}) async-start(bf16[2,1024,1,1,128]{4,0,3,2,1:T(2,128)(2,1)} %copy.280), calls=%async_computation.4 | async-start | bytes 1048576 | tf_op jit(solution)/shard_map/all_to_all | solution.py:84
  764.1 8.6 copy-start.28
  768.0 13.3 copy-start.10
  768.0 13.3 copy-start.85
  768.2 13.1 copy-start.94
  786.5 18.8 %all-to-all-start.5 = ((bf16[2,128,1,8,128]{4,1,0,2,3:T(8,128)(2,1)}), bf16[2,128,1,8,128]{4,1,0,2,3:T(8,128)(2,1)S(1)}, u32[]{:S(2)}, u32[]{:S(2)}) async-start(bf16[2,128,1,8,128]{4,1,0,2,3:T(8,128)(2,1)} %copy.283), calls=%async_computation.5 | async-start | bytes 1048576 | tf_op jit(solution)/shard_map/all_to_all | solution.py:80
  808.9 14.7 copy-start.8
  911.1 14.7 copy-start.8
  1013.4 24.2 %copy-start.6 = (f32[2,128,1024]{2,1,0:T(8,128)S(1)}, f32[2,128,1024]{2,1,0:T(8,128)}, u32[]{:S(2)}) copy-start(f32[2,128,1024]{2,1,0:T(8,128)} %copy-done.5) | copy-start | bytes 3145732
  1013.4 24.2 %copy-start.55 = (f32[2,1024]{1,0:T(2,128)S(1)}, f32[2,1024]{1,0:T(2,128)}, u32[]{:S(2)}) copy-start(f32[2,1024]{1,0:T(2,128)} %copy-done.54) | copy-start | bytes 24580
  1013.4 24.2 %copy-start.73 = (f32[2,128]{1,0:T(2,128)S(1)}, f32[2,128]{1,0:T(2,128)}, u32[]{:S(2)}) copy-start(f32[2,128]{1,0:T(2,128)} %copy-done.72) | copy-start | bytes 3076
  1034.2 6.2 copy-start.90
  1034.2 6.2 copy-start.92
  1041.2 9.3 copy-start.62
  1052.9 25.6 %copy-start.2 = (bf16[2,1024,2,64]{1,3,2,0:T(8,128)(2,1)S(1)}, bf16[2,1024,2,64]{1,3,2,0:T(8,128)(2,1)}, u32[]{:S(2)}) copy-start(bf16[2,1024,2,64]{1,3,2,0:T(8,128)(2,1)} %copy-done.1) | copy-start | bytes 1572868
  1052.9 25.5 %copy-start.4 = (bf16[2,1024,2,64]{1,3,2,0:T(8,128)(2,1)S(1)}, bf16[2,1024,2,64]{1,3,2,0:T(8,128)(2,1)}, u32[]{:S(2)}) copy-start(bf16[2,1024,2,64]{1,3,2,0:T(8,128)(2,1)} %copy-done.3) | copy-start | bytes 1572868
  1052.9 25.5 %copy-start.58 = (f32[2,2,1024]{2,1,0:T(2,128)S(1)}, f32[2,2,1024]{2,1,0:T(2,128)}, u32[]{:S(2)}) copy-start(f32[2,2,1024]{2,1,0:T(2,128)} %copy-done.57) | copy-start | bytes 49156
  1108.7 42.1 %all-to-all-start.8 = ((bf16[2,1024,3,1,128]{4,0,3,2,1:T(2,128)(2,1)}), bf16[2,1024,3,1,128]{4,0,3,2,1:T(2,128)(2,1)}, u32[]{:S(2)}, u32[]{:S(2)}) async-start(bf16[2,1024,3,1,128]{4,0,3,2,1:T(2,128)(2,1)} %copy.290), calls=%async_computation.8 | async-start | bytes 3145728 | tf_op jit(solution)/shard_map/all_to_all | solution.py:84
  1128.8 26.7 %copy-start.12 = (f32[2,128,1024]{2,1,0:T(8,128)S(1)}, f32[2,128,1024]{2,1,0:T(8,128)}, u32[]{:S(2)}) copy-start(f32[2,128,1024]{2,1,0:T(8,128)} %copy-done.10) | copy-start | bytes 3145732
  1128.8 26.7 %copy-start.69 = (f32[2,1024]{1,0:T(2,128)S(1)}, f32[2,1024]{1,0:T(2,128)}, u32[]{:S(2)}) copy-start(f32[2,1024]{1,0:T(2,128)} %get-tuple-element.356) | copy-start | bytes 24580
  1128.8 26.7 %copy-start.80 = (f32[2,1024]{1,0:T(2,128)S(1)}, f32[2,1024]{1,0:T(2,128)}, u32[]{:S(2)}) copy-start(f32[2,1024]{1,0:T(2,128)} %get-tuple-element.355) | copy-start | bytes 24580
  1128.8 26.7 %copy-start.86 = (f32[2,128]{1,0:T(2,128)S(1)}, f32[2,128]{1,0:T(2,128)}, u32[]{:S(2)}) copy-start(f32[2,128]{1,0:T(2,128)} %copy-done.85) | copy-start | bytes 3076
  1128.8 26.7 %copy-start.95 = (f32[2,128]{1,0:T(2,128)S(1)}, f32[2,128]{1,0:T(2,128)}, u32[]{:S(2)}) copy-start(f32[2,128]{1,0:T(2,128)} %copy-done.94) | copy-start | bytes 3076
  1150.8 102.8 %all-to-all-start.9 = ((bf16[2,4096,2,1,128]{4,0,3,2,1:T(2,128)(2,1)}), bf16[2,4096,2,1,128]{4,0,3,2,1:T(2,128)(2,1)}, u32[]{:S(2)}, u32[]{:S(2)}) async-start(bf16[2,4096,2,1,128]{4,0,3,2,1:T(2,128)(2,1)} %copy.293), calls=%async_computation.9 | async-start | bytes 8388608 | tf_op jit(solution)/shard_map/all_to_all | solution.py:259
  1155.4 152.4 %all-reduce.4.cloned.1.call-start = ((), (), s32[]{:S(2)}) async-start(), calls=%async_computation.17 | async-start | bytes 835584
  1171.3 7.9 copy-start.53
  1188.0 7.5 copy-start.14
  1188.0 7.5 copy-start.67
  1188.0 7.5 copy-start.82
  1195.6 5.9 copy-start.84
  1195.6 6.6 copy-start.99
  1195.6 6.6 copy-start.98
  1195.6 6.7 copy-start.101
  1205.0 424.9 %reduce-scatter.6.cloned.1.call-start = ((), (), s32[]{:S(2)}) async-start(), calls=%async_computation.15 | async-start | bytes 37748736 | tf_op jit(solution)/shard_map/reduce_scatter | solution.py:338
  1223.4 11.0 copy-start.23
  1292.8 6.9 slice-start
  1306.6 348.5 %copy-start.60 = (f32[17,288]{1,0:T(8,128)S(1)}, f32[17,288]{1,0:T(8,128)}, u32[]{:S(2)}) copy-start(f32[17,288]{1,0:T(8,128)} %param.28) | copy-start | bytes 58756
  1306.6 348.5 %copy-start.70 = (f32[17,288]{1,0:T(8,128)S(1)}, f32[17,288]{1,0:T(8,128)}, u32[]{:S(2)}) copy-start(f32[17,288]{1,0:T(8,128)} %param.29) | copy-start | bytes 58756
  1306.6 348.5 %copy-start.71 = (f32[17,288]{1,0:T(8,128)S(1)}, f32[17,288]{1,0:T(8,128)}, u32[]{:S(2)}) copy-start(f32[17,288]{1,0:T(8,128)} %param.30) | copy-start | bytes 58756
  1306.6 348.5 %reduce-scatter.10.cloned.1.call-start = ((), (), s32[]{:S(2)}) async-start(), calls=%async_computation.18 | async-start | bytes 92160
  1309.9 400.6 %reduce-scatter.8.cloned.1.call-start = ((), (), s32[]{:S(2)}) async-start(), calls=%async_computation.16 | async-start | bytes 5242880 | tf_op jit(solution)/shard_map/reduce_scatter | solution.py:346
  (67 other events, 214.8 us)
Sparse Core Ops, SparseCore 0:
  10.2 84.7 all-gather.4
  96.9 298.9 all-gather.6
  1205.2 75.6 all-reduce.3
  1306.7 323.1 reduce-scatter.5
  1633.1 21.9 reduce-scatter.9
  1657.9 52.5 reduce-scatter.7
where the time goes:
time: 1730 us; the launch traced here: 1720 us
  waiting for transfers between devices  914 us (53%)
  matrix products  330 us (19%)
  local copies, waits for them, and re-layouts  213 us (12%)
  other arithmetic  119 us (7%)
  blocking collectives  67.6 us (4%)
  between operations  46.7 us (3%)
  starting transfers between devices  34.4 us (2%)
    dot_general x49, matrix products, contract(): return jnp.einsum(form, left, right, preferred_element_type=jnp.float32)  328 us
    reduce_scatter x1, waiting for transfers between devices, shards(): lax.psum_scatter(slot_grads.astype(jnp.bfloat16), 'fsdp', scatter_dimensi...  320 us
    all_gather x1, waiting for transfers between devices, fetch_weights(): lax.all_gather(row_blocks, 'dp', axis=0, tiled=True)  240 us
    all_to_all x1, waiting for transfers between devices, shards(): lax.all_to_all(image_pairs.reshape(objects, img_local, 2, groups, head_wi...  93.4 us
    all_gather x1, waiting for transfers between devices, fetch_weights(): lax.all_gather(narrow, 'fsdp', axis=1, tiled=True)  84.9 us
    convert_element_type x4, other arithmetic, attend_backward(): grad_scores = (probs * (grad_probs - row_terms)).astype(jnp.bfloat16)  60.1 us
    all_to_all x2, waiting for transfers between devices, split_heads(): lax.all_to_all(pieces, 'fsdp', split_axis=3, concat_axis=1, tiled=True)  53.1 us
    all_to_all x3, waiting for transfers between devices, merge_heads(): lax.all_to_all(pieces, 'fsdp', split_axis=1, concat_axis=3, tiled=True)  47 us
  transfers between devices with their start and end apart: 14, of which 12 were waited for; matrix products, arithmetic and copies ran while one was open for 12% of the time, Pallas kernels for 0%

commit v1 on v0

v1 whole, which is shorter than its diff:
```python
import functools

import jax
import jax.numpy as jnp
from jax import lax
from jax.experimental import pallas as pl
from jax.experimental.pallas import tpu as pltpu
from jax.sharding import PartitionSpec as P

HD = 64
STEP = 5
VIEW = 1024
LANES = 128


HIGHEST = lax.Precision.HIGHEST
NEGATIVE = -1e30
BETA_ONE = 0.5
BETA_TWO = 0.5
EPSILON = 1e-08
WEIGHT_DECAY = 0.01
RATE_TILES = 0.03
RATE_MODULATION = 0.15


def contract(form, left, right):
    return jnp.einsum(form, left, right, preferred_element_type=jnp.float32)


def layer_norm(values):
    center = values - jnp.mean(values, axis=-1, keepdims=True)
    spread = jnp.mean(center * center, axis=-1, keepdims=True)
    return center * lax.rsqrt(spread + 1e-06)


def modulate(values, shift, scale):
    return layer_norm(values) * (1.0 + scale) + shift


def modulate_back(values, shift, scale, grad_normed):
    unused, pull = jax.vjp(modulate, values, shift, scale)
    return pull(grad_normed)


def gelu_tanh(values):
    return jax.nn.gelu(values, approximate=True)


NT = (((1,), (1,)), ((), ()))
NN = (((1,), (0,)), ((), ()))
TN = (((0,), (0,)), ((), ()))


def dot(left, right, dims):
    return lax.dot_general(left, right, dims, preferred_element_type=jnp.float32)


def head_part(values, head, heads):
    if heads == 1:
        return values
    lanes = lax.broadcasted_iota(jnp.int32, values.shape, 1)
    return jnp.where(lanes // HD == head, values, jnp.zeros_like(values))


def rows_of(ref, start, amount):
    block = ref[pl.ds(start, amount), 0]
    return block.reshape(block.shape[0] * block.shape[1], block.shape[2])


def forward_body(step_rows, live_ref, q_ref, k_ref, v_ref, out_ref, lse_ref):
    key_groups, unused_one, key_rows, width = k_ref.shape
    heads = width // HD
    per_block = step_rows // key_rows
    blocks = live_ref[pl.program_id(0)] // step_rows
    queries = rows_of(q_ref, 0, q_ref.shape[0]) * jnp.bfloat16(0.125)
    result = jnp.zeros(queries.shape, jnp.float32)
    for head in range(heads):
        own = head_part(queries, head, heads)

        def step(position, carried, own=own):
            highest, total, acc = carried
            keys = rows_of(k_ref, position * per_block, per_block)
            values = rows_of(v_ref, position * per_block, per_block)
            scores = dot(own, keys, NT)
            new_highest = jnp.maximum(highest, jnp.max(scores, axis=1, keepdims=True))
            weights = jnp.exp(scores - new_highest)
            scale = jnp.exp(highest - new_highest)
            total = total * scale + jnp.sum(weights, axis=1, keepdims=True)
            acc = acc * scale + dot(weights.astype(jnp.bfloat16), values, NN)
            return (new_highest, total, acc)

        first = (
            jnp.full((own.shape[0], 1), -jnp.inf, jnp.float32),
            jnp.zeros((own.shape[0], 1), jnp.float32),
            jnp.zeros(own.shape, jnp.float32),
        )
        highest, total, acc = lax.fori_loop(0, blocks, step, first)
        result = result + head_part(acc / total, head, heads)
        level = jnp.broadcast_to(highest + jnp.log(total), (own.shape[0], 128))
        lse_ref[0, head] = jnp.transpose(level)[0:1]
    out_ref[...] = result.astype(jnp.bfloat16).reshape(out_ref.shape)


def attend_forward(live, query_source, key_source, value_source, query_block, step_rows):
    (q_array, q_at), (k_array, k_at), (v_array, v_at) = query_source, key_source, value_source
    groups, objects, q_rows, unused_width = q_array.shape
    k_rows = k_array.shape[2]
    width = q_at[1]
    heads = width // HD
    total_q = groups * q_rows
    per_q = query_block // q_rows
    grid = (objects, total_q // query_block)
    whole = lambda index: (lambda o, j, live: (0, o, 0, index))
    part = lambda index: (lambda o, j, live: (j, o, 0, index))
    return pl.pallas_call(
        functools.partial(forward_body, step_rows),
        grid_spec=pltpu.PrefetchScalarGridSpec(
            num_scalar_prefetch=1,
            grid=grid,
            in_specs=[
                pl.BlockSpec((per_q, 1, q_rows, width), part(q_at[0])),
                pl.BlockSpec((groups, 1, k_rows, width), whole(k_at[0])),
                pl.BlockSpec((groups, 1, k_rows, width), whole(v_at[0])),
            ],
            out_specs=[
                pl.BlockSpec((per_q, 1, q_rows, width), part(0)),
                pl.BlockSpec((1, heads, 1, query_block), lambda o, j, live: (o, 0, 0, j)),
            ],
        ),
        out_shape=[
            jax.ShapeDtypeStruct((groups, objects, q_rows, width), jnp.bfloat16),
            jax.ShapeDtypeStruct((objects, heads, 1, total_q), jnp.float32),
        ],
        cost_estimate=pl.CostEstimate(
            flops=4 * objects * total_q * groups * k_rows * width,
            bytes_accessed=4 * objects * groups * (q_rows + k_rows) * width,
            transcendentals=objects * heads * total_q * groups * k_rows,
        ),
    )(live, q_array, k_array, v_array)


def backward_prepare(q_ref, out_ref, grad_ref, qs, gs, delta):
    heads = qs.shape[0]
    queries = rows_of(q_ref, 0, q_ref.shape[0]) * jnp.bfloat16(0.125)
    grads = rows_of(grad_ref, 0, grad_ref.shape[0])
    outs = rows_of(out_ref, 0, out_ref.shape[0])
    product = jnp.transpose(grads.astype(jnp.float32) * outs.astype(jnp.float32))
    for head in range(heads):
        qs[head] = head_part(queries, head, heads)
        gs[head] = head_part(grads, head, heads)
        delta[head] = jnp.sum(product[head * HD : (head + 1) * HD], axis=0, keepdims=True)


def backward_block(keys, values, lse_ref, qs, gs, delta):
    heads = qs.shape[0]
    grad_q, grad_k, grad_v = None, None, None
    for head in range(heads):
        own, grads = qs[head], gs[head]
        weights = jnp.exp(dot(keys, own, NT) - lse_ref[0, head])
        grad_weights = dot(values, grads, NT)
        grad_scores = (weights * (grad_weights - delta[head])).astype(jnp.bfloat16)
        new_v = dot(weights.astype(jnp.bfloat16), grads, NN)
        new_k = dot(grad_scores, own, NN)
        new_q = dot(grad_scores, head_part(keys, head, heads), TN)
        grad_q = new_q if grad_q is None else grad_q + new_q
        grad_k = new_k if grad_k is None else grad_k + new_k
        grad_v = new_v if grad_v is None else grad_v + new_v
    return grad_q, grad_k, grad_v


def cross_backward_body(
    live_ref, q_ref, k_ref, v_ref, out_ref, lse_ref, grad_ref, dq_ref, dkv_ref, qs, gs, delta, dq_acc
):
    position = pl.program_id(1)
    width = q_ref.shape[3]
    rows = k_ref.shape[0] * k_ref.shape[2]

    @pl.when(position == 0)
    def _():
        backward_prepare(q_ref, out_ref, grad_ref, qs, gs, delta)
        dq_acc[...] = jnp.zeros_like(dq_acc)

    alive = position * rows < live_ref[pl.program_id(0)]

    @pl.when(alive)
    def _():
        keys = rows_of(k_ref, 0, k_ref.shape[0])
        values = rows_of(v_ref, 0, v_ref.shape[0])
        grad_q, grad_k, grad_v = backward_block(keys, values, lse_ref, qs, gs, delta)
        dq_acc[...] += grad_q
        shape = (k_ref.shape[0], 1, k_ref.shape[2], width)
        dkv_ref[:, :, :, 0:width] = grad_k.astype(jnp.bfloat16).reshape(shape)
        dkv_ref[:, :, :, width : 2 * width] = grad_v.astype(jnp.bfloat16).reshape(shape)

    @pl.when(jnp.logical_not(alive))
    def _():
        dkv_ref[...] = jnp.zeros_like(dkv_ref)

    @pl.when(position == pl.num_programs(1) - 1)
    def _():
        dq_ref[...] = (dq_acc[...] * 0.125).astype(jnp.bfloat16).reshape(dq_ref.shape)


def attend_backward(live, query_source, key_source, value_source, outs, lse, grads, step_rows):
    (q_array, q_at), (k_array, k_at), (v_array, v_at) = query_source, key_source, value_source
    groups, objects, q_rows, unused_width = q_array.shape
    k_rows = k_array.shape[2]
    width = q_at[1]
    heads = width // HD
    total_q = groups * q_rows
    per_k = max(step_rows // k_rows, 1)
    grid = (objects, groups // per_k)
    whole = lambda index: (lambda o, j, live: (0, o, 0, index))
    part = lambda index: (lambda o, j, live: (j, o, 0, index))
    return pl.pallas_call(
        cross_backward_body,
        grid_spec=pltpu.PrefetchScalarGridSpec(
            num_scalar_prefetch=1,
            grid=grid,
            in_specs=[
                pl.BlockSpec((groups, 1, q_rows, width), whole(q_at[0])),
                pl.BlockSpec((per_k, 1, k_rows, width), part(k_at[0])),
                pl.BlockSpec((per_k, 1, k_rows, width), part(v_at[0])),
                pl.BlockSpec((groups, 1, q_rows, width), whole(0)),
                pl.BlockSpec((1, heads, 1, total_q), lambda o, j, live: (o, 0, 0, 0)),
                pl.BlockSpec((groups, 1, q_rows, width), whole(0)),
            ],
            out_specs=[
                pl.BlockSpec((groups, 1, q_rows, width), whole(0)),
                pl.BlockSpec((per_k, 1, k_rows, 2 * width), part(0)),
            ],
            scratch_shapes=[
                pltpu.VMEM((heads, total_q, width), jnp.bfloat16),
                pltpu.VMEM((heads, total_q, width), jnp.bfloat16),
                pltpu.VMEM((heads, 1, total_q), jnp.float32),
                pltpu.VMEM((total_q, width), jnp.float32),
            ],
        ),
        out_shape=[
            jax.ShapeDtypeStruct((groups, objects, q_rows, width), jnp.bfloat16),
            jax.ShapeDtypeStruct((groups, objects, k_rows, 2 * width), jnp.bfloat16),
        ],
        cost_estimate=pl.CostEstimate(
            flops=10 * objects * total_q * groups * k_rows * width,
            bytes_accessed=8 * objects * groups * (q_rows + k_rows) * width,
            transcendentals=objects * heads * total_q * groups * k_rows,
        ),
    )(live, q_array, k_array, v_array, outs, lse, grads)

CHUNKS = ((0, 1, 2), (5, 6), (3, 4, 7), (8, 9, 10, 11), (12, 13, 14, 15))
MOD_ROWS = 16
MESH = pl.DeviceIdType.MESH


def fetch_generic(master, modulation, tile_slots):
    narrow = master.astype(jnp.bfloat16)
    mod_narrow = modulation.astype(jnp.bfloat16)[:, None, None, :]
    row_blocks = lax.all_gather(narrow, "fsdp", axis=1, tiled=True)
    mod_blocks = lax.all_gather(mod_narrow, "fsdp", axis=2, tiled=True)
    gathered = lax.all_gather(row_blocks, "dp", axis=0, tiled=True)
    mod_all = lax.all_gather(mod_blocks, "dp", axis=1, tiled=True)
    chunks = [
        jnp.stack(
            [lax.dynamic_index_in_dim(gathered, tile_slots[tile], 0, keepdims=False) for tile in chunk]
        )
        for chunk in CHUNKS
    ]
    return chunks, mod_all.reshape(mod_all.shape[0], -1)


def pick_body(index_ref, source_ref, out_ref):
    out_ref[...] = source_ref[...]


def pick_rows(source, index):
    count = index.shape[0]
    block = (1,) + source.shape[1:]
    return pl.pallas_call(
        pick_body,
        grid_spec=pltpu.PrefetchScalarGridSpec(
            num_scalar_prefetch=1,
            grid=(count,),
            in_specs=[pl.BlockSpec(block, lambda t, index: (index[t], 0, 0))],
            out_specs=pl.BlockSpec(block, lambda t, index: (t, 0, 0)),
        ),
        out_shape=jax.ShapeDtypeStruct((count,) + source.shape[1:], source.dtype),
    )(index, source)


def move_dp(value, flip):
    owners = lax.axis_size("dp")
    return lax.ppermute(value, "dp", [(i, i ^ flip) for i in range(owners)])


def move_z(value, shift):
    groups = lax.axis_size("fsdp")
    return lax.ppermute(value, "fsdp", [(i, (i + 2 * shift) % groups) for i in range(groups)])


def assemble_body(tiles, rows, extra, *refs):
    pieces, refs = refs[:8], refs[8:]
    out_ref, refs = refs[0], refs[1:]
    extra_ref, refs = (refs[0], refs[1:]) if extra else (None, refs)
    hold, in_sem, out_sem, send_sem, recv_sem = refs
    dp_index = lax.axis_index("dp")
    fsdp_index = lax.axis_index("fsdp")
    z_index, core = fsdp_index // 2, fsdp_index % 2
    partner = {"fsdp": fsdp_index + 1 - 2 * core}
    loads = []
    for position in range(16):
        half, side, turn = position // 8, (position // 4) % 2, position % 4
        load = pltpu.make_async_copy(
            pieces[half * 4 + turn].at[side], hold.at[position], in_sem.at[position]
        )
        load.start()
        loads.append(load)
    barrier = pltpu.get_barrier_semaphore()
    pl.semaphore_signal(barrier, inc=1, device_id=partner, device_id_type=MESH)
    pl.semaphore_wait(barrier, 1)
    copies = []
    for position in range(16):
        half, side, turn = position // 8, (position // 4) % 2, position % 4
        z_from = (z_index + 8 - (2 * half + side)) % 4
        quarter = dp_index ^ turn
        loads[position].wait()
        targets = [(slice(tile * rows, (tile + 1) * rows), out_ref.at[tile]) for tile in range(tiles)]
        if extra:
            targets.append((slice(tiles * rows, tiles * rows + extra), extra_ref))
        for place, (window, target) in enumerate(targets):
            source = hold.at[position, window]
            target = target.at[z_from, core, quarter]
            away = pltpu.make_async_remote_copy(
                source,
                target,
                send_sem.at[position, place],
                recv_sem.at[position, place],
                device_id=partner,
                device_id_type=MESH,
            )
            away.start()
            here = pltpu.make_async_copy(source, target, out_sem.at[position, place])
            here.start()
            copies.append((away, here))
    for away, here in copies:
        away.wait()
        here.wait()


def assemble(pieces, tiles, rows, extra, collective):
    width = pieces[0].shape[2]
    places = tiles + (1 if extra else 0)
    out_shape = [jax.ShapeDtypeStruct((tiles, 4, 2, 4, rows, width), jnp.bfloat16)]
    if extra:
        out_shape.append(jax.ShapeDtypeStruct((4, 2, 4, extra, width), jnp.bfloat16))
    any_spec = pl.BlockSpec(memory_space=pl.ANY)
    return pl.pallas_call(
        functools.partial(assemble_body, tiles, rows, extra),
        out_shape=out_shape,
        in_specs=[any_spec] * 8,
        out_specs=[any_spec] * len(out_shape),
        scratch_shapes=[
            pltpu.VMEM((16, tiles * rows + extra, width), jnp.bfloat16),
            pltpu.SemaphoreType.DMA((16,)),
            pltpu.SemaphoreType.DMA((16, places)),
            pltpu.SemaphoreType.DMA((16, places)),
            pltpu.SemaphoreType.DMA((16, places)),
        ],
        compiler_params=pltpu.CompilerParams(collective_id=collective, has_side_effects=True),
        cost_estimate=pl.CostEstimate(
            flops=0, bytes_accessed=5 * tiles * 16 * rows * width * 2, transcendentals=0
        ),
    )(*pieces)


def fetch_weights(master, modulation, tile_slots):
    owners, groups = lax.axis_size("dp"), lax.axis_size("fsdp")
    if owners != 4 or groups != 8 or master.shape[1] != 128:
        return fetch_generic(master, modulation, tile_slots)
    slots_here, row_count, width = master.shape
    rows = row_count // owners
    dp_index = lax.axis_index("dp")
    narrow = master.astype(jnp.bfloat16).reshape(slots_here, owners, rows, width)
    parts = []
    for flip in range(4):
        part = lax.dynamic_index_in_dim(narrow, dp_index ^ flip, 1, keepdims=False)
        parts.append(part if flip == 0 else move_dp(part, flip))
    stacked = jnp.concatenate(parts, axis=0)
    index = ((tile_slots // slots_here) ^ dp_index) * slots_here + tile_slots % slots_here
    order = jnp.array([tile for chunk in CHUNKS for tile in chunk], jnp.int32)
    mine = pick_rows(stacked, index[order]).reshape(-1, width)
    mod_rows, mod_columns = modulation.shape
    mod_flat = modulation.astype(jnp.bfloat16).reshape(-1)
    mod_flat = jnp.pad(mod_flat, (0, MOD_ROWS * width - mod_flat.shape[0])).reshape(MOD_ROWS, width)
    chunks, mod_all, start, previous = [], None, 0, None
    for number, chunk in enumerate(CHUNKS):
        tiles = len(chunk)
        local = mine[start * rows : (start + tiles) * rows]
        start += tiles
        extra = MOD_ROWS if number == 0 else 0
        if extra:
            local = jnp.concatenate([local, mod_flat], axis=0)
        if previous is not None:
            local, unused_order = lax.optimization_barrier((local, previous))
        arrived = [local] + [move_z(local, shift) for shift in (1, 2, 3)]
        low, high = jnp.stack(arrived[:2]), jnp.stack(arrived[2:])
        previous = high
        low_x, high_y = move_dp(low, 1), move_dp(high, 2)
        low_y, high_x = move_dp(low, 2), move_dp(high, 1)
        low_xy, high_xy = move_dp(low_x, 2), move_dp(high_y, 1)
        pieces = (low, low_x, low_y, low_xy, high, high_x, high_y, high_xy)
        outs = assemble(pieces, tiles, rows, extra, number)
        chunks.append(outs[0].reshape(tiles, 32 * rows, width))
        if extra:
            flat = outs[1].reshape(8, 4, MOD_ROWS * width)[:, :, : mod_rows * mod_columns]
            mod_all = flat.reshape(8, 4, mod_rows, mod_columns).transpose(2, 1, 0, 3)
            mod_all = mod_all.reshape(mod_rows, -1)
    return chunks, mod_all


def exchange(pieces):
    return lax.all_to_all(pieces, "fsdp", split_axis=0, concat_axis=0, tiled=True)


def by_head(values, groups):
    objects, rows, blocks, width = values.shape
    share = width // groups
    moved = values.reshape(objects, rows, blocks, groups, share).transpose(3, 0, 1, 2, 4)
    return moved.reshape(groups, objects, rows, blocks * share)


def from_head(pieces, blocks):
    groups, objects, rows, share = pieces.shape
    share = share // blocks
    moved = pieces.reshape(groups, objects, rows, blocks, share).transpose(1, 2, 3, 0, 4)
    return moved.reshape(objects, rows, blocks, groups * share)


def source(array, index, width):
    if width % LANES == 0:
        return (array, (index, width))
    return (array[..., index * width : (index + 1) * width], (0, width))


def adamw(weights, grads, first, second, rate):
    first_new = BETA_ONE * first + (1.0 - BETA_ONE) * grads
    second_new = BETA_TWO * second + (1.0 - BETA_TWO) * grads * grads
    first_hat = first_new / (1.0 - BETA_ONE**STEP)
    second_hat = second_new / (1.0 - BETA_TWO**STEP)
    weights_new = weights - rate * (
        first_hat / (jnp.sqrt(second_hat) + EPSILON) + WEIGHT_DECAY * weights
    )
    return (weights_new, first_new, second_new)


def shards(
    triplane,
    image_tokens,
    camera,
    view_tokens,
    master,
    moment1,
    moment2,
    tile_slots,
    modulation,
    mod_moment1,
    mod_moment2,
    cotangent,
):
    objects, tri_local, model_width = triplane.shape
    img_local = image_tokens.shape[1]
    groups = lax.axis_size("fsdp")
    owners = lax.axis_size("dp")
    tri_total = tri_local * groups
    head_width = model_width // groups
    tile_count = master.shape[0] * owners
    chunks, mod_all = fetch_weights(master, modulation, tile_slots)
    mod_full = mod_all.astype(jnp.float32)
    modulations = (
        jnp.dot(camera, mod_full[:-1], precision=HIGHEST, preferred_element_type=jnp.float32)
        + mod_full[-1]
    )
    blocks = [
        modulations[:, position * model_width : (position + 1) * model_width][:, None, :]
        for position in range(9)
    ]
    tiles_qkv, tiles_pair, tiles_mixed, tiles_up, tiles_down = chunks
    tile_out_one, tile_query_two, tile_out_two = tiles_mixed[0], tiles_mixed[1], tiles_mixed[2]
    residual_in = triplane.astype(jnp.float32)
    normed_one = modulate(residual_in, blocks[0], blocks[1]).astype(jnp.bfloat16)
    triples = contract("otd,kde->otke", normed_one, tiles_qkv).astype(jnp.bfloat16)
    triple_heads = exchange(by_head(triples, groups))
    every_key = jnp.full((objects,), tri_total, jnp.int32)
    self_sources = [source(triple_heads, index, head_width) for index in range(3)]
    self_result, self_logsum = attend_forward(every_key, *self_sources, tri_total, VIEW)
    merged_one = from_head(exchange(self_result), 1)[:, :, 0]
    branch_one = contract("otd,de->ote", merged_one, tile_out_one)
    residual_mid = residual_in + blocks[2] * branch_one
    normed_two = modulate(residual_mid, blocks[3], blocks[4]).astype(jnp.bfloat16)
    cross_query = contract("otd,de->ote", normed_two, tile_query_two).astype(jnp.bfloat16)
    image_pairs = contract("oid,kde->oike", image_tokens, tiles_pair).astype(jnp.bfloat16)
    query_heads = exchange(by_head(cross_query[:, :, None], groups))
    pair_heads = exchange(by_head(image_pairs, groups))
    cross_sources = [
        source(query_heads, 0, head_width),
        source(pair_heads, 0, head_width),
        source(pair_heads, 1, head_width),
    ]
    cross_result, cross_logsum = attend_forward(view_tokens, *cross_sources, tri_total, VIEW)
    merged_two = from_head(exchange(cross_result), 1)[:, :, 0]
    branch_two = contract("otd,de->ote", merged_two, tile_out_two)
    residual_late = residual_mid + blocks[5] * branch_two
    normed_three = modulate(residual_late, blocks[6], blocks[7]).astype(jnp.bfloat16)
    hidden_pre = contract("otd,kde->otke", normed_three, tiles_up)
    hidden = gelu_tanh(hidden_pre).astype(jnp.bfloat16)
    branch_three = contract("otkd,kde->ote", hidden, tiles_down)
    block_output = (residual_late + blocks[8] * branch_three).astype(jnp.bfloat16)
    grad_final = cotangent.astype(jnp.float32)
    grad_gate_three = jnp.sum(grad_final * branch_three, axis=1)
    grad_branch_three = (blocks[8] * grad_final).astype(jnp.bfloat16)
    grad_down = contract("otkd,ote->kde", hidden, grad_branch_three)
    grad_hidden = contract("ote,kde->otkd", grad_branch_three, tiles_down)
    unused_gelu, gelu_pull = jax.vjp(gelu_tanh, hidden_pre)
    grad_pre = gelu_pull(grad_hidden)[0].astype(jnp.bfloat16)
    grad_up = contract("otd,otke->kde", normed_three, grad_pre)
    grad_normed_three = contract("otke,kde->otd", grad_pre, tiles_up)
    grad_late_norm, grad_shift_three, grad_scale_three = modulate_back(
        residual_late, blocks[6], blocks[7], grad_normed_three
    )
    grad_late = grad_final + grad_late_norm
    grad_gate_two = jnp.sum(grad_late * branch_two, axis=1)
    grad_branch_two = (blocks[5] * grad_late).astype(jnp.bfloat16)
    grad_out_two = contract("otd,ote->de", merged_two, grad_branch_two)
    grad_merged_two = contract("ote,de->otd", grad_branch_two, tile_out_two).astype(jnp.bfloat16)
    grad_cross_heads = exchange(by_head(grad_merged_two[:, :, None], groups))
    grad_query_heads, grad_pair_heads = attend_backward(
        view_tokens, *cross_sources, cross_result, cross_logsum, grad_cross_heads, VIEW
    )
    grad_query_two = from_head(exchange(grad_query_heads), 1)[:, :, 0]
    grad_pairs = from_head(exchange(grad_pair_heads), 2)
    grad_tile_query = contract("otd,ote->de", normed_two, grad_query_two)
    grad_tiles_pair = contract("oid,oike->kde", image_tokens, grad_pairs)
    grad_image = contract("oike,kde->oid", grad_pairs, tiles_pair)
    grad_normed_two = contract("ote,de->otd", grad_query_two, tile_query_two)
    grad_mid_norm, grad_shift_two, grad_scale_two = modulate_back(
        residual_mid, blocks[3], blocks[4], grad_normed_two
    )
    grad_mid = grad_late + grad_mid_norm
    grad_gate_one = jnp.sum(grad_mid * branch_one, axis=1)
    grad_branch_one = (blocks[2] * grad_mid).astype(jnp.bfloat16)
    grad_out_one = contract("otd,ote->de", merged_one, grad_branch_one)
    grad_merged_one = contract("ote,de->otd", grad_branch_one, tile_out_one).astype(jnp.bfloat16)
    grad_self_heads = exchange(by_head(grad_merged_one[:, :, None], groups))
    grad_self_query, grad_self_pair = attend_backward(
        every_key, *self_sources, self_result, self_logsum, grad_self_heads, VIEW
    )
    grad_triple_heads = jnp.concatenate([grad_self_query, grad_self_pair], axis=-1)
    grad_triples = from_head(exchange(grad_triple_heads), 3)
    grad_qkv = contract("otd,otke->kde", normed_one, grad_triples)
    grad_normed_one = contract("otke,kde->otd", grad_triples, tiles_qkv)
    grad_in_norm, grad_shift_one, grad_scale_one = modulate_back(
        residual_in, blocks[0], blocks[1], grad_normed_one
    )
    grad_triplane = grad_mid + grad_in_norm
    grad_mods = jnp.concatenate(
        [
            grad_shift_one[:, 0],
            grad_scale_one[:, 0],
            grad_gate_one,
            grad_shift_two[:, 0],
            grad_scale_two[:, 0],
            grad_gate_two,
            grad_shift_three[:, 0],
            grad_scale_three[:, 0],
            grad_gate_three,
        ],
        axis=-1,
    )
    grad_mod_rows = jnp.dot(
        camera.T, grad_mods, precision=HIGHEST, preferred_element_type=jnp.float32
    )
    grad_modulation = jnp.concatenate(
        [grad_mod_rows, jnp.sum(grad_mods, axis=0, keepdims=True)], axis=0
    )
    mod_columns = modulation.shape[1]
    grad_mod_blocks = grad_modulation.reshape(grad_modulation.shape[0], owners, groups, mod_columns)
    logical = [
        grad_qkv[0],
        grad_qkv[1],
        grad_qkv[2],
        grad_out_one,
        grad_tile_query,
        grad_tiles_pair[0],
        grad_tiles_pair[1],
        grad_out_two,
        grad_up[0],
        grad_up[1],
        grad_up[2],
        grad_up[3],
        grad_down[0],
        grad_down[1],
        grad_down[2],
        grad_down[3],
    ]
    slot_grads = jnp.zeros((tile_count, model_width, model_width), jnp.float32)
    for position in range(tile_count):
        slot_grads = lax.dynamic_update_index_in_dim(
            slot_grads, logical[position], tile_slots[position], 0
        )
    row_sums, mod_row_sums = (
        lax.psum_scatter(
            slot_grads.astype(jnp.bfloat16), "fsdp", scatter_dimension=1, tiled=True
        ).astype(jnp.float32),
        lax.psum_scatter(
            grad_mod_blocks.astype(jnp.bfloat16), "fsdp", scatter_dimension=2, tiled=True
        ).astype(jnp.float32),
    )
    tile_grad, mod_grad = (
        lax.psum_scatter(
            row_sums.astype(jnp.bfloat16), "dp", scatter_dimension=0, tiled=True
        ).astype(jnp.float32),
        lax.psum_scatter(
            mod_row_sums.astype(jnp.bfloat16), "dp", scatter_dimension=1, tiled=True
        ).astype(jnp.float32),
    )
    mod_grad = mod_grad.reshape(mod_grad.shape[0], mod_columns)
    new_master, new_moment1, new_moment2 = adamw(master, tile_grad, moment1, moment2, RATE_TILES)
    new_modulation, new_mod_moment1, new_mod_moment2 = adamw(
        modulation, mod_grad, mod_moment1, mod_moment2, RATE_MODULATION
    )
    return (
        block_output,
        grad_triplane,
        grad_image,
        new_master,
        new_moment1,
        new_moment2,
        new_master.astype(jnp.bfloat16),
        new_modulation,
        new_mod_moment1,
        new_mod_moment2,
    )


def solution(mesh):
    in_specs = (
        P("dp", "fsdp", None),
        P("dp", "fsdp", None),
        P("dp", None),
        P("dp"),
        P("dp", "fsdp", None),
        P("dp", "fsdp", None),
        P("dp", "fsdp", None),
        P(),
        P(None, ("dp", "fsdp")),
        P(None, ("dp", "fsdp")),
        P(None, ("dp", "fsdp")),
        P("dp", "fsdp", None),
    )
    out_specs = (
        P("dp", "fsdp", None),
        P("dp", "fsdp", None),
        P("dp", "fsdp", None),
        P("dp", "fsdp", None),
        P("dp", "fsdp", None),
        P("dp", "fsdp", None),
        P("dp", "fsdp", None),
        P(None, ("dp", "fsdp")),
        P(None, ("dp", "fsdp")),
        P(None, ("dp", "fsdp")),
    )
    return jax.shard_map(shards, mesh=mesh, in_specs=in_specs, out_specs=out_specs, check_vma=False)
```

time: 1730 us -> 1380 us (0.80)
  waiting for transfers between devices: 914 us -> 686 us
  matrix products: 330 us -> 105 us
  Pallas kernels: 0 us -> 140 us
  other arithmetic: 119 us -> 27.8 us
  starting transfers between devices: 34.4 us -> 95.1 us
  blocking collectives: 67.6 us -> 101 us
  local copies, waits for them, and re-layouts: 213 us -> 184 us
    all_gather x2 -> x0, waiting for transfers between devices: 324 us -> none  [the longest x1 240 us: fetch_weights(): lax.all_gather(row_blocks, 'dp', axis=0, tiled=True)]
    ppermute x0 -> x48, waiting for transfers between devices: none -> 282 us  [the longest x15 199 us: move_z(): lax.ppermute(value, 'fsdp', [(i, (i + 2 * shift) % groups) for i in range...]
    dot_general x49 -> x21, matrix products: 328 us -> 104 us  [contract(): return jnp.einsum(form, left, right, preferred_element_type=jnp.float32)]
    all_to_all x8 -> x6, waiting for transfers between devices: 203 us -> 0.02 us  [exchange(): lax.all_to_all(pieces, 'fsdp', split_axis=0, concat_axis=0, tiled=True)]
    pallas_call x0 -> x10, Pallas kernels: none -> 140 us  [the longest x2 50.7 us: attend_backward(): pl.pallas_call(cross_backward_body, grid_spec=pltpu.PrefetchScalarGridSpe...]
    ppermute x0 -> x48, starting transfers between devices: none -> 67.6 us  [the longest x33 45.2 us: move_dp(): return lax.ppermute(value, 'dp', [(i, i ^ flip) for i in range(owners)])]
    all_to_all x2 -> x4, blocking collectives: 37.3 us -> 101 us  [exchange(): lax.all_to_all(pieces, 'fsdp', split_axis=0, concat_axis=0, tiled=True)]
    convert_element_type x5 -> x2, other arithmetic: 63 us -> 1.89 us  [the longest x1 1.89 us: fetch_weights(): master.astype(jnp.bfloat16).reshape(slots_here, owners, rows, width)]
  transfers between devices with their start and end apart: 14 -> 58, of which waited for: 12 -> 26; matrix products, arithmetic and copies ran while one was open for 12% -> 15% of each run, Pallas kernels for 0% -> 5%
where the time goes in v1:
time: 1380 us
  waiting for transfers between devices  686 us (50%)
  local copies, waits for them, and re-layouts  184 us (13%)
  Pallas kernels  140 us (10%)
  matrix products  105 us (8%)
  blocking collectives  101 us (7%)
  starting transfers between devices  95.1 us (7%)
  between operations  45.9 us (3%)
  other arithmetic  27.8 us (2%)
    reduce_scatter x1, waiting for transfers between devices, shards(): lax.psum_scatter(slot_grads.astype(jnp.bfloat16), 'fsdp', scatter_dimensi...  337 us
    ppermute x15, waiting for transfers between devices, move_z(): lax.ppermute(value, 'fsdp', [(i, (i + 2 * shift) % groups) for i in range...  199 us
    dot_general x21, matrix products, contract(): return jnp.einsum(form, left, right, preferred_element_type=jnp.float32)  104 us
    all_to_all x4, blocking collectives, exchange(): lax.all_to_all(pieces, 'fsdp', split_axis=0, concat_axis=0, tiled=True)  101 us
    ppermute x33, waiting for transfers between devices, move_dp(): return lax.ppermute(value, 'dp', [(i, i ^ flip) for i in range(owners)])  83.1 us
    pallas_call x2, Pallas kernels, attend_backward(): pl.pallas_call(cross_backward_body, grid_spec=pltpu.PrefetchScalarGridSpe...  50.7 us
    ppermute x33, starting transfers between devices, move_dp(): return lax.ppermute(value, 'dp', [(i, i ^ flip) for i in range(owners)])  45.2 us
    reduce_scatter x1, waiting for transfers between devices, shards(): lax.psum_scatter(row_sums.astype(jnp.bfloat16), 'dp', scatter_dimension=0...  44.1 us
  transfers between devices with their start and end apart: 58, of which 26 were waited for; matrix products, arithmetic and copies ran while one was open for 15% of the time, Pallas kernels for 5%

profile of v1, /device:TPU:0, one launch (start us, length us, event | category | flops | bytes accessed | tf_op | source)
XLA Modules:
  0.0 1384.6 jit_solution(12391029264193575789)
XLA Ops:
  15.9 5.5 collective-permute-done.2
  21.4 4.8 collective-permute-done.1
  28.6 9.5 shard_map.204
  44.6 5.7 collective-permute-done.3
  53.7 10.4 collective-permute-done.7
  68.0 9.5 collective-permute-done.10.refs_6_
  79.4 8.0 collective-permute-done.5.refs_2_
  87.4 8.8 collective-permute-done.6.refs_3_
  97.1 9.0 shard_map.205
  115.0 4.7 convolution_convert_fusion.2
  126.7 4.3 all-to-all-start
  136.8 23.6 %collective-permute-done.13 = bf16[64,1024]{1,0:T(8,128)(2,1)S(1)} collective-permute-done((bf16[64,1024]{1,0:T(8,128)(2,1)S(1)}, bf16[64,1024]{1,0:T(8,128)(2,1)S(1)}, u32[]{:S(2)}, u32[]{:S(2)}) %collective-permute-start.13) | collective-permute-done | bytes 131104 | tf_op jit(solution)/shard_map/ppermute | solution.py:297
  160.4 19.5 %collective-permute-done.12 = bf16[64,1024]{1,0:T(8,128)(2,1)S(1)} collective-permute-done((bf16[64,1024]{1,0:T(8,128)(2,1)S(1)}, bf16[64,1024]{1,0:T(8,128)(2,1)S(1)}, u32[]{:S(2)}, u32[]{:S(2)}) %collective-permute-start.12) | collective-permute-done | bytes 131104 | tf_op jit(solution)/shard_map/ppermute | solution.py:297
  180.7 4.0 collective-permute-start.19
  193.2 5.9 collective-permute-done.18
  204.3 12.7 shard_map.206
  226.4 21.2 %collective-permute-done.29.refs_7_ = bf16[2,64,1024]{2,1,0:T(8,128)(2,1)} collective-permute-done((bf16[2,64,1024]{2,1,0:T(8,128)(2,1)}, bf16[2,64,1024]{2,1,0:T(8,128)(2,1)}, u32[]{:S(2)}, u32[]{:S(2)}) %collective-permute-start.29) | collective-permute-done | bytes 262176 | tf_op jit(solution)/shard_map/ppermute | solution.py:292
  247.6 5.8 shard_map.208
  253.5 8.0 shard_map.207
  261.5 5.9 fusion.52
  278.1 5.2 all-to-all-start.2
  283.3 8.4 convolution_convert_fusion.1
  291.7 11.2 copy.147
  302.8 7.6 reshape.215
  310.4 5.1 all-to-all-start.3
  321.6 72.6 %collective-permute-done.30 = bf16[128,1024]{1,0:T(8,128)(2,1)S(1)} collective-permute-done((bf16[128,1024]{1,0:T(8,128)(2,1)S(1)}, bf16[128,1024]{1,0:T(8,128)(2,1)S(1)}, u32[]{:S(2)}, u32[]{:S(2)}) %collective-permute-start.30) | collective-permute-done | bytes 262176 | tf_op jit(solution)/shard_map/ppermute | solution.py:297
  396.4 35.6 %collective-permute-done.34 = bf16[128,1024]{1,0:T(8,128)(2,1)S(1)} collective-permute-done((bf16[128,1024]{1,0:T(8,128)(2,1)S(1)}, bf16[128,1024]{1,0:T(8,128)(2,1)S(1)}, u32[]{:S(2)}, u32[]{:S(2)}) %collective-permute-start.34) | collective-permute-done | bytes 262176 | tf_op jit(solution)/shard_map/ppermute | solution.py:297
  436.6 7.2 collective-permute-done.39
  447.1 10.7 collective-permute-done.43
  462.0 24.8 %shard_map.209 = (bf16[8,2,128,128]{3,2,1,0:T(8,128)(2,1)}, f32[2,2,1,1024]{3,2,1,0:T(1,128)}) custom-call(s32[2]{0:T(128)} %live_ref.3, bf16[8,2,128,128]{3,2,1,0:T(8,128)(2,1)} %all-to-all-done.2.q_ref, bf16[8,2,512,256]{3,2,1,0:T(8,128)(2,1)} %all-to-all-done.3.k_ref.v_ref, bf16[8,2,512,256]{3,2,1,0:T(8,128)(2,1)} %all-to-all-done.3.k_ref.v_ref), custom_call_target="tpu_custom_call" | custom-call | flops 4294967296 | bytes 5242880 | tf_op jit(solution)/shard_map/pallas_call | solution.py:115
  486.8 4.3 all-to-all-start.4
  491.2 13.2 collective-permute-start.41
  506.6 12.9 collective-permute-done.38.refs_7_
  519.5 9.7 shard_map.210
  530.7 10.4 collective-permute-done.47.refs_7_
  541.1 9.7 shard_map.211
  556.8 8.4 fusion.42
  565.1 6.5 fusion.8
  571.7 7.1 multiply_reduce_fusion
  586.9 20.2 %all_to_all.50.grad_ref = bf16[8,2,128,128]{3,2,1,0:T(8,128)(2,1)} all-to-all(bf16[8,2,128,128]{3,2,1,0:T(8,128)(2,1)} %bitcast.279), channel_id=1, replica_groups=mesh['dp'=4,'fsdp'=8] {'fsdp'}, dimensions={0} | all-to-all | bytes 1048576 | tf_op jit(solution)/shard_map/all_to_all | solution.py:421
  607.0 35.3 %shard_map.212 = (bf16[8,2,128,128]{3,2,1,0:T(8,128)(2,1)}, bf16[8,2,512,256]{3,2,1,0:T(8,128)(2,1)}) custom-call(s32[2]{0:T(128)} %live_ref.3, bf16[8,2,128,128]{3,2,1,0:T(8,128)(2,1)} %all-to-all-done.2.q_ref, bf16[8,2,512,256]{3,2,1,0:T(8,128)(2,1)} %all-to-all-done.3.k_ref.v_ref, bf16[8,2,512,256]{3,2,1,0:T(8,128)(2,1)} %all-to-all-done.3.k_ref.v_ref, ...), custom_call_target="tpu_custom_call" | custom-call | flops 10737418240 | bytes 10485760 | tf_op jit(solution)/shard_map/pallas_call | solution.py:215
  642.4 19.7 %all_to_all.51 = bf16[8,2,128,128]{3,2,1,0:T(8,128)(2,1)} all-to-all(bf16[8,2,128,128]{3,2,1,0:T(8,128)(2,1)} %get-tuple-element.33), channel_id=1, replica_groups=mesh['dp'=4,'fsdp'=8] {'fsdp'}, dimensions={0} | all-to-all | bytes 1048576 | tf_op jit(solution)/shard_map/all_to_all | solution.py:421
  667.7 8.9 fusion.24
  683.1 19.9 %all_to_all.52.grad_ref = bf16[8,2,128,128]{3,2,1,0:T(8,128)(2,1)} all-to-all(bf16[8,2,128,128]{3,2,1,0:T(8,128)(2,1)} %bitcast.282), channel_id=1, replica_groups=mesh['dp'=4,'fsdp'=8] {'fsdp'}, dimensions={0} | all-to-all | bytes 1048576 | tf_op jit(solution)/shard_map/all_to_all | solution.py:421
  703.0 15.4 %shard_map.213 = (bf16[8,2,128,128]{3,2,1,0:T(8,128)(2,1)}, bf16[8,2,128,256]{3,2,1,0:T(8,128)(2,1)}) custom-call(s32[2]{0:T(128)} %broadcast_31_live_ref.2.live_ref, bf16[8,2,128,384]{3,2,1,0:T(8,128)(2,1)} %all-to-all-done.q_ref.k_ref.v_ref, bf16[8,2,128,384]{3,2,1,0:T(8,128)(2,1)} %all-to-all-done.q_ref.k_ref.v_ref, ...), custom_call_target="tpu_custom_call" | custom-call | flops 2684354560 | bytes 4194304 | tf_op jit(solution)/shard_map/pallas_call | solution.py:215
  720.0 40.9 %all_to_all.53 = bf16[8,2,128,384]{3,2,1,0:T(8,128)(2,1)} all-to-all(bf16[8,2,128,384]{3,2,1,0:T(8,128)(2,1)S(1)} %pad_maximum_fusion), channel_id=1, replica_groups=mesh['dp'=4,'fsdp'=8] {'fsdp'}, dimensions={0} | all-to-all | bytes 3145728 | tf_op jit(solution)/shard_map/all_to_all | solution.py:421
  761.0 4.7 all-to-all-start.9
  796.8 4.4 convolution_bitcast_fusion.1
  804.8 3.9 copy.169
  808.7 3.9 copy.170
  812.6 4.0 copy.171
  816.6 3.9 copy.172
  820.5 8.7 convolution_bitcast_fusion
  856.6 5.3 fusion.22
  869.1 11.2 broadcast_in_dim.76
  890.0 6.9 reshape.224
  896.9 6.8 copy.158
  903.7 7.3 reshape.225
  911.1 7.0 convolution_bitcast_fusion.3
  952.7 336.8 %reduce-scatter.6.cloned.1.call-done = bf16[16,128,1024]{2,1,0:T(8,128)(2,1)} async-done(((bf16[16,1024,1024]{2,1,0:T(8,128)(2,1)}), bf16[16,128,1024]{2,1,0:T(8,128)(2,1)}) %reduce-scatter.6.cloned.1.call-update) | async-done | bytes 4194320 | tf_op jit(solution)/shard_map/reduce_scatter | solution.py:610
  1292.5 22.4 %reduce-scatter.10.cloned.1.call-done = bf16[17,1,1,288]{3,0,2,1:T(8,128)(2,1)} async-done(((bf16[17,4,1,288]{3,0,2,1:T(8,128)(2,1)}), bf16[17,1,1,288]{3,0,2,1:T(8,128)(2,1)}) %reduce-scatter.10.cloned.1.call-update) | async-done | bytes 9808
  1316.2 10.0 convolution_bitcast_fusion.4
  1326.2 44.1 %reduce-scatter.8.cloned.1.call-done = bf16[4,128,1024]{2,1,0:T(8,128)(2,1)} async-done(((bf16[16,128,1024]{2,1,0:T(8,128)(2,1)}), bf16[4,128,1024]{2,1,0:T(8,128)(2,1)}) %reduce-scatter.8.cloned.1.call-update) | async-done | bytes 1048592 | tf_op jit(solution)/shard_map/reduce_scatter | solution.py:618
  1370.3 7.3 fusion.45
  (392 shorter events, 222.1 us)
Async XLA Ops:
  10.1 11.3 collective-permute-start.2
  14.0 12.2 collective-permute-start.1
  14.5 12.0 collective-permute-start
  40.0 10.4 collective-permute-start.3
  41.6 12.1 collective-permute-start.8
  43.8 20.2 %collective-permute-start.7 = (bf16[112,1024]{1,0:T(8,128)(2,1)S(1)}, bf16[112,1024]{1,0:T(8,128)(2,1)S(1)}, u32[]{:S(2)}, u32[]{:S(2)}) collective-permute-start(bf16[112,1024]{1,0:T(8,128)(2,1)S(1)} %get-tuple-element.88), channel_id=1, source_target_pairs={{0,4},{1,5},{2,6},{3,7},{4,0},{5,1},{6,2},{7,3},{8,12},{9,13},{10,... | collective-permute-start | bytes 688136 | tf_op jit(solution)/shard_map/ppermute | solution.py:297
  50.4 17.5 %collective-permute-start.4 = (bf16[2,112,1024]{2,1,0:T(8,128)(2,1)S(1)}, bf16[2,112,1024]{2,1,0:T(8,128)(2,1)S(1)}, u32[]{:S(2)}, u32[]{:S(2)}) collective-permute-start(bf16[2,112,1024]{2,1,0:T(8,128)(2,1)S(1)} %pad_maximum_fusion.6.refs_0_), channel_id=1, source_target_pairs={{0,8},{8,0},{16,24},{24,16},{1,9},{9,1},{17,25},{25,17},{2,10},{10... | collective-permute-start | bytes 1376264 | tf_op jit(solution)/shard_map/ppermute | solution.py:292
  64.1 13.5 collective-permute-start.10
  65.9 21.6 %collective-permute-start.5 = (bf16[2,112,1024]{2,1,0:T(8,128)(2,1)S(1)}, bf16[2,112,1024]{2,1,0:T(8,128)(2,1)S(1)}, u32[]{:S(2)}, u32[]{:S(2)}) collective-permute-start(bf16[2,112,1024]{2,1,0:T(8,128)(2,1)S(1)} %pad_maximum_fusion.6.refs_0_), channel_id=1, source_target_pairs={{0,16},{8,24},{16,0},{24,8},{1,17},{9,25},{17,1},{25,9},{2,18},{10... | collective-permute-start | bytes 1376264 | tf_op jit(solution)/shard_map/ppermute | solution.py:292
  66.4 21.0 %collective-permute-start.9 = (bf16[2,112,1024]{2,1,0:T(8,128)(2,1)S(1)}, bf16[2,112,1024]{2,1,0:T(8,128)(2,1)S(1)}, u32[]{:S(2)}, u32[]{:S(2)}) collective-permute-start(bf16[2,112,1024]{2,1,0:T(8,128)(2,1)S(1)} %pad_maximum_fusion.7.refs_4_), channel_id=1, source_target_pairs={{0,8},{8,0},{16,24},{24,16},{1,9},{9,1},{17,25},{25,17},{2,10},{10... | collective-permute-start | bytes 1376264 | tf_op jit(solution)/shard_map/ppermute | solution.py:292
  67.9 28.4 %collective-permute-start.6 = (bf16[2,112,1024]{2,1,0:T(8,128)(2,1)S(1)}, bf16[2,112,1024]{2,1,0:T(8,128)(2,1)S(1)}, u32[]{:S(2)}, u32[]{:S(2)}) collective-permute-start(bf16[2,112,1024]{2,1,0:T(8,128)(2,1)S(1)} %collective-permute-done.4.refs_1_), channel_id=1, source_target_pairs={{0,16},{8,24},{16,0},{24,8},{1,17},{9,25},{17,1},{25,9},{2,18},{10... | collective-permute-start | bytes 1376264 | tf_op jit(solution)/shard_map/ppermute | solution.py:292
  77.6 19.5 %collective-permute-start.11 = (bf16[2,112,1024]{2,1,0:T(8,128)(2,1)S(1)}, bf16[2,112,1024]{2,1,0:T(8,128)(2,1)}, u32[]{:S(2)}, u32[]{:S(2)}) collective-permute-start(bf16[2,112,1024]{2,1,0:T(8,128)(2,1)S(1)} %collective-permute-done.10.refs_6_), channel_id=1, source_target_pairs={{0,8},{8,0},{16,24},{24,16},{1,9},{9,1},{17,25},{25,17},{2,10},{10... | collective-permute-start | bytes 1376264 | tf_op jit(solution)/shard_map/ppermute | solution.py:292
  126.7 77.0 %all-to-all-start = ((bf16[8,2,128,384]{3,2,1,0:T(8,128)(2,1)}), bf16[8,2,128,384]{3,2,1,0:T(8,128)(2,1)}, u32[]{:S(2)}, u32[]{:S(2)}) async-start(bf16[8,2,128,384]{3,2,1,0:T(8,128)(2,1)} %copy.141), calls=%async_computation | async-start | bytes 3145728 | tf_op jit(solution)/shard_map/all_to_all | solution.py:421
  131.9 28.5 %collective-permute-start.13 = (bf16[64,1024]{1,0:T(8,128)(2,1)S(1)}, bf16[64,1024]{1,0:T(8,128)(2,1)S(1)}, u32[]{:S(2)}, u32[]{:S(2)}) collective-permute-start(bf16[64,1024]{1,0:T(8,128)(2,1)S(1)} %bitcast.299), channel_id=1, source_target_pairs={{0,6},{1,7},{2,0},{3,1},{4,2},{5,3},{6,4},{7,5},{8,14},{9,15},{10,... | collective-permute-start | bytes 393224 | tf_op jit(solution)/shard_map/ppermute | solution.py:297
  135.7 44.2 %collective-permute-start.12 = (bf16[64,1024]{1,0:T(8,128)(2,1)S(1)}, bf16[64,1024]{1,0:T(8,128)(2,1)S(1)}, u32[]{:S(2)}, u32[]{:S(2)}) collective-permute-start(bf16[64,1024]{1,0:T(8,128)(2,1)S(1)} %bitcast.300), channel_id=1, source_target_pairs={{0,4},{1,5},{2,6},{3,7},{4,0},{5,1},{6,2},{7,3},{8,12},{9,13},{10,... | collective-permute-start | bytes 393224 | tf_op jit(solution)/shard_map/ppermute | solution.py:297
  135.7 49.0 %collective-permute-start.23 = (bf16[64,1024]{1,0:T(8,128)(2,1)S(1)}, bf16[64,1024]{1,0:T(8,128)(2,1)S(1)}, u32[]{:S(2)}, u32[]{:S(2)}) collective-permute-start(bf16[64,1024]{1,0:T(8,128)(2,1)S(1)} %bitcast.301), channel_id=1, source_target_pairs={{0,2},{1,3},{2,4},{3,5},{4,6},{5,7},{6,0},{7,1},{8,10},{9,11},{10,... | collective-permute-start | bytes 393224 | tf_op jit(solution)/shard_map/ppermute | solution.py:297
  180.7 9.6 collective-permute-start.14
  180.7 12.5 collective-permute-start.19
  184.7 14.4 %collective-permute-start.18 = (bf16[96,1024]{1,0:T(8,128)(2,1)S(1)}, bf16[96,1024]{1,0:T(8,128)(2,1)S(1)}, u32[]{:S(2)}, u32[]{:S(2)}) collective-permute-start(bf16[96,1024]{1,0:T(8,128)(2,1)S(1)} %bitcast.296), channel_id=1, source_target_pairs={{0,4},{1,5},{2,6},{3,7},{4,0},{5,1},{6,2},{7,3},{8,12},{9,13},{10,... | collective-permute-start | bytes 589832 | tf_op jit(solution)/shard_map/ppermute | solution.py:297
  184.8 16.3 %collective-permute-start.24 = (bf16[2,64,1024]{2,1,0:T(8,128)(2,1)S(1)}, bf16[2,64,1024]{2,1,0:T(8,128)(2,1)}, u32[]{:S(2)}, u32[]{:S(2)}) collective-permute-start(bf16[2,64,1024]{2,1,0:T(8,128)(2,1)S(1)} %pad_maximum_fusion.12.refs_0_), channel_id=1, source_target_pairs={{0,8},{8,0},{16,24},{24,16},{1,9},{9,1},{17,25},{25,17},{2,10},{10... | collective-permute-start | bytes 786440 | tf_op jit(solution)/shard_map/ppermute | solution.py:292
  186.3 16.5 %collective-permute-start.25 = (bf16[2,64,1024]{2,1,0:T(8,128)(2,1)S(1)}, bf16[2,64,1024]{2,1,0:T(8,128)(2,1)S(1)}, u32[]{:S(2)}, u32[]{:S(2)}) collective-permute-start(bf16[2,64,1024]{2,1,0:T(8,128)(2,1)S(1)} %pad_maximum_fusion.12.refs_0_), channel_id=1, source_target_pairs={{0,16},{8,24},{16,0},{24,8},{1,17},{9,25},{17,1},{25,9},{2,18},{10... | collective-permute-start | bytes 786440 | tf_op jit(solution)/shard_map/ppermute | solution.py:292
  190.3 32.5 %collective-permute-start.15 = (bf16[2,96,1024]{2,1,0:T(8,128)(2,1)S(1)}, bf16[2,96,1024]{2,1,0:T(8,128)(2,1)}, u32[]{:S(2)}, u32[]{:S(2)}) collective-permute-start(bf16[2,96,1024]{2,1,0:T(8,128)(2,1)S(1)} %pad_maximum_fusion.9.refs_0_), channel_id=1, source_target_pairs={{0,8},{8,0},{16,24},{24,16},{1,9},{9,1},{17,25},{25,17},{2,10},{10... | collective-permute-start | bytes 1179656 | tf_op jit(solution)/shard_map/ppermute | solution.py:292
  199.2 25.2 %collective-permute-start.21 = (bf16[2,96,1024]{2,1,0:T(8,128)(2,1)S(1)}, bf16[2,96,1024]{2,1,0:T(8,128)(2,1)}, u32[]{:S(2)}, u32[]{:S(2)}) collective-permute-start(bf16[2,96,1024]{2,1,0:T(8,128)(2,1)S(1)} %pad_maximum_fusion.10.refs_4_), channel_id=1, source_target_pairs={{0,16},{8,24},{16,0},{24,8},{1,17},{9,25},{17,1},{25,9},{2,18},{10... | collective-permute-start | bytes 1179656 | tf_op jit(solution)/shard_map/ppermute | solution.py:292
  200.8 19.7 %collective-permute-start.27 = (bf16[2,64,1024]{2,1,0:T(8,128)(2,1)}, bf16[2,64,1024]{2,1,0:T(8,128)(2,1)}, u32[]{:S(2)}, u32[]{:S(2)}) collective-permute-start(bf16[2,64,1024]{2,1,0:T(8,128)(2,1)} %pad_maximum_fusion.11.refs_4_), channel_id=1, source_target_pairs={{0,8},{8,0},{16,24},{24,16},{1,9},{9,1},{17,25},{25,17},{2,10},{10... | collective-permute-start | bytes 786440 | tf_op jit(solution)/shard_map/ppermute | solution.py:292
  201.0 21.3 %collective-permute-start.28 = (bf16[2,64,1024]{2,1,0:T(8,128)(2,1)}, bf16[2,64,1024]{2,1,0:T(8,128)(2,1)}, u32[]{:S(2)}, u32[]{:S(2)}) collective-permute-start(bf16[2,64,1024]{2,1,0:T(8,128)(2,1)} %pad_maximum_fusion.11.refs_4_), channel_id=1, source_target_pairs={{0,16},{8,24},{16,0},{24,8},{1,17},{9,25},{17,1},{25,9},{2,18},{10... | collective-permute-start | bytes 786440 | tf_op jit(solution)/shard_map/ppermute | solution.py:292
  203.5 21.1 %collective-permute-start.26 = (bf16[2,64,1024]{2,1,0:T(8,128)(2,1)}, bf16[2,64,1024]{2,1,0:T(8,128)(2,1)}, u32[]{:S(2)}, u32[]{:S(2)}) collective-permute-start(bf16[2,64,1024]{2,1,0:T(8,128)(2,1)} %collective-permute-done.24.refs_1_), channel_id=1, source_target_pairs={{0,16},{8,24},{16,0},{24,8},{1,17},{9,25},{17,1},{25,9},{2,18},{10... | collective-permute-start | bytes 786440 | tf_op jit(solution)/shard_map/ppermute | solution.py:292
  217.0 50.4 %all-to-all-start.1 = ((bf16[8,2,128,128]{3,2,1,0:T(8,128)(2,1)}), bf16[8,2,128,128]{3,2,1,0:T(8,128)(2,1)S(1)}, u32[]{:S(2)}, u32[]{:S(2)}) async-start(bf16[8,2,128,128]{3,2,1,0:T(8,128)(2,1)} %get-tuple-element.26.out_ref), calls=%async_computation.1 | async-start | bytes 1048576 | tf_op jit(solution)/shard_map/all_to_all | solution.py:421
  220.5 32.9 %collective-permute-start.16 = (bf16[2,96,1024]{2,1,0:T(8,128)(2,1)S(1)}, bf16[2,96,1024]{2,1,0:T(8,128)(2,1)}, u32[]{:S(2)}, u32[]{:S(2)}) collective-permute-start(bf16[2,96,1024]{2,1,0:T(8,128)(2,1)S(1)} %pad_maximum_fusion.9.refs_0_), channel_id=1, source_target_pairs={{0,16},{8,24},{16,0},{24,8},{1,17},{9,25},{17,1},{25,9},{2,18},{10... | collective-permute-start | bytes 1179656 | tf_op jit(solution)/shard_map/ppermute | solution.py:292
  222.3 31.1 %collective-permute-start.20 = (bf16[2,96,1024]{2,1,0:T(8,128)(2,1)S(1)}, bf16[2,96,1024]{2,1,0:T(8,128)(2,1)}, u32[]{:S(2)}, u32[]{:S(2)}) collective-permute-start(bf16[2,96,1024]{2,1,0:T(8,128)(2,1)S(1)} %pad_maximum_fusion.10.refs_4_), channel_id=1, source_target_pairs={{0,8},{8,0},{16,24},{24,16},{1,9},{9,1},{17,25},{25,17},{2,10},{10... | collective-permute-start | bytes 1179656 | tf_op jit(solution)/shard_map/ppermute | solution.py:292
  222.8 30.6 %collective-permute-start.17 = (bf16[2,96,1024]{2,1,0:T(8,128)(2,1)}, bf16[2,96,1024]{2,1,0:T(8,128)(2,1)}, u32[]{:S(2)}, u32[]{:S(2)}) collective-permute-start(bf16[2,96,1024]{2,1,0:T(8,128)(2,1)} %collective-permute-done.15.refs_1_), channel_id=1, source_target_pairs={{0,16},{8,24},{16,0},{24,8},{1,17},{9,25},{17,1},{25,9},{2,18},{10... | collective-permute-start | bytes 1179656 | tf_op jit(solution)/shard_map/ppermute | solution.py:292
  224.4 29.1 %collective-permute-start.22 = (bf16[2,96,1024]{2,1,0:T(8,128)(2,1)}, bf16[2,96,1024]{2,1,0:T(8,128)(2,1)}, u32[]{:S(2)}, u32[]{:S(2)}) collective-permute-start(bf16[2,96,1024]{2,1,0:T(8,128)(2,1)} %collective-permute-done.21.refs_6_), channel_id=1, source_target_pairs={{0,8},{8,0},{16,24},{24,16},{1,9},{9,1},{17,25},{25,17},{2,10},{10... | collective-permute-start | bytes 1179656 | tf_op jit(solution)/shard_map/ppermute | solution.py:292
  224.6 23.0 %collective-permute-start.29 = (bf16[2,64,1024]{2,1,0:T(8,128)(2,1)}, bf16[2,64,1024]{2,1,0:T(8,128)(2,1)}, u32[]{:S(2)}, u32[]{:S(2)}) collective-permute-start(bf16[2,64,1024]{2,1,0:T(8,128)(2,1)} %collective-permute-done.28.refs_6_), channel_id=1, source_target_pairs={{0,8},{8,0},{16,24},{24,16},{1,9},{9,1},{17,25},{25,17},{2,10},{10... | collective-permute-start | bytes 786440 | tf_op jit(solution)/shard_map/ppermute | solution.py:292
  272.1 395.5 %copy-start.62 = (f32[2,128]{1,0:T(2,128)}, f32[2,128]{1,0:T(2,128)S(1)}, u32[]{:S(2)}) copy-start(f32[2,128]{1,0:T(2,128)S(1)} %broadcast_multiply_fusion.1) | copy-start | bytes 3076
  272.4 395.2 %copy-start.74 = (f32[2,128]{1,0:T(2,128)}, f32[2,128]{1,0:T(2,128)S(1)}, u32[]{:S(2)}) copy-start(f32[2,128]{1,0:T(2,128)S(1)} %fusion.37) | copy-start | bytes 3076
  278.1 32.3 %all-to-all-start.2 = ((bf16[8,2,128,128]{3,2,1,0:T(8,128)(2,1)}), bf16[8,2,128,128]{3,2,1,0:T(8,128)(2,1)}, u32[]{:S(2)}, u32[]{:S(2)}) async-start(bf16[8,2,128,128]{3,2,1,0:T(8,128)(2,1)} %bitcast.276), calls=%async_computation.2 | async-start | bytes 1048576 | tf_op jit(solution)/shard_map/all_to_all | solution.py:421
  310.4 151.6 %all-to-all-start.3 = ((bf16[8,2,512,256]{3,2,1,0:T(8,128)(2,1)}), bf16[8,2,512,256]{3,2,1,0:T(8,128)(2,1)}, u32[]{:S(2)}, u32[]{:S(2)}) async-start(bf16[8,2,512,256]{3,2,1,0:T(8,128)(2,1)} %reshape.215), calls=%async_computation.3 | async-start | bytes 8388608 | tf_op jit(solution)/shard_map/all_to_all | solution.py:421
  316.6 77.6 %collective-permute-start.30 = (bf16[128,1024]{1,0:T(8,128)(2,1)S(1)}, bf16[128,1024]{1,0:T(8,128)(2,1)S(1)}, u32[]{:S(2)}, u32[]{:S(2)}) collective-permute-start(bf16[128,1024]{1,0:T(8,128)(2,1)S(1)} %bitcast.290), channel_id=1, source_target_pairs={{0,2},{1,3},{2,4},{3,5},{4,6},{5,7},{6,0},{7,1},{8,10},{9,11},{10,... | collective-permute-start | bytes 786440 | tf_op jit(solution)/shard_map/ppermute | solution.py:297
  318.7 77.7 %collective-permute-start.35 = (bf16[128,1024]{1,0:T(8,128)(2,1)S(1)}, bf16[128,1024]{1,0:T(8,128)(2,1)S(1)}, u32[]{:S(2)}, u32[]{:S(2)}) collective-permute-start(bf16[128,1024]{1,0:T(8,128)(2,1)S(1)} %bitcast.291), channel_id=1, source_target_pairs={{0,6},{1,7},{2,0},{3,1},{4,2},{5,3},{6,4},{7,5},{8,14},{9,15},{10,... | collective-permute-start | bytes 786440 | tf_op jit(solution)/shard_map/ppermute | solution.py:297
  320.5 111.4 %collective-permute-start.34 = (bf16[128,1024]{1,0:T(8,128)(2,1)S(1)}, bf16[128,1024]{1,0:T(8,128)(2,1)S(1)}, u32[]{:S(2)}, u32[]{:S(2)}) collective-permute-start(bf16[128,1024]{1,0:T(8,128)(2,1)S(1)} %bitcast.292), channel_id=1, source_target_pairs={{0,4},{1,5},{2,6},{3,7},{4,0},{5,1},{6,2},{7,3},{8,12},{9,13},{10,... | collective-permute-start | bytes 786440 | tf_op jit(solution)/shard_map/ppermute | solution.py:297
  394.3 64.9 %collective-permute-start.31 = (bf16[2,128,1024]{2,1,0:T(8,128)(2,1)S(1)}, bf16[2,128,1024]{2,1,0:T(8,128)(2,1)}, u32[]{:S(2)}, u32[]{:S(2)}) collective-permute-start(bf16[2,128,1024]{2,1,0:T(8,128)(2,1)S(1)} %pad_maximum_fusion.2.refs_0_), channel_id=1, source_target_pairs={{0,8},{8,0},{16,24},{24,16},{1,9},{9,1},{17,25},{25,17},{2,10},{10... | collective-permute-start | bytes 1572872 | tf_op jit(solution)/shard_map/ppermute | solution.py:292
  395.0 65.6 %collective-permute-start.32 = (bf16[2,128,1024]{2,1,0:T(8,128)(2,1)S(1)}, bf16[2,128,1024]{2,1,0:T(8,128)(2,1)S(1)}, u32[]{:S(2)}, u32[]{:S(2)}) collective-permute-start(bf16[2,128,1024]{2,1,0:T(8,128)(2,1)S(1)} %pad_maximum_fusion.2.refs_0_), channel_id=1, source_target_pairs={{0,16},{8,24},{16,0},{24,8},{1,17},{9,25},{17,1},{25,9},{2,18},{10... | collective-permute-start | bytes 1572872 | tf_op jit(solution)/shard_map/ppermute | solution.py:292
  432.8 11.0 collective-permute-start.39
  432.8 13.9 %collective-permute-start.44 = (bf16[128,1024]{1,0:T(8,128)(2,1)S(1)}, bf16[128,1024]{1,0:T(8,128)(2,1)S(1)}, u32[]{:S(2)}, u32[]{:S(2)}) collective-permute-start(bf16[128,1024]{1,0:T(8,128)(2,1)S(1)} %bitcast.287), channel_id=1, source_target_pairs={{0,6},{1,7},{2,0},{3,1},{4,2},{5,3},{6,4},{7,5},{8,14},{9,15},{10,... | collective-permute-start | bytes 786440 | tf_op jit(solution)/shard_map/ppermute | solution.py:297
  436.6 21.1 %collective-permute-start.43 = (bf16[128,1024]{1,0:T(8,128)(2,1)S(1)}, bf16[128,1024]{1,0:T(8,128)(2,1)S(1)}, u32[]{:S(2)}, u32[]{:S(2)}) collective-permute-start(bf16[128,1024]{1,0:T(8,128)(2,1)S(1)} %bitcast.288), channel_id=1, source_target_pairs={{0,4},{1,5},{2,6},{3,7},{4,0},{5,1},{6,2},{7,3},{8,12},{9,13},{10,... | collective-permute-start | bytes 786440 | tf_op jit(solution)/shard_map/ppermute | solution.py:297
  443.8 47.4 %collective-permute-start.36 = (bf16[2,128,1024]{2,1,0:T(8,128)(2,1)}, bf16[2,128,1024]{2,1,0:T(8,128)(2,1)}, u32[]{:S(2)}, u32[]{:S(2)}) collective-permute-start(bf16[2,128,1024]{2,1,0:T(8,128)(2,1)} %pad_maximum_fusion.3.refs_4_), channel_id=1, source_target_pairs={{0,8},{8,0},{16,24},{24,16},{1,9},{9,1},{17,25},{25,17},{2,10},{10... | collective-permute-start | bytes 1572872 | tf_op jit(solution)/shard_map/ppermute | solution.py:292
  446.7 57.7 %collective-permute-start.37 = (bf16[2,128,1024]{2,1,0:T(8,128)(2,1)}, bf16[2,128,1024]{2,1,0:T(8,128)(2,1)}, u32[]{:S(2)}, u32[]{:S(2)}) collective-permute-start(bf16[2,128,1024]{2,1,0:T(8,128)(2,1)} %pad_maximum_fusion.3.refs_4_), channel_id=1, source_target_pairs={{0,16},{8,24},{16,0},{24,8},{1,17},{9,25},{17,1},{25,9},{2,18},{10... | collective-permute-start | bytes 1572872 | tf_op jit(solution)/shard_map/ppermute | solution.py:292
  457.8 46.6 %collective-permute-start.40 = (bf16[2,128,1024]{2,1,0:T(8,128)(2,1)}, bf16[2,128,1024]{2,1,0:T(8,128)(2,1)}, u32[]{:S(2)}, u32[]{:S(2)}) collective-permute-start(bf16[2,128,1024]{2,1,0:T(8,128)(2,1)} %pad_maximum_fusion.4.refs_0_), channel_id=1, source_target_pairs={{0,8},{8,0},{16,24},{24,16},{1,9},{9,1},{17,25},{25,17},{2,10},{10... | collective-permute-start | bytes 1572872 | tf_op jit(solution)/shard_map/ppermute | solution.py:292
  459.2 47.2 %collective-permute-start.46 = (bf16[2,128,1024]{2,1,0:T(8,128)(2,1)}, bf16[2,128,1024]{2,1,0:T(8,128)(2,1)}, u32[]{:S(2)}, u32[]{:S(2)}) collective-permute-start(bf16[2,128,1024]{2,1,0:T(8,128)(2,1)} %pad_maximum_fusion.5.refs_4_), channel_id=1, source_target_pairs={{0,16},{8,24},{16,0},{24,8},{1,17},{9,25},{17,1},{25,9},{2,18},{10... | collective-permute-start | bytes 1572872 | tf_op jit(solution)/shard_map/ppermute | solution.py:292
  461.5 45.0 %collective-permute-start.33 = (bf16[2,128,1024]{2,1,0:T(8,128)(2,1)}, bf16[2,128,1024]{2,1,0:T(8,128)(2,1)}, u32[]{:S(2)}, u32[]{:S(2)}) collective-permute-start(bf16[2,128,1024]{2,1,0:T(8,128)(2,1)} %collective-permute-done.31.refs_1_), channel_id=1, source_target_pairs={{0,16},{8,24},{16,0},{24,8},{1,17},{9,25},{17,1},{25,9},{2,18},{10... | collective-permute-start | bytes 1572872 | tf_op jit(solution)/shard_map/ppermute | solution.py:292
  486.8 64.1 %all-to-all-start.4 = ((bf16[8,2,128,128]{3,2,1,0:T(8,128)(2,1)}), bf16[8,2,128,128]{3,2,1,0:T(8,128)(2,1)}, u32[]{:S(2)}, u32[]{:S(2)}) async-start(bf16[8,2,128,128]{3,2,1,0:T(8,128)(2,1)} %get-tuple-element.29.out_ref), calls=%async_computation.4 | async-start | bytes 1048576 | tf_op jit(solution)/shard_map/all_to_all | solution.py:421
  491.2 38.1 %collective-permute-start.41 = (bf16[2,128,1024]{2,1,0:T(8,128)(2,1)}, bf16[2,128,1024]{2,1,0:T(8,128)(2,1)}, u32[]{:S(2)}, u32[]{:S(2)}) collective-permute-start(bf16[2,128,1024]{2,1,0:T(8,128)(2,1)} %pad_maximum_fusion.4.refs_0_), channel_id=1, source_target_pairs={{0,16},{8,24},{16,0},{24,8},{1,17},{9,25},{17,1},{25,9},{2,18},{10... | collective-permute-start | bytes 1572872 | tf_op jit(solution)/shard_map/ppermute | solution.py:292
  504.3 15.1 %collective-permute-start.38 = (bf16[2,128,1024]{2,1,0:T(8,128)(2,1)}, bf16[2,128,1024]{2,1,0:T(8,128)(2,1)}, u32[]{:S(2)}, u32[]{:S(2)}) collective-permute-start(bf16[2,128,1024]{2,1,0:T(8,128)(2,1)} %collective-permute-done.37.refs_6_), channel_id=1, source_target_pairs={{0,8},{8,0},{16,24},{24,16},{1,9},{9,1},{17,25},{25,17},{2,10},{10... | collective-permute-start | bytes 1572872 | tf_op jit(solution)/shard_map/ppermute | solution.py:292
  504.4 26.3 %collective-permute-start.45 = (bf16[2,128,1024]{2,1,0:T(8,128)(2,1)}, bf16[2,128,1024]{2,1,0:T(8,128)(2,1)}, u32[]{:S(2)}, u32[]{:S(2)}) collective-permute-start(bf16[2,128,1024]{2,1,0:T(8,128)(2,1)} %pad_maximum_fusion.5.refs_4_), channel_id=1, source_target_pairs={{0,8},{8,0},{16,24},{24,16},{1,9},{9,1},{17,25},{25,17},{2,10},{10... | collective-permute-start | bytes 1572872 | tf_op jit(solution)/shard_map/ppermute | solution.py:292
  506.4 24.3 %collective-permute-start.42 = (bf16[2,128,1024]{2,1,0:T(8,128)(2,1)}, bf16[2,128,1024]{2,1,0:T(8,128)(2,1)}, u32[]{:S(2)}, u32[]{:S(2)}) collective-permute-start(bf16[2,128,1024]{2,1,0:T(8,128)(2,1)} %collective-permute-done.40.refs_1_), channel_id=1, source_target_pairs={{0,16},{8,24},{16,0},{24,8},{1,17},{9,25},{17,1},{25,9},{2,18},{10... | collective-permute-start | bytes 1572872 | tf_op jit(solution)/shard_map/ppermute | solution.py:292
  506.5 34.6 %collective-permute-start.47 = (bf16[2,128,1024]{2,1,0:T(8,128)(2,1)}, bf16[2,128,1024]{2,1,0:T(8,128)(2,1)}, u32[]{:S(2)}, u32[]{:S(2)}) collective-permute-start(bf16[2,128,1024]{2,1,0:T(8,128)(2,1)} %collective-permute-done.46.refs_6_), channel_id=1, source_target_pairs={{0,8},{8,0},{16,24},{24,16},{1,9},{9,1},{17,25},{25,17},{2,10},{10... | collective-permute-start | bytes 1572872 | tf_op jit(solution)/shard_map/ppermute | solution.py:292
  761.0 129.0 %all-to-all-start.9 = ((bf16[8,2,512,256]{3,2,1,0:T(8,128)(2,1)}), bf16[8,2,512,256]{3,2,1,0:T(8,128)(2,1)}, u32[]{:S(2)}, u32[]{:S(2)}) async-start(bf16[8,2,512,256]{3,2,1,0:T(8,128)(2,1)} %get-tuple-element.37), calls=%async_computation.9 | async-start | bytes 8388608 | tf_op jit(solution)/shard_map/all_to_all | solution.py:421
  765.6 184.6 %all-reduce.5.cloned.1.call-start = ((), (), s32[]{:S(2)}) async-start(), calls=%async_computation.15 | async-start | bytes 835584
  869.0 420.5 %reduce-scatter.6.cloned.1.call-start = ((), (), s32[]{:S(2)}) async-start(), calls=%async_computation.13 | async-start | bytes 37748736 | tf_op jit(solution)/shard_map/reduce_scatter | solution.py:610
  949.0 340.5 %copy-start.3 = (bf16[2,128,1024]{2,1,0:T(8,128)(2,1)S(1)}, bf16[2,128,1024]{2,1,0:T(8,128)(2,1)}, u32[]{:S(2)}) copy-start(bf16[2,128,1024]{2,1,0:T(8,128)(2,1)} %param.13) | copy-start | bytes 1572868
  949.1 365.8 %copy-start.47 = (f32[17,288]{1,0:T(8,128)S(1)}, f32[17,288]{1,0:T(8,128)}, u32[]{:S(2)}) copy-start(f32[17,288]{1,0:T(8,128)} %param.21) | copy-start | bytes 58756
  949.1 365.8 %copy-start.55 = (f32[17,288]{1,0:T(8,128)S(1)}, f32[17,288]{1,0:T(8,128)}, u32[]{:S(2)}) copy-start(f32[17,288]{1,0:T(8,128)} %param.22) | copy-start | bytes 58756
  949.1 365.8 %copy-start.56 = (f32[17,288]{1,0:T(8,128)S(1)}, f32[17,288]{1,0:T(8,128)}, u32[]{:S(2)}) copy-start(f32[17,288]{1,0:T(8,128)} %param.23) | copy-start | bytes 58756
  949.1 365.8 %reduce-scatter.10.cloned.1.call-start = ((), (), s32[]{:S(2)}) async-start(), calls=%async_computation.16 | async-start | bytes 92160
  952.4 418.0 %reduce-scatter.8.cloned.1.call-start = ((), (), s32[]{:S(2)}) async-start(), calls=%async_computation.14 | async-start | bytes 5242880 | tf_op jit(solution)/shard_map/reduce_scatter | solution.py:618
  (80 other events, 2733.3 us)
Sparse Core Ops, SparseCore 0:
  869.1 69.5 all-reduce.4
  949.1 340.3 reduce-scatter.5
  1292.8 21.9 reduce-scatter.9
  1317.7 52.5 reduce-scatter.7

commit v2 on v1

--- a/solution.py
+++ b/solution.py
@@ -248,8 +248,251 @@
     )(live, q_array, k_array, v_array, outs, lse, grads)
 
 CHUNKS = ((0, 1, 2), (5, 6), (3, 4, 7), (8, 9, 10, 11), (12, 13, 14, 15))
+EARLY = 8
 MOD_ROWS = 16
 MESH = pl.DeviceIdType.MESH
+
+
+def places():
+    dp_index, fsdp_index = lax.axis_index("dp"), lax.axis_index("fsdp")
+    return dp_index, fsdp_index, fsdp_index // 2, fsdp_index % 2
+
+
+def z_peer(fsdp_index, shift):
+    return {"fsdp": (fsdp_index + 2 * shift) % 8}
+
+
+def core_peer(fsdp_index):
+    return {"fsdp": fsdp_index + 1 - 2 * (fsdp_index % 2)}
+
+
+def dp_peer(dp_index, flip):
+    return {"dp": dp_index ^ flip}
+
+
+def greet(peers):
+    barrier = pltpu.get_barrier_semaphore()
+    for peer in peers:
+        pl.semaphore_signal(barrier, inc=1, device_id=peer, device_id_type=MESH)
+    pl.semaphore_wait(barrier, len(peers))
+
+
+def remote(source, target, send_sem, recv_sem, peer):
+    copy = pltpu.make_async_remote_copy(
+        source, target, send_sem, recv_sem, device_id=peer, device_id_type=MESH
+    )
+    copy.start()
+    return copy
+
+
+def send_z(unit, full, fsdp_index, dp_index, z_index, sems):
+    own = full.at[z_index, dp_index]
+    return [
+        remote(own, own, sems[0].at[unit, shift - 1], sems[1].at[unit, shift - 1], z_peer(fsdp_index, shift))
+        for shift in (1, 2, 3)
+    ]
+
+
+def spread(units, fulls, outs, z_copies, z_local, sems, where):
+    send_sems, recv_sems, out_sems = sems
+    dp_index, fsdp_index, z_index, core = where
+    near_x, near_y = dp_peer(dp_index, 1), dp_peer(dp_index, 2)
+    first, second, last = {}, {}, []
+    for step in range(units + 2):
+        if step < units:
+            unit, full = step, fulls[step]
+            for copy in z_copies[unit]:
+                copy.wait() if z_local else copy.wait_recv()
+            low, high = full.at[0:2, dp_index], full.at[2:4, dp_index]
+            pairs = [(low, near_x), (high, near_y), (low, near_y), (high, near_x)]
+            first[unit] = [
+                remote(ref, ref, send_sems.at[unit, 3 + n], recv_sems.at[unit, 3 + n], peer)
+                for n, (ref, peer) in enumerate(pairs)
+            ]
+        if 0 <= step - 1 < units:
+            unit, full = step - 1, fulls[step - 1]
+            first[unit][0].wait_recv()
+            first[unit][1].wait_recv()
+            low, high = full.at[0:2, dp_index ^ 1], full.at[2:4, dp_index ^ 2]
+            pairs = [(low, near_y), (high, near_x)]
+            second[unit] = [
+                remote(ref, ref, send_sems.at[unit, 7 + n], recv_sems.at[unit, 7 + n], peer)
+                for n, (ref, peer) in enumerate(pairs)
+            ]
+        if 0 <= step - 2 < units:
+            unit, full, out = step - 2, fulls[step - 2], outs[step - 2]
+            for copy in first[unit][2:] + second[unit]:
+                copy.wait_recv()
+            target = out.at[:, core]
+            last.append(
+                remote(full, target, send_sems.at[unit, 9], recv_sems.at[unit, 9], core_peer(fsdp_index))
+            )
+            here = pltpu.make_async_copy(full, target, out_sems.at[unit])
+            here.start()
+            last.append(here)
+    for unit in range(units):
+        for copy in first[unit] + second[unit]:
+            copy.wait_send()
+    for copy in last:
+        copy.wait()
+
+
+def first_gather_body(tiles, rows, index_ref, narrow_ref, mod_ref, out_ref, mod_out_ref, wait_ref, rest_ref, stacked, mine, full, mod_full, zoned, swap_sems, load_sems, send_sems, recv_sems, out_sems, zone_sems):
+    where = places()
+    dp_index, fsdp_index, z_index, core = where
+    peers = [z_peer(fsdp_index, shift) for shift in (1, 2, 3)]
+    peers += [dp_peer(dp_index, flip) for flip in (1, 2, 3)] + [core_peer(fsdp_index)]
+    greet(peers)
+    swaps = [
+        remote(narrow_ref.at[:, dp_index ^ flip], stacked.at[pl.ds(4 * flip, 4)], swap_sems.at[0, flip], swap_sems.at[1, flip], dp_peer(dp_index, flip))
+        for flip in (1, 2, 3)
+    ]
+    own = pltpu.make_async_copy(narrow_ref.at[:, dp_index], stacked.at[pl.ds(0, 4)], load_sems.at[0])
+    own.start()
+    mod_load = pltpu.make_async_copy(mod_ref, mod_full.at[z_index, dp_index], load_sems.at[1])
+    mod_load.start()
+    mod_load.wait()
+    z_copies = {tiles: send_z(tiles, mod_full, fsdp_index, dp_index, z_index, (send_sems, recv_sems))}
+    own.wait()
+    for swap in swaps:
+        swap.wait()
+    for tile in range(tiles):
+        full[tile, z_index, dp_index] = stacked[index_ref[tile]]
+        z_copies[tile] = send_z(tile, full.at[tile], fsdp_index, dp_index, z_index, (send_sems, recv_sems))
+
+    def take(position, carried):
+        mine[position] = stacked[index_ref[position + tiles]]
+        return carried
+
+    lax.fori_loop(0, 16 - tiles, take, 0)
+    early = EARLY - tiles
+    zone = [
+        remote(mine.at[pl.ds(0, early)], zoned.at[z_index], zone_sems.at[0, shift - 1], zone_sems.at[1, shift - 1], z_peer(fsdp_index, shift))
+        for shift in (1, 2, 3)
+    ]
+    zone_own = pltpu.make_async_copy(mine.at[pl.ds(0, early)], wait_ref.at[z_index], load_sems.at[2])
+    zone_own.start()
+    rest = pltpu.make_async_copy(mine.at[pl.ds(early, 16 - EARLY)], rest_ref, load_sems.at[3])
+    rest.start()
+    fulls = [full.at[tile] for tile in range(tiles)] + [mod_full]
+    outs = [out_ref.at[tile] for tile in range(tiles)] + [mod_out_ref]
+    spread(tiles + 1, fulls, outs, z_copies, False, (send_sems, recv_sems, out_sems), where)
+    for unit in range(tiles + 1):
+        for copy in z_copies[unit]:
+            copy.wait_send()
+    for copy in zone:
+        copy.wait()
+    zone_own.wait()
+    rest.wait()
+    stores = []
+    for shift in (1, 2, 3):
+        z_from = (z_index + shift) % 4
+        store = pltpu.make_async_copy(zoned.at[z_from], wait_ref.at[z_from], load_sems.at[3 + shift])
+        store.start()
+        stores.append(store)
+    for store in stores:
+        store.wait()
+
+
+ANY = pl.BlockSpec(memory_space=pl.ANY)
+
+
+def comm_params(collective):
+    return pltpu.CompilerParams(
+        collective_id=collective, has_side_effects=True, vmem_limit_bytes=58 * 1024 * 1024
+    )
+
+
+def first_gather(narrow, mod_rows, index):
+    tiles = len(CHUNKS[0])
+    slots, owners, rows, width = narrow.shape
+    bf = jnp.bfloat16
+    return pl.pallas_call(
+        functools.partial(first_gather_body, tiles, rows),
+        grid_spec=pltpu.PrefetchScalarGridSpec(
+            num_scalar_prefetch=1,
+            grid=(),
+            in_specs=[ANY, ANY],
+            out_specs=[ANY] * 4,
+            scratch_shapes=[
+                pltpu.VMEM((16, rows, width), bf),
+                pltpu.VMEM((16 - tiles, rows, width), bf),
+                pltpu.VMEM((tiles, 4, 4, rows, width), bf),
+                pltpu.VMEM((4, 4, MOD_ROWS, width), bf),
+                pltpu.VMEM((4, EARLY - tiles, rows, width), bf),
+                pltpu.SemaphoreType.DMA((2, 4)),
+                pltpu.SemaphoreType.DMA((8,)),
+                pltpu.SemaphoreType.DMA((tiles + 1, 10)),
+                pltpu.SemaphoreType.DMA((tiles + 1, 10)),
+                pltpu.SemaphoreType.DMA((tiles + 1,)),
+                pltpu.SemaphoreType.DMA((2, 3)),
+            ],
+        ),
+        out_shape=[
+            jax.ShapeDtypeStruct((tiles, 4, 2, 4, rows, width), bf),
+            jax.ShapeDtypeStruct((4, 2, 4, MOD_ROWS, width), bf),
+            jax.ShapeDtypeStruct((4, EARLY - tiles, rows, width), bf),
+            jax.ShapeDtypeStruct((16 - EARLY, rows, width), bf),
+        ],
+        compiler_params=comm_params(0),
+        cost_estimate=pl.CostEstimate(flops=0, bytes_accessed=200_000_000, transcendentals=0),
+    )(index, narrow, mod_rows)
+
+
+def next_gather_body(tiles, start, zoned, source_ref, out_ref, full, load_sems, send_sems, recv_sems, out_sems):
+    where = places()
+    dp_index, fsdp_index, z_index, core = where
+    loads = []
+    for tile in range(tiles):
+        if zoned:
+            load = pltpu.make_async_copy(source_ref.at[:, start + tile], full.at[tile, :, dp_index], load_sems.at[tile])
+        else:
+            load = pltpu.make_async_copy(source_ref.at[start + tile], full.at[tile, z_index, dp_index], load_sems.at[tile])
+        load.start()
+        loads.append(load)
+    peers = [dp_peer(dp_index, flip) for flip in (1, 2)] + [core_peer(fsdp_index)]
+    if not zoned:
+        peers += [z_peer(fsdp_index, shift) for shift in (1, 2, 3)]
+    greet(peers)
+    z_copies = {}
+    for tile in range(tiles):
+        if zoned:
+            z_copies[tile] = [loads[tile]]
+        else:
+            loads[tile].wait()
+            z_copies[tile] = send_z(tile, full.at[tile], fsdp_index, dp_index, z_index, (send_sems, recv_sems))
+    fulls = [full.at[tile] for tile in range(tiles)]
+    outs = [out_ref.at[tile] for tile in range(tiles)]
+    spread(tiles, fulls, outs, z_copies, zoned, (send_sems, recv_sems, out_sems), where)
+    if not zoned:
+        for tile in range(tiles):
+            for copy in z_copies[tile]:
+                copy.wait_send()
+
+
+def next_gather(source, tiles, start, zoned, collective):
+    rows, width = source.shape[-2:]
+    bf = jnp.bfloat16
+    return pl.pallas_call(
+        functools.partial(next_gather_body, tiles, start, zoned),
+        in_specs=[ANY],
+        out_specs=ANY,
+        scratch_shapes=[
+            pltpu.VMEM((tiles, 4, 4, rows, width), bf),
+            pltpu.SemaphoreType.DMA((tiles,)),
+            pltpu.SemaphoreType.DMA((tiles, 10)),
+            pltpu.SemaphoreType.DMA((tiles, 10)),
+            pltpu.SemaphoreType.DMA((tiles,)),
+        ],
+        out_shape=jax.ShapeDtypeStruct((tiles, 4, 2, 4, rows, width), bf),
+        compiler_params=comm_params(collective),
+        cost_estimate=pl.CostEstimate(flops=0, bytes_accessed=tiles * 30_000_000, transcendentals=0),
+    )(source).reshape(tiles, 32 * rows, width)
+
+
+def fast_layout(master):
+    owners, groups = lax.axis_size("dp"), lax.axis_size("fsdp")
+    return owners == 4 and groups == 8 and master.shape[1:] == (128, 1024)
 
 
 def fetch_generic(master, modulation, tile_slots):
@@ -268,153 +511,343 @@
     return chunks, mod_all.reshape(mod_all.shape[0], -1)
 
 
-def pick_body(index_ref, source_ref, out_ref):
-    out_ref[...] = source_ref[...]
-
-
-def pick_rows(source, index):
-    count = index.shape[0]
-    block = (1,) + source.shape[1:]
+def sums_generic(logical, tile_slots):
+    slot_grads = jnp.zeros((len(logical),) + logical[0].shape, jnp.bfloat16)
+    for position, grad in enumerate(logical):
+        slot_grads = lax.dynamic_update_index_in_dim(
+            slot_grads, grad.astype(jnp.bfloat16), tile_slots[position], 0
+        )
+    row_sums = lax.psum_scatter(slot_grads, "fsdp", scatter_dimension=1, tiled=True)
+    return lax.psum_scatter(row_sums, "dp", scatter_dimension=0, tiled=True)
+
+
+def mod_generic(grad_modulation):
+    owners, groups = lax.axis_size("dp"), lax.axis_size("fsdp")
+    rows, width = grad_modulation.shape
+    blocks = grad_modulation.reshape(rows, owners, groups, width // (owners * groups))
+    sums = lax.psum_scatter(blocks.astype(jnp.bfloat16), "fsdp", scatter_dimension=2, tiled=True)
+    sums = lax.psum_scatter(sums, "dp", scatter_dimension=1, tiled=True)
+    return sums.reshape(rows, -1).astype(jnp.float32)
+
+
+def wide(value):
+    return value.astype(jnp.float32)
+
+
+def reduce_scratch(tiles, rows, width):
+    bf, f32 = jnp.bfloat16, jnp.float32
+    return [
+        pltpu.VMEM((2, tiles, 4, 4, rows, width), bf),
+        pltpu.VMEM((4, tiles, 2, 2, rows, width), bf),
+        pltpu.VMEM((2, tiles, 2, 2, rows, width), f32),
+        pltpu.VMEM((4, tiles, 2, rows, width), bf),
+        pltpu.VMEM((tiles, 4, rows, width), f32),
+        pltpu.VMEM((2, 3, tiles, rows, width), bf),
+        pltpu.VMEM((tiles, rows, width), bf),
+        pltpu.SemaphoreType.DMA((2, tiles)),
+        pltpu.SemaphoreType.DMA((8, tiles)),
+        pltpu.SemaphoreType.DMA((8, tiles)),
+    ]
+
+
+def reduce_stages(tiles, scratch, out_ref, where):
+    core_buf, swap, kept, swap_two, whole, zbuf, out_buf, load_sems, send_sems, recv_sems = scratch
+    dp_index, fsdp_index, z_index, core = where
+    x_bit, y_bit = dp_index % 2, dp_index // 2
+    near_x, near_y = dp_peer(dp_index, 1), dp_peer(dp_index, 2)
+
+    def moved(stage, tile):
+        if stage == 1:
+            ends = (swap.at[0, tile], swap.at[1, tile], near_x)
+        elif stage == 2:
+            ends = (swap.at[2, tile], swap.at[3, tile], near_y)
+        elif stage == 3:
+            ends = (swap_two.at[0, tile], swap_two.at[1, tile], near_y)
+        elif stage == 4:
+            ends = (swap_two.at[2, tile], swap_two.at[3, tile], near_x)
+        else:
+            shift = stage - 4
+            ends = (zbuf.at[0, shift - 1, tile], zbuf.at[1, shift - 1, tile], z_peer(fsdp_index, shift))
+        return pltpu.make_async_remote_copy(
+            ends[0], ends[1], send_sems.at[stage, tile], recv_sems.at[stage, tile], device_id=ends[2], device_id_type=MESH
+        )
+
+    def both(tile, z_place, quarter):
+        return wide(core_buf[0, tile, z_place, quarter]) + wide(core_buf[1, tile, z_place, quarter])
+
+    def add_core(tile):
+        for side in range(2):
+            for other in range(2):
+                kept[0, tile, side, other] = both(tile, side, 2 * other + x_bit)
+                swap[0, tile, side, other] = both(tile, side, 2 * other + 1 - x_bit).astype(jnp.bfloat16)
+                kept[1, tile, side, other] = both(tile, 2 + side, 2 * y_bit + other)
+                swap[2, tile, side, other] = both(tile, 2 + side, 2 * (1 - y_bit) + other).astype(jnp.bfloat16)
+        moved(1, tile).start()
+        moved(2, tile).start()
+
+    def add_first(tile):
+        moved(1, tile).wait_recv()
+        moved(2, tile).wait_recv()
+        for side in range(2):
+            whole[tile, side] = kept[0, tile, side, y_bit] + wide(swap[1, tile, side, y_bit])
+            away = kept[0, tile, side, 1 - y_bit] + wide(swap[1, tile, side, 1 - y_bit])
+            swap_two[0, tile, side] = away.astype(jnp.bfloat16)
+            whole[tile, 2 + side] = kept[1, tile, side, x_bit] + wide(swap[3, tile, side, x_bit])
+            away = kept[1, tile, side, 1 - x_bit] + wide(swap[3, tile, side, 1 - x_bit])
+            swap_two[2, tile, side] = away.astype(jnp.bfloat16)
+        moved(3, tile).start()
+        moved(4, tile).start()
+
+    def add_second(tile):
+        moved(3, tile).wait_recv()
+        moved(4, tile).wait_recv()
+        for side in range(2):
+            whole[tile, side] = whole[tile, side] + wide(swap_two[1, tile, side])
+            whole[tile, 2 + side] = whole[tile, 2 + side] + wide(swap_two[3, tile, side])
+        for shift in (1, 2, 3):
+            zbuf[0, shift - 1, tile] = whole[tile, (z_index + shift) % 4].astype(jnp.bfloat16)
+            moved(4 + shift, tile).start()
+
+    def add_z(tile):
+        total = whole[tile, z_index]
+        for shift in (1, 2, 3):
+            moved(4 + shift, tile).wait_recv()
+            total = total + wide(zbuf[1, shift - 1, tile])
+        out_buf[tile] = total.astype(jnp.bfloat16)
+
+    def finish(tile):
+        for stage in range(1, 8):
+            moved(stage, tile).wait_send()
+
+    return add_core, add_first, add_second, add_z, finish
+
+
+def core_copies(entries, scratch, where):
+    core_buf, load_sems, send_sems, recv_sems = scratch[0], scratch[-3], scratch[-2], scratch[-1]
+    copies = []
+    for tile, (theirs, ours) in enumerate(entries):
+        away = remote(theirs, core_buf.at[1, tile], send_sems.at[0, tile], recv_sems.at[0, tile], core_peer(where[1]))
+        load = pltpu.make_async_copy(ours, core_buf.at[0, tile], load_sems.at[0, tile])
+        load.start()
+        copies.append((away, load))
+    return copies
+
+
+def reduce_body(counts, extra, *refs):
+    groups = len(counts)
+    tiles = sum(counts)
+    theirs, refs = refs[:groups], refs[groups:]
+    ours, refs = refs[:groups], refs[groups:]
+    if extra:
+        mod_theirs, mod_ours, out_ref, mod_out_ref = refs[:4]
+        refs = refs[4:]
+    else:
+        out_ref, refs = refs[0], refs[1:]
+    scratch, mod_scratch = refs[:10], refs[10:]
+    where = places()
+    dp_index, fsdp_index = where[0], where[1]
+    peers = [z_peer(fsdp_index, shift) for shift in (1, 2, 3)]
+    peers += [dp_peer(dp_index, flip) for flip in (1, 2)] + [core_peer(fsdp_index)]
+    greet(peers)
+    entries = [
+        (theirs[group].at[tile], ours[group].at[tile])
+        for group in range(groups)
+        for tile in range(counts[group])
+    ]
+    mod_copies = core_copies([(mod_theirs, mod_ours)], mod_scratch, where) if extra else []
+    copies = core_copies(entries, scratch, where)
+    stages = reduce_stages(tiles, scratch, out_ref, where)
+    if extra:
+        mod_stages = reduce_stages(1, mod_scratch, mod_out_ref, where)
+        mod_copies[0][0].wait()
+        mod_copies[0][1].wait()
+        mod_stages[0](0)
+
+    def arrive(tile):
+        pltpu.make_async_copy(scratch[0].at[0, tile], scratch[0].at[0, tile], scratch[-3].at[0, tile]).wait()
+        pltpu.make_async_remote_copy(
+            scratch[0].at[1, tile], scratch[0].at[1, tile], scratch[-2].at[0, tile], scratch[-1].at[0, tile],
+            device_id=core_peer(fsdp_index), device_id_type=MESH,
+        ).wait_recv()
+
+    def step(position, carried):
+        @pl.when(position < tiles)
+        def _():
+            arrive(position)
+            stages[0](position)
+
+        for place in (1, 2, 3):
+            tile = position - place
+
+            @pl.when((tile >= 0) & (tile < tiles))
+            def _():
+                stages[place](tile)
+
+        return carried
+
+    if extra:
+        step(0, 0)
+        mod_stages[1](0)
+        step(1, 0)
+        mod_stages[2](0)
+        step(2, 0)
+        mod_stages[3](0)
+        lax.fori_loop(3, tiles + 3, step, 0)
+        mod_stages[4](0)
+    else:
+        lax.fori_loop(0, tiles + 3, step, 0)
+
+    def close(tile, carried):
+        stages[4](tile)
+        return carried
+
+    lax.fori_loop(0, tiles, close, 0)
+    for away, load in copies:
+        away.wait_send()
+    store = pltpu.make_async_copy(scratch[6], out_ref, scratch[-3].at[1, 0])
+    store.start()
+    if extra:
+        mod_store = pltpu.make_async_copy(mod_scratch[6], mod_out_ref, mod_scratch[-3].at[1, 0])
+        mod_store.start()
+        mod_store.wait()
+    store.wait()
+
+
+def reduce_tiles(theirs, ours, mods, collective):
+    counts = tuple(part.shape[0] for part in theirs)
+    tiles = sum(counts)
+    rows, width = theirs[0].shape[-2:]
+    bf = jnp.bfloat16
+    operands = list(theirs) + list(ours)
+    out_shape = [jax.ShapeDtypeStruct((tiles, rows, width), bf)]
+    scratch = reduce_scratch(tiles, rows, width)
+    if mods is not None:
+        operands += list(mods)
+        out_shape.append(jax.ShapeDtypeStruct((1, MOD_ROWS, width), bf))
+        scratch = scratch + reduce_scratch(1, MOD_ROWS, width)
     return pl.pallas_call(
-        pick_body,
+        functools.partial(reduce_body, counts, mods is not None),
+        in_specs=[ANY] * len(operands),
+        out_specs=[ANY] * len(out_shape),
+        scratch_shapes=scratch,
+        out_shape=out_shape,
+        compiler_params=comm_params(collective),
+        cost_estimate=pl.CostEstimate(flops=0, bytes_accessed=tiles * 40_000_000, transcendentals=0),
+    )(*operands)
+
+
+def owner_body(counts, index_ref, *refs):
+    sources, refs = refs[: len(counts)], refs[len(counts) :]
+    out_ref, held, picked, load_sems, send_sems, recv_sems = refs
+    dp_index = lax.axis_index("dp")
+    loads, start = [], 0
+    for place, count in enumerate(counts):
+        load = pltpu.make_async_copy(sources[place], held.at[pl.ds(start, count)], load_sems.at[place])
+        load.start()
+        loads.append(load)
+        start += count
+    greet([dp_peer(dp_index, flip) for flip in (1, 2, 3)])
+    for load in loads:
+        load.wait()
+    copies = []
+    for flip in (3, 1, 2, 0):
+        for slot in range(4):
+            picked[flip, slot] = held[index_ref[4 * flip + slot]]
+        target = out_ref.at[:, dp_index]
+        if flip:
+            copies.append(
+                remote(picked.at[flip], target, send_sems.at[flip], recv_sems.at[flip], dp_peer(dp_index, flip))
+            )
+        else:
+            here = pltpu.make_async_copy(picked.at[flip], target, load_sems.at[0])
+            here.start()
+            copies.append(here)
+    for copy in copies:
+        copy.wait()
+
+
+def to_owners(sums, order, tile_slots, collective):
+    rows, width = sums[0].shape[-2:]
+    counts = tuple(part.shape[0] for part in sums)
+    dp_index = lax.axis_index("dp")
+    spots = jnp.arange(16, dtype=jnp.int32)
+    wanted = ((spots // 4) ^ dp_index) * 4 + spots % 4
+    slots = tile_slots[jnp.array(order, jnp.int32)]
+    matches = slots[None, :] == wanted[:, None]
+    index = jnp.sum(jnp.where(matches, spots[None, :], 0), axis=1).astype(jnp.int32)
+    bf = jnp.bfloat16
+    return pl.pallas_call(
+        functools.partial(owner_body, counts),
         grid_spec=pltpu.PrefetchScalarGridSpec(
             num_scalar_prefetch=1,
-            grid=(count,),
-            in_specs=[pl.BlockSpec(block, lambda t, index: (index[t], 0, 0))],
-            out_specs=pl.BlockSpec(block, lambda t, index: (t, 0, 0)),
+            grid=(),
+            in_specs=[ANY] * len(counts),
+            out_specs=ANY,
+            scratch_shapes=[
+                pltpu.VMEM((16, rows, width), bf),
+                pltpu.VMEM((4, 4, rows, width), bf),
+                pltpu.SemaphoreType.DMA((len(counts),)),
+                pltpu.SemaphoreType.DMA((4,)),
+                pltpu.SemaphoreType.DMA((4,)),
+            ],
         ),
-        out_shape=jax.ShapeDtypeStruct((count,) + source.shape[1:], source.dtype),
-    )(index, source)
-
-
-def move_dp(value, flip):
-    owners = lax.axis_size("dp")
-    return lax.ppermute(value, "dp", [(i, i ^ flip) for i in range(owners)])
-
-
-def move_z(value, shift):
-    groups = lax.axis_size("fsdp")
-    return lax.ppermute(value, "fsdp", [(i, (i + 2 * shift) % groups) for i in range(groups)])
-
-
-def assemble_body(tiles, rows, extra, *refs):
-    pieces, refs = refs[:8], refs[8:]
-    out_ref, refs = refs[0], refs[1:]
-    extra_ref, refs = (refs[0], refs[1:]) if extra else (None, refs)
-    hold, in_sem, out_sem, send_sem, recv_sem = refs
+        out_shape=jax.ShapeDtypeStruct((4, 4, rows, width), bf),
+        compiler_params=comm_params(collective),
+        cost_estimate=pl.CostEstimate(flops=0, bytes_accessed=50_000_000, transcendentals=0),
+    )(index, *sums)
+
+
+def half_sums(form, left, right):
+    core = lax.axis_index("fsdp") % 2
+    parts = left.reshape(left.shape[:-1] + (4, 2, left.shape[-1] // 8))
+    shape = parts.shape[:-3] + (left.shape[-1] // 2,)
+    halves = []
+    for side in (1 - core, core):
+        half = lax.dynamic_index_in_dim(parts, side, parts.ndim - 2, keepdims=False).reshape(shape)
+        total = contract(form, half, right).astype(jnp.bfloat16)
+        halves.append(total.reshape(-1, 4, 4, total.shape[-2] // 16, total.shape[-1]))
+    return halves
+
+
+def mod_halves(grad_modulation):
+    rows, width = grad_modulation.shape
+    columns = width // 32
+    core = lax.axis_index("fsdp") % 2
+    blocks = grad_modulation.reshape(rows, 4, 4, 2, columns).transpose(3, 2, 1, 0, 4)
+    flat = blocks.astype(jnp.bfloat16).reshape(2, 4, 4, rows * columns)
+    flat = jnp.pad(flat, ((0, 0), (0, 0), (0, 0), (0, MOD_ROWS * 1024 - rows * columns)))
+    flat = flat.reshape(2, 4, 4, MOD_ROWS, 1024)
+    return [lax.dynamic_index_in_dim(flat, side, 0, keepdims=False) for side in (1 - core, core)]
+
+def after(value, *others):
+    return lax.optimization_barrier((value,) + others)[0]
+
+
+def weight_source(master, modulation, tile_slots):
+    if not fast_layout(master):
+        chunks, mod_all = fetch_generic(master, modulation, tile_slots)
+        return (lambda number, *others: chunks[number]), mod_all
+    slots_here, row_count, width = master.shape
     dp_index = lax.axis_index("dp")
-    fsdp_index = lax.axis_index("fsdp")
-    z_index, core = fsdp_index // 2, fsdp_index % 2
-    partner = {"fsdp": fsdp_index + 1 - 2 * core}
-    loads = []
-    for position in range(16):
-        half, side, turn = position // 8, (position // 4) % 2, position % 4
-        load = pltpu.make_async_copy(
-            pieces[half * 4 + turn].at[side], hold.at[position], in_sem.at[position]
-        )
-        load.start()
-        loads.append(load)
-    barrier = pltpu.get_barrier_semaphore()
-    pl.semaphore_signal(barrier, inc=1, device_id=partner, device_id_type=MESH)
-    pl.semaphore_wait(barrier, 1)
-    copies = []
-    for position in range(16):
-        half, side, turn = position // 8, (position // 4) % 2, position % 4
-        z_from = (z_index + 8 - (2 * half + side)) % 4
-        quarter = dp_index ^ turn
-        loads[position].wait()
-        targets = [(slice(tile * rows, (tile + 1) * rows), out_ref.at[tile]) for tile in range(tiles)]
-        if extra:
-            targets.append((slice(tiles * rows, tiles * rows + extra), extra_ref))
-        for place, (window, target) in enumerate(targets):
-            source = hold.at[position, window]
-            target = target.at[z_from, core, quarter]
-            away = pltpu.make_async_remote_copy(
-                source,
-                target,
-                send_sem.at[position, place],
-                recv_sem.at[position, place],
-                device_id=partner,
-                device_id_type=MESH,
-            )
-            away.start()
-            here = pltpu.make_async_copy(source, target, out_sem.at[position, place])
-            here.start()
-            copies.append((away, here))
-    for away, here in copies:
-        away.wait()
-        here.wait()
-
-
-def assemble(pieces, tiles, rows, extra, collective):
-    width = pieces[0].shape[2]
-    places = tiles + (1 if extra else 0)
-    out_shape = [jax.ShapeDtypeStruct((tiles, 4, 2, 4, rows, width), jnp.bfloat16)]
-    if extra:
-        out_shape.append(jax.ShapeDtypeStruct((4, 2, 4, extra, width), jnp.bfloat16))
-    any_spec = pl.BlockSpec(memory_space=pl.ANY)
-    return pl.pallas_call(
-        functools.partial(assemble_body, tiles, rows, extra),
-        out_shape=out_shape,
-        in_specs=[any_spec] * 8,
-        out_specs=[any_spec] * len(out_shape),
-        scratch_shapes=[
-            pltpu.VMEM((16, tiles * rows + extra, width), jnp.bfloat16),
-            pltpu.SemaphoreType.DMA((16,)),
-            pltpu.SemaphoreType.DMA((16, places)),
-            pltpu.SemaphoreType.DMA((16, places)),
-            pltpu.SemaphoreType.DMA((16, places)),
-        ],
-        compiler_params=pltpu.CompilerParams(collective_id=collective, has_side_effects=True),
-        cost_estimate=pl.CostEstimate(
-            flops=0, bytes_accessed=5 * tiles * 16 * rows * width * 2, transcendentals=0
-        ),
-    )(*pieces)
-
-
-def fetch_weights(master, modulation, tile_slots):
-    owners, groups = lax.axis_size("dp"), lax.axis_size("fsdp")
-    if owners != 4 or groups != 8 or master.shape[1] != 128:
-        return fetch_generic(master, modulation, tile_slots)
-    slots_here, row_count, width = master.shape
-    rows = row_count // owners
-    dp_index = lax.axis_index("dp")
-    narrow = master.astype(jnp.bfloat16).reshape(slots_here, owners, rows, width)
-    parts = []
-    for flip in range(4):
-        part = lax.dynamic_index_in_dim(narrow, dp_index ^ flip, 1, keepdims=False)
-        parts.append(part if flip == 0 else move_dp(part, flip))
-    stacked = jnp.concatenate(parts, axis=0)
+    narrow = master.astype(jnp.bfloat16).reshape(slots_here, 4, row_count // 4, width)
     index = ((tile_slots // slots_here) ^ dp_index) * slots_here + tile_slots % slots_here
-    order = jnp.array([tile for chunk in CHUNKS for tile in chunk], jnp.int32)
-    mine = pick_rows(stacked, index[order]).reshape(-1, width)
+    index = index[jnp.array([tile for chunk in CHUNKS for tile in chunk], jnp.int32)]
     mod_rows, mod_columns = modulation.shape
     mod_flat = modulation.astype(jnp.bfloat16).reshape(-1)
     mod_flat = jnp.pad(mod_flat, (0, MOD_ROWS * width - mod_flat.shape[0])).reshape(MOD_ROWS, width)
-    chunks, mod_all, start, previous = [], None, 0, None
-    for number, chunk in enumerate(CHUNKS):
-        tiles = len(chunk)
-        local = mine[start * rows : (start + tiles) * rows]
-        start += tiles
-        extra = MOD_ROWS if number == 0 else 0
-        if extra:
-            local = jnp.concatenate([local, mod_flat], axis=0)
-        if previous is not None:
-            local, unused_order = lax.optimization_barrier((local, previous))
-        arrived = [local] + [move_z(local, shift) for shift in (1, 2, 3)]
-        low, high = jnp.stack(arrived[:2]), jnp.stack(arrived[2:])
-        previous = high
-        low_x, high_y = move_dp(low, 1), move_dp(high, 2)
-        low_y, high_x = move_dp(low, 2), move_dp(high, 1)
-        low_xy, high_xy = move_dp(low_x, 2), move_dp(high_y, 1)
-        pieces = (low, low_x, low_y, low_xy, high, high_x, high_y, high_xy)
-        outs = assemble(pieces, tiles, rows, extra, number)
-        chunks.append(outs[0].reshape(tiles, 32 * rows, width))
-        if extra:
-            flat = outs[1].reshape(8, 4, MOD_ROWS * width)[:, :, : mod_rows * mod_columns]
-            mod_all = flat.reshape(8, 4, mod_rows, mod_columns).transpose(2, 1, 0, 3)
-            mod_all = mod_all.reshape(mod_rows, -1)
-    return chunks, mod_all
+    first, mods, zoned, rest = first_gather(narrow, mod_flat, index)
+    flat = mods.reshape(8, 4, MOD_ROWS * width)[:, :, : mod_rows * mod_columns]
+    mod_all = flat.reshape(8, 4, mod_rows, mod_columns).transpose(2, 1, 0, 3).reshape(mod_rows, -1)
+
+    def chunk(number, *others):
+        tiles = len(CHUNKS[number])
+        if number == 0:
+            return first.reshape(tiles, row_count * 8, width)
+        if number < 3:
+            return next_gather(after(zoned, *others), tiles, (0, 2)[number - 1], True, number)
+        return next_gather(after(rest, *others), tiles, (0, 4)[number - 3], False, number)
+
+    return chunk, mod_all
 
 
 def exchange(pieces):
@@ -467,13 +900,12 @@
     cotangent,
 ):
     objects, tri_local, model_width = triplane.shape
-    img_local = image_tokens.shape[1]
     groups = lax.axis_size("fsdp")
-    owners = lax.axis_size("dp")
     tri_total = tri_local * groups
     head_width = model_width // groups
-    tile_count = master.shape[0] * owners
-    chunks, mod_all = fetch_weights(master, modulation, tile_slots)
+    fast = fast_layout(master)
+    partial_sums = half_sums if fast else contract
+    chunk, mod_all = weight_source(master, modulation, tile_slots)
     mod_full = mod_all.astype(jnp.float32)
     modulations = (
         jnp.dot(camera, mod_full[:-1], precision=HIGHEST, preferred_element_type=jnp.float32)
@@ -483,30 +915,40 @@
         modulations[:, position * model_width : (position + 1) * model_width][:, None, :]
         for position in range(9)
     ]
-    tiles_qkv, tiles_pair, tiles_mixed, tiles_up, tiles_down = chunks
-    tile_out_one, tile_query_two, tile_out_two = tiles_mixed[0], tiles_mixed[1], tiles_mixed[2]
+    tiles_qkv = chunk(0)
     residual_in = triplane.astype(jnp.float32)
     normed_one = modulate(residual_in, blocks[0], blocks[1]).astype(jnp.bfloat16)
     triples = contract("otd,kde->otke", normed_one, tiles_qkv).astype(jnp.bfloat16)
-    triple_heads = exchange(by_head(triples, groups))
+    triple_sent = by_head(triples, groups)
+    triple_heads = exchange(triple_sent)
+    tiles_pair = chunk(1, triple_sent)
+    triple_heads = after(triple_heads, tiles_pair)
+    image_pairs = contract("oid,kde->oike", image_tokens, tiles_pair).astype(jnp.bfloat16)
+    pair_sent = by_head(image_pairs, groups)
+    pair_heads = exchange(pair_sent)
+    triple_heads = after(triple_heads, pair_sent)
     every_key = jnp.full((objects,), tri_total, jnp.int32)
     self_sources = [source(triple_heads, index, head_width) for index in range(3)]
     self_result, self_logsum = attend_forward(every_key, *self_sources, tri_total, VIEW)
-    merged_one = from_head(exchange(self_result), 1)[:, :, 0]
+    tiles_mixed = chunk(2, self_result, pair_sent)
+    tile_out_one, tile_query_two, tile_out_two = tiles_mixed[0], tiles_mixed[1], tiles_mixed[2]
+    merged_one = from_head(after(exchange(self_result), tiles_mixed), 1)[:, :, 0]
     branch_one = contract("otd,de->ote", merged_one, tile_out_one)
     residual_mid = residual_in + blocks[2] * branch_one
     normed_two = modulate(residual_mid, blocks[3], blocks[4]).astype(jnp.bfloat16)
     cross_query = contract("otd,de->ote", normed_two, tile_query_two).astype(jnp.bfloat16)
-    image_pairs = contract("oid,kde->oike", image_tokens, tiles_pair).astype(jnp.bfloat16)
-    query_heads = exchange(by_head(cross_query[:, :, None], groups))
-    pair_heads = exchange(by_head(image_pairs, groups))
+    query_sent = by_head(cross_query[:, :, None], groups)
+    query_heads = exchange(query_sent)
+    tiles_up = chunk(3, query_sent)
+    query_heads = after(query_heads, tiles_up)
     cross_sources = [
         source(query_heads, 0, head_width),
         source(pair_heads, 0, head_width),
         source(pair_heads, 1, head_width),
     ]
     cross_result, cross_logsum = attend_forward(view_tokens, *cross_sources, tri_total, VIEW)
-    merged_two = from_head(exchange(cross_result), 1)[:, :, 0]
+    tiles_down = chunk(4, cross_result)
+    merged_two = from_head(after(exchange(cross_result), tiles_down), 1)[:, :, 0]
     branch_two = contract("otd,de->ote", merged_two, tile_out_two)
     residual_late = residual_mid + blocks[5] * branch_two
     normed_three = modulate(residual_late, blocks[6], blocks[7]).astype(jnp.bfloat16)
@@ -517,11 +959,9 @@
     grad_final = cotangent.astype(jnp.float32)
     grad_gate_three = jnp.sum(grad_final * branch_three, axis=1)
     grad_branch_three = (blocks[8] * grad_final).astype(jnp.bfloat16)
-    grad_down = contract("otkd,ote->kde", hidden, grad_branch_three)
     grad_hidden = contract("ote,kde->otkd", grad_branch_three, tiles_down)
     unused_gelu, gelu_pull = jax.vjp(gelu_tanh, hidden_pre)
     grad_pre = gelu_pull(grad_hidden)[0].astype(jnp.bfloat16)
-    grad_up = contract("otd,otke->kde", normed_three, grad_pre)
     grad_normed_three = contract("otke,kde->otd", grad_pre, tiles_up)
     grad_late_norm, grad_shift_three, grad_scale_three = modulate_back(
         residual_late, blocks[6], blocks[7], grad_normed_three
@@ -529,17 +969,27 @@
     grad_late = grad_final + grad_late_norm
     grad_gate_two = jnp.sum(grad_late * branch_two, axis=1)
     grad_branch_two = (blocks[5] * grad_late).astype(jnp.bfloat16)
-    grad_out_two = contract("otd,ote->de", merged_two, grad_branch_two)
     grad_merged_two = contract("ote,de->otd", grad_branch_two, tile_out_two).astype(jnp.bfloat16)
-    grad_cross_heads = exchange(by_head(grad_merged_two[:, :, None], groups))
+    grad_cross_sent = by_head(grad_merged_two[:, :, None], groups)
+    grad_cross_heads = exchange(grad_cross_sent)
+    grad_down = partial_sums("otkd,ote->kde", hidden, grad_branch_three)
+    grad_up = partial_sums("otd,otke->kde", normed_three, grad_pre)
+    grad_out_two = partial_sums("otd,ote->de", merged_two, grad_branch_two)
+    if fast:
+        theirs, ours = after(tuple(grad_down), grad_cross_sent)
+        (sums_down,) = reduce_tiles([theirs], [ours], None, 5)
+        grad_cross_heads = after(grad_cross_heads, sums_down)
     grad_query_heads, grad_pair_heads = attend_backward(
         view_tokens, *cross_sources, cross_result, cross_logsum, grad_cross_heads, VIEW
     )
-    grad_query_two = from_head(exchange(grad_query_heads), 1)[:, :, 0]
-    grad_pairs = from_head(exchange(grad_pair_heads), 2)
-    grad_tile_query = contract("otd,ote->de", normed_two, grad_query_two)
-    grad_tiles_pair = contract("oid,oike->kde", image_tokens, grad_pairs)
-    grad_image = contract("oike,kde->oid", grad_pairs, tiles_pair)
+    grad_query_back = exchange(grad_query_heads)
+    grad_pair_back = exchange(grad_pair_heads)
+    if fast:
+        theirs, ours = after(tuple(grad_up), grad_pair_heads, sums_down)
+        (sums_up,) = reduce_tiles([theirs], [ours], None, 6)
+        grad_query_back = after(grad_query_back, sums_up)
+    grad_query_two = from_head(grad_query_back, 1)[:, :, 0]
+    grad_tile_query = partial_sums("otd,ote->de", normed_two, grad_query_two)
     grad_normed_two = contract("ote,de->otd", grad_query_two, tile_query_two)
     grad_mid_norm, grad_shift_two, grad_scale_two = modulate_back(
         residual_mid, blocks[3], blocks[4], grad_normed_two
@@ -547,15 +997,30 @@
     grad_mid = grad_late + grad_mid_norm
     grad_gate_one = jnp.sum(grad_mid * branch_one, axis=1)
     grad_branch_one = (blocks[2] * grad_mid).astype(jnp.bfloat16)
-    grad_out_one = contract("otd,ote->de", merged_one, grad_branch_one)
     grad_merged_one = contract("ote,de->otd", grad_branch_one, tile_out_one).astype(jnp.bfloat16)
-    grad_self_heads = exchange(by_head(grad_merged_one[:, :, None], groups))
+    grad_self_sent = by_head(grad_merged_one[:, :, None], groups)
+    grad_self_heads = exchange(grad_self_sent)
+    grad_out_one = partial_sums("otd,ote->de", merged_one, grad_branch_one)
+    if fast:
+        halves = after(tuple(grad_out_two) + tuple(grad_tile_query), grad_self_sent, sums_up)
+        (sums_mid,) = reduce_tiles([halves[0], halves[2]], [halves[1], halves[3]], None, 7)
+        grad_self_heads = after(grad_self_heads, sums_mid)
     grad_self_query, grad_self_pair = attend_backward(
         every_key, *self_sources, self_result, self_logsum, grad_self_heads, VIEW
     )
     grad_triple_heads = jnp.concatenate([grad_self_query, grad_self_pair], axis=-1)
-    grad_triples = from_head(exchange(grad_triple_heads), 3)
-    grad_qkv = contract("otd,otke->kde", normed_one, grad_triples)
+    grad_triple_back = exchange(grad_triple_heads)
+    if fast:
+        grad_pair_back = after(grad_pair_back, grad_triple_heads)
+    grad_pairs = from_head(grad_pair_back, 2)
+    grad_tiles_pair = partial_sums("oid,oike->kde", image_tokens, grad_pairs)
+    grad_image = contract("oike,kde->oid", grad_pairs, tiles_pair)
+    if fast:
+        halves = after(tuple(grad_tiles_pair) + tuple(grad_out_one), grad_triple_heads, sums_mid)
+        (sums_late,) = reduce_tiles([halves[0], halves[2]], [halves[1], halves[3]], None, 8)
+        grad_triple_back = after(grad_triple_back, sums_late)
+    grad_triples = from_head(grad_triple_back, 3)
+    grad_qkv = partial_sums("otd,otke->kde", normed_one, grad_triples)
     grad_normed_one = contract("otke,kde->otd", grad_triples, tiles_qkv)
     grad_in_norm, grad_shift_one, grad_scale_one = modulate_back(
         residual_in, blocks[0], blocks[1], grad_normed_one
@@ -581,48 +1046,21 @@
     grad_modulation = jnp.concatenate(
         [grad_mod_rows, jnp.sum(grad_mods, axis=0, keepdims=True)], axis=0
     )
-    mod_columns = modulation.shape[1]
-    grad_mod_blocks = grad_modulation.reshape(grad_modulation.shape[0], owners, groups, mod_columns)
-    logical = [
-        grad_qkv[0],
-        grad_qkv[1],
-        grad_qkv[2],
-        grad_out_one,
-        grad_tile_query,
-        grad_tiles_pair[0],
-        grad_tiles_pair[1],
-        grad_out_two,
-        grad_up[0],
-        grad_up[1],
-        grad_up[2],
-        grad_up[3],
-        grad_down[0],
-        grad_down[1],
-        grad_down[2],
-        grad_down[3],
-    ]
-    slot_grads = jnp.zeros((tile_count, model_width, model_width), jnp.float32)
-    for position in range(tile_count):
-        slot_grads = lax.dynamic_update_index_in_dim(
-            slot_grads, logical[position], tile_slots[position], 0
-        )
-    row_sums, mod_row_sums = (
-        lax.psum_scatter(
-            slot_grads.astype(jnp.bfloat16), "fsdp", scatter_dimension=1, tiled=True
-        ).astype(jnp.float32),
-        lax.psum_scatter(
-            grad_mod_blocks.astype(jnp.bfloat16), "fsdp", scatter_dimension=2, tiled=True
-        ).astype(jnp.float32),
-    )
-    tile_grad, mod_grad = (
-        lax.psum_scatter(
-            row_sums.astype(jnp.bfloat16), "dp", scatter_dimension=0, tiled=True
-        ).astype(jnp.float32),
-        lax.psum_scatter(
-            mod_row_sums.astype(jnp.bfloat16), "dp", scatter_dimension=1, tiled=True
-        ).astype(jnp.float32),
-    )
-    mod_grad = mod_grad.reshape(mod_grad.shape[0], mod_columns)
+    if fast:
+        theirs, ours = after(tuple(grad_qkv), sums_late)
+        sums_qkv, mod_sum = reduce_tiles([theirs], [ours], mod_halves(grad_modulation), 9)
+        sums = [sums_qkv, sums_late, sums_mid, sums_up, sums_down]
+        order = (0, 1, 2, 5, 6, 3, 7, 4, 8, 9, 10, 11, 12, 13, 14, 15)
+        tile_grad = to_owners(sums, order, tile_slots, 10).reshape(master.shape)
+        mod_grad = mod_sum.reshape(-1)[: modulation.size].reshape(modulation.shape)
+        tile_grad, mod_grad = tile_grad.astype(jnp.float32), mod_grad.astype(jnp.float32)
+    else:
+        logical = [grad_qkv[0], grad_qkv[1], grad_qkv[2], grad_out_one, grad_tile_query]
+        logical = logical + [grad_tiles_pair[0], grad_tiles_pair[1], grad_out_two]
+        logical = logical + [grad_up[tile] for tile in range(4)]
+        logical = logical + [grad_down[tile] for tile in range(4)]
+        tile_grad = sums_generic(logical, tile_slots).astype(jnp.float32)
+        mod_grad = mod_generic(grad_modulation)
     new_master, new_moment1, new_moment2 = adamw(master, tile_grad, moment1, moment2, RATE_TILES)
     new_modulation, new_mod_moment1, new_mod_moment2 = adamw(
         modulation, mod_grad, mod_moment1, mod_moment2, RATE_MODULATION

time: 1380 us -> 1110 us (0.80)
  waiting for transfers between devices: 686 us -> 94 us
  Pallas kernels: 140 us -> 668 us
  blocking collectives: 101 us -> 38.5 us
  between operations: 45.9 us -> 2.14 us
  local copies, waits for them, and re-layouts: 184 us -> 141 us
  starting transfers between devices: 95.1 us -> 52.1 us
    pallas_call x6 -> x11, Pallas kernels: 51.8 us -> 553 us  [the longest x5 296 us: reduce_tiles(): pl.pallas_call(functools.partial(reduce_body, counts, mods is not None),...]
    reduce_scatter x2 -> x0, waiting for transfers between devices: 381 us -> none  [the longest x1 337 us: shards(): lax.psum_scatter(slot_grads.astype(jnp.bfloat16), 'fsdp', scatter_dimensi...]
    ppermute x48 -> x0, waiting for transfers between devices: 282 us -> none  [the longest x15 199 us: move_z(): lax.ppermute(value, 'fsdp', [(i, (i + 2 * shift) % groups) for i in range...]
    all_to_all x6 -> x8, waiting for transfers between devices: 0.02 us -> 94 us  [exchange(): lax.all_to_all(pieces, 'fsdp', split_axis=0, concat_axis=0, tiled=True)]
    ppermute x48 -> x0, starting transfers between devices: 67.6 us -> none  [the longest x33 45.2 us: move_dp(): return lax.ppermute(value, 'dp', [(i, i ^ flip) for i in range(owners)])]
    all_to_all x4 -> x2, blocking collectives: 101 us -> 38.5 us  [exchange(): lax.all_to_all(pieces, 'fsdp', split_axis=0, concat_axis=0, tiled=True)]
    slice x17 -> x1, local copies, waits for them, and re-layouts: 49.8 us -> 0.11 us  [weight_source(): flat = mods.reshape(8, 4, MOD_ROWS * width)[:, :, :mod_rows * mod_columns]]
    dynamic_slice x0 -> x19, local copies, waits for them, and re-layouts: none -> 36.4 us  [half_sums(): lax.dynamic_index_in_dim(parts, side, parts.ndim - 2, keepdims=False)]
  transfers between devices with their start and end apart: 58 -> 8, of which waited for: 26 -> 1; matrix products, arithmetic and copies ran while one was open for 15% -> 13% of each run, Pallas kernels for 5% -> 39%
where the time goes in v2:
time: 1110 us; the launch traced here: 1120 us
  Pallas kernels  668 us (60%)
  local copies, waits for them, and re-layouts  141 us (13%)
  matrix products  104 us (9%)
  waiting for transfers between devices  94 us (8%)
  starting transfers between devices  52.1 us (5%)
  blocking collectives  38.5 us (3%)
  other arithmetic  16.5 us (1%)
    pallas_call x5, Pallas kernels, reduce_tiles(): pl.pallas_call(functools.partial(reduce_body, counts, mods is not None),...  296 us
    pallas_call x4, Pallas kernels, next_gather(): pl.pallas_call(functools.partial(next_gather_body, tiles, start, zoned),...  168 us
    dot_general x28, matrix products, contract(): return jnp.einsum(form, left, right, preferred_element_type=jnp.float32)  103 us
    all_to_all x8, waiting for transfers between devices, exchange(): lax.all_to_all(pieces, 'fsdp', split_axis=0, concat_axis=0, tiled=True)  94 us
    pallas_call x1, Pallas kernels, first_gather(): pl.pallas_call(functools.partial(first_gather_body, tiles, rows), grid_sp...  73.2 us
    pallas_call x2, Pallas kernels, attend_backward(): pl.pallas_call(cross_backward_body, grid_spec=pltpu.PrefetchScalarGridSpe...  66.5 us
    all_to_all x8, starting transfers between devices, exchange(): lax.all_to_all(pieces, 'fsdp', split_axis=0, concat_axis=0, tiled=True)  52.1 us
    pallas_call x2, Pallas kernels, attend_forward(): pl.pallas_call(functools.partial(forward_body, step_rows), grid_spec=pltp...  49.3 us
  transfers between devices with their start and end apart: 8, of which 1 were waited for; matrix products, arithmetic and copies ran while one was open for 13% of the time, Pallas kernels for 39%

profile of v2, /device:TPU:0, one launch (start us, length us, event | category | flops | bytes accessed | tf_op | source)
XLA Modules:
  0.0 1115.8 jit_solution(9386982290408471043)
XLA Ops:
  0.7 2.7 convert_element_type.143
  5.4 73.2 %shard_map.213 = (bf16[3,4,2,4,32,1024]{5,4,3,2,1,0:T(8,128)(2,1)}, bf16[4,2,4,16,1024]{4,3,2,1,0:T(8,128)(2,1)}, bf16[4,5,32,1024]{3,2,1,0:T(8,128)(2,1)}, bf16[8,32,1024]{2,1,0:T(8,128)(2,1)}) custom-call(s32[16]{0:T(128)} %gather_fusion, bf16[4,4,32,1024]{3,2,1,0:T(8,128)(2,1)} %bitcast.326, bf16[16,1024]{1,0:T(8,128)(2,1)} %reshape.345.mod_ref), custom_call_target="tpu_custom_call" | custom-call | bytes 200000000 | tf_op jit(solution)/shard_map/pallas_call | solution.py:410
  83.3 4.8 convolution_convert_fusion.2
  90.4 2.6 copy.135
  93.0 4.8 all-to-all-start
  97.8 23.5 %shard_map.214 = bf16[2,4,2,4,32,1024]{5,4,3,2,1,0:T(8,128)(2,1)} custom-call(bf16[4,5,32,1024]{3,2,1,0:T(8,128)(2,1)} %get-tuple-element.58.source_ref), custom_call_target="tpu_custom_call" | custom-call | bytes 60000000 | tf_op jit(solution)/shard_map/pallas_call | solution.py:476
  121.4 8.4 convolution_convert_fusion.1
  129.8 11.2 copy.137
  140.9 7.6 reshape.353
  149.7 12.7 %shard_map.215 = (bf16[8,2,128,128]{3,2,1,0:T(8,128)(2,1)}, f32[2,2,1,1024]{3,2,1,0:T(1,128)}) custom-call(s32[2]{0:T(128)} %broadcast_31_live_ref.2.live_ref, bf16[8,2,128,384]{3,2,1,0:T(8,128)(2,1)} %copy-done.37, bf16[8,2,128,384]{3,2,1,0:T(8,128)(2,1)} %copy-done.37, bf16[8,2,128,384]{3,2,1,0:T(8,128)(2,1)} %copy-done.37), custom_call_target="tpu_custom_call" | custom-call | flops 1073741824 | bytes 2097152 | tf_op jit(solution)/shard_map/pallas_call | solution.py:115
  162.4 4.7 all-to-all-start.1
  167.1 31.4 %shard_map.216 = bf16[3,4,2,4,32,1024]{5,4,3,2,1,0:T(8,128)(2,1)} custom-call(bf16[4,5,32,1024]{3,2,1,0:T(8,128)(2,1)} %get-tuple-element.58.source_ref), custom_call_target="tpu_custom_call" | custom-call | bytes 90000000 | tf_op jit(solution)/shard_map/pallas_call | solution.py:476
  198.5 5.9 fusion.50
  205.2 3.3 fusion.49
  211.6 19.9 %all_to_all.50.q_ref = bf16[8,2,128,128]{3,2,1,0:T(8,128)(2,1)} all-to-all(bf16[8,2,128,128]{3,2,1,0:T(8,128)(2,1)S(1)} %bitcast.342), channel_id=1, replica_groups=mesh['dp'=4,'fsdp'=8] {'fsdp'}, dimensions={0} | all-to-all | bytes 1048576 | tf_op jit(solution)/shard_map/all_to_all | solution.py:854
  231.5 16.8 %all-to-all-start.3 = ((bf16[8,2,512,256]{3,2,1,0:T(8,128)(2,1)}), bf16[8,2,512,256]{3,2,1,0:T(8,128)(2,1)}, u32[]{:S(2)}, u32[]{:S(2)}) async-start(bf16[8,2,512,256]{3,2,1,0:T(8,128)(2,1)} %reshape.353), calls=%async_computation.3 | async-start | bytes 8388608 | tf_op jit(solution)/shard_map/all_to_all | solution.py:854
  248.4 94.0 %all-to-all-done.3.k_ref.v_ref = bf16[8,2,512,256]{3,2,1,0:T(8,128)(2,1)} async-done(((bf16[8,2,512,256]{3,2,1,0:T(8,128)(2,1)}), bf16[8,2,512,256]{3,2,1,0:T(8,128)(2,1)}, u32[]{:S(2)}, u32[]{:S(2)}) %all-to-all-start.3) | async-done | bytes 4194336 | tf_op jit(solution)/shard_map/all_to_all | solution.py:854
  342.3 36.5 %shard_map.218 = (bf16[8,2,128,128]{3,2,1,0:T(8,128)(2,1)}, f32[2,2,1,1024]{3,2,1,0:T(1,128)}) custom-call(s32[2]{0:T(128)} %live_ref.3, bf16[8,2,128,128]{3,2,1,0:T(8,128)(2,1)} %all_to_all.50.q_ref, bf16[8,2,512,256]{3,2,1,0:T(8,128)(2,1)} %all-to-all-done.3.k_ref.v_ref, bf16[8,2,512,256]{3,2,1,0:T(8,128)(2,1)} %all-to-all-done.3.k_ref.v_ref), custom_call_target="tpu_custom_call" | custom-call | flops 4294967296 | bytes 5242880 | tf_op jit(solution)/shard_map/pallas_call | solution.py:115
  378.9 3.5 all-to-all-start.4
  382.4 60.7 %shard_map.217 = bf16[4,4,2,4,32,1024]{5,4,3,2,1,0:T(8,128)(2,1)} custom-call(bf16[8,32,1024]{2,1,0:T(8,128)(2,1)} %get-tuple-element.63.source_ref), custom_call_target="tpu_custom_call" | custom-call | bytes 120000000 | tf_op jit(solution)/shard_map/pallas_call | solution.py:476
  443.1 52.1 %shard_map.219 = bf16[4,4,2,4,32,1024]{5,4,3,2,1,0:T(8,128)(2,1)} custom-call(bf16[8,32,1024]{2,1,0:T(8,128)(2,1)} %get-tuple-element.63.source_ref), custom_call_target="tpu_custom_call" | custom-call | bytes 120000000 | tf_op jit(solution)/shard_map/pallas_call | solution.py:476
  496.0 3.3 fusion.48
  501.1 8.2 multiply_convert_fusion
  509.3 8.0 fusion.8
  517.3 3.1 multiply_reduce_fusion
  528.5 7.2 all-to-all-start.5
  535.7 4.4 reshape.360
  540.1 9.2 constant_dynamic-slice_fusion.12
  549.3 5.8 copy.146
  555.1 5.8 copy.147
  561.0 4.6 bitcast_convert_fusion.3
  565.6 3.3 bitcast_convert_fusion.2
  568.8 54.5 %shard_map.220.refs_4_ = bf16[4,32,1024]{2,1,0:T(8,128)(2,1)} custom-call(bf16[4,4,4,32,1024]{4,3,2,1,0:T(8,128)(2,1)} %bitcast.300, bf16[4,4,4,32,1024]{4,3,2,1,0:T(8,128)(2,1)} %bitcast.301), custom_call_target="tpu_custom_call" | custom-call | bytes 160000000 | tf_op jit(solution)/shard_map/pallas_call | solution.py:728
  623.4 51.1 %shard_map.221 = (bf16[8,2,128,128]{3,2,1,0:T(8,128)(2,1)}, bf16[8,2,512,256]{3,2,1,0:T(8,128)(2,1)}) custom-call(s32[2]{0:T(128)} %live_ref.3, bf16[8,2,128,128]{3,2,1,0:T(8,128)(2,1)} %all_to_all.50.q_ref, bf16[8,2,512,256]{3,2,1,0:T(8,128)(2,1)} %all-to-all-done.3.k_ref.v_ref, bf16[8,2,512,256]{3,2,1,0:T(8,128)(2,1)} %all-to-all-done.3.k_ref.v_ref, ...), custom_call_target="tpu_custom_call" | custom-call | flops 10737418240 | bytes 10485760 | tf_op jit(solution)/shard_map/pallas_call | solution.py:215
  674.5 5.3 all-to-all-start.6
  679.9 2.1 constant_dynamic-slice_fusion.10
  684.6 5.0 bitcast_convert_fusion.1
  689.6 3.2 bitcast_convert_fusion
  692.8 52.6 %shard_map.222.refs_3_ = bf16[4,32,1024]{2,1,0:T(8,128)(2,1)} custom-call(bf16[4,4,4,32,1024]{4,3,2,1,0:T(8,128)(2,1)} %bitcast.296, bf16[4,4,4,32,1024]{4,3,2,1,0:T(8,128)(2,1)} %bitcast.297), custom_call_target="tpu_custom_call" | custom-call | bytes 160000000 | tf_op jit(solution)/shard_map/pallas_call | solution.py:728
  746.8 2.7 multiply_reduce_fusion.4
  750.9 7.1 fusion.23
  761.3 18.5 %all_to_all.51.grad_ref = bf16[8,2,128,128]{3,2,1,0:T(8,128)(2,1)} all-to-all(bf16[8,2,128,128]{3,2,1,0:T(8,128)(2,1)S(1)} %bitcast.345), channel_id=1, replica_groups=mesh['dp'=4,'fsdp'=8] {'fsdp'}, dimensions={0} | all-to-all | bytes 1048576 | tf_op jit(solution)/shard_map/all_to_all | solution.py:854
  779.8 4.9 all-to-all-start.9
  793.1 96.8 %shard_map.223.refs_2_ = bf16[2,32,1024]{2,1,0:T(8,128)(2,1)} custom-call(bf16[1,4,4,32,1024]{4,3,2,1,0:T(8,128)(2,1)} %bitcast.332, bf16[1,4,4,32,1024]{4,3,2,1,0:T(8,128)(2,1)} %bitcast.334, bf16[1,4,4,32,1024]{4,3,2,1,0:T(8,128)(2,1)} %bitcast.333, bf16[1,4,4,32,1024]{4,3,2,1,0:T(8,128)(2,1)} %bitcast.335), custom_call_target="tpu_custom_call" | custom-call | bytes 80000000 | tf_op jit(solution)/shard_map/pallas_call | solution.py:728
  890.0 15.4 %shard_map.224 = (bf16[8,2,128,128]{3,2,1,0:T(8,128)(2,1)}, bf16[8,2,128,256]{3,2,1,0:T(8,128)(2,1)}) custom-call(s32[2]{0:T(128)} %broadcast_31_live_ref.2.live_ref, bf16[8,2,128,384]{3,2,1,0:T(8,128)(2,1)} %copy-done.37, bf16[8,2,128,384]{3,2,1,0:T(8,128)(2,1)} %copy-done.37, bf16[8,2,128,384]{3,2,1,0:T(8,128)(2,1)} %copy-done.37, ...), custom_call_target="tpu_custom_call" | custom-call | flops 2684354560 | bytes 4194304 | tf_op jit(solution)/shard_map/pallas_call | solution.py:215
  907.3 2.3 constant_dynamic-update-slice_fusion
  909.6 4.7 all-to-all-start.8
  914.3 3.2 reshape.383
  918.9 6.3 constant_dynamic-slice_fusion.4
  925.3 6.0 copy.201
  931.2 4.2 copy.202
  942.0 6.9 reshape.381
  948.9 6.8 copy.160
  955.8 7.5 reshape.382
  963.3 6.0 bitcast_convert_fusion.7
  969.3 3.7 bitcast_convert_fusion.6
  973.0 45.3 %shard_map.225.refs_1_ = bf16[3,32,1024]{2,1,0:T(8,128)(2,1)} custom-call(bf16[2,4,4,32,1024]{4,3,2,1,0:T(8,128)(2,1)} %bitcast.336, bf16[1,4,4,32,1024]{4,3,2,1,0:T(8,128)(2,1)} %bitcast.324, bf16[2,4,4,32,1024]{4,3,2,1,0:T(8,128)(2,1)} %bitcast.337, bf16[1,4,4,32,1024]{4,3,2,1,0:T(8,128)(2,1)} %bitcast.325), custom_call_target="tpu_custom_call" | custom-call | bytes 120000000 | tf_op jit(solution)/shard_map/pallas_call | solution.py:728
  1021.0 4.9 fusion.21
  1028.5 6.2 convolution_bitcast_fusion
  1034.7 2.7 bitcast_convert_fusion.5
  1037.4 2.7 bitcast_convert_fusion.4
  1044.7 46.6 %shard_map.226 = (bf16[3,32,1024]{2,1,0:T(8,128)(2,1)}, bf16[1,16,1024]{2,1,0:T(8,128)(2,1)}) custom-call(bf16[3,4,4,32,1024]{4,3,2,1,0:T(8,128)(2,1)} %bitcast.298, bf16[3,4,4,32,1024]{4,3,2,1,0:T(8,128)(2,1)} %bitcast.299, bf16[4,4,16,1024]{3,2,1,0:T(8,128)(2,1)} %get-tuple-element.128.refs_2_, bf16[4,4,16,1024]{3,2,1,0:T(8,128)(2,1)} %get-tuple-element.127.refs_3_), custom_call_target="tpu_custom_call" | custom-call | bytes 120000000 | tf_op jit(solution)/shard_map/pallas_call | solution.py:728
  1092.3 15.7 %shard_map.227 = bf16[4,4,32,1024]{3,2,1,0:T(8,128)(2,1)} custom-call(s32[16]{0:T(128)} %select_reduce_fusion.index_ref, bf16[3,32,1024]{2,1,0:T(8,128)(2,1)} %get-tuple-element.90.refs_0_, bf16[3,32,1024]{2,1,0:T(8,128)(2,1)} %shard_map.225.refs_1_, bf16[2,32,1024]{2,1,0:T(8,128)(2,1)} %shard_map.223.refs_2_, bf16[4,32,1024]{2,1,0:T(8,128)(2,1)} %shard_map.222.refs_3_, ...), custom_call_target="tpu_custom_call" | custom-call | bytes 50000000 | tf_op jit(solution)/shard_map/pallas_call | solution.py:779
  1108.1 6.8 fusion.45
  (230 shorter events, 62.3 us)
Async XLA Ops:
  0.6 81.5 %copy-start = (f32[2,16]{1,0:T(2,128)S(1)}, f32[2,16]{1,0:T(2,128)}, u32[]{:S(2)}) copy-start(f32[2,16]{1,0:T(2,128)} %param.16) | copy-start | bytes 388
  0.7 3.6 copy-start.52
  0.7 3.6 copy-start.53
  0.7 2.8 copy-start.40
  0.7 3.5 copy-start.1
  80.7 1.8 copy-start.2
  82.5 0.8 copy-start.42
  82.7 5.4 copy-start.46
  82.9 5.1 copy-start.50
  83.0 5.1 copy-start.48
  83.3 4.8 copy-start.33
  93.0 55.5 %all-to-all-start = ((bf16[8,2,128,384]{3,2,1,0:T(8,128)(2,1)}), bf16[8,2,128,384]{3,2,1,0:T(8,128)(2,1)S(1)}, u32[]{:S(2)}, u32[]{:S(2)}) async-start(bf16[8,2,128,384]{3,2,1,0:T(8,128)(2,1)} %copy.135), calls=%async_computation | async-start | bytes 3145728 | tf_op jit(solution)/shard_map/all_to_all | solution.py:854
  97.8 23.5 %copy-start.32 = (bf16[2,512,1024]{2,1,0:T(8,128)(2,1)S(1)}, bf16[2,512,1024]{2,1,0:T(8,128)(2,1)}, u32[]{:S(2)}) copy-start(bf16[2,512,1024]{2,1,0:T(8,128)(2,1)} %param.15) | copy-start | bytes 6291460
  148.5 1.2 copy-start.37
  162.4 42.0 %all-to-all-start.1 = ((bf16[8,2,128,128]{3,2,1,0:T(8,128)(2,1)}), bf16[8,2,128,128]{3,2,1,0:T(8,128)(2,1)S(1)}, u32[]{:S(2)}, u32[]{:S(2)}) async-start(bf16[8,2,128,128]{3,2,1,0:T(8,128)(2,1)} %get-tuple-element.57.out_ref), calls=%async_computation.1 | async-start | bytes 1048576 | tf_op jit(solution)/shard_map/all_to_all | solution.py:854
  204.4 0.8 copy-start.19
  208.5 1.7 copy-start.13
  209.1 0.8 copy-start.34
  231.5 110.8 %all-to-all-start.3 = ((bf16[8,2,512,256]{3,2,1,0:T(8,128)(2,1)}), bf16[8,2,512,256]{3,2,1,0:T(8,128)(2,1)}, u32[]{:S(2)}, u32[]{:S(2)}) async-start(bf16[8,2,512,256]{3,2,1,0:T(8,128)(2,1)} %reshape.353), calls=%async_computation.3 | async-start | bytes 8388608 | tf_op jit(solution)/shard_map/all_to_all | solution.py:854
  378.9 116.4 %all-to-all-start.4 = ((bf16[8,2,128,128]{3,2,1,0:T(8,128)(2,1)}), bf16[8,2,128,128]{3,2,1,0:T(8,128)(2,1)S(1)}, u32[]{:S(2)}, u32[]{:S(2)}) async-start(bf16[8,2,128,128]{3,2,1,0:T(8,128)(2,1)} %get-tuple-element.62.out_ref), calls=%async_computation.4 | async-start | bytes 1048576 | tf_op jit(solution)/shard_map/all_to_all | solution.py:854
  495.2 0.8 copy-start.21
  499.9 1.2 copy-start.36
  501.1 8.2 copy-start.15
  501.1 16.2 %slice-start = ((s8[8388608]{0:T(1024)(128)(4,1)}), s8[4194304]{0:T(1024)(128)(4,1)S(1)}, s32[]{:S(2)}) async-start(s8[8388608]{0:T(1024)(128)(4,1)} %bitcast.308), calls=%async_computation.10 | async-start | bytes 8388608
  509.3 8.0 slice-start.1
  517.3 3.1 copy-start.3
  520.4 2.4 copy-start.14
  520.8 1.0 copy-start.5
  522.1 0.8 copy-start.23
  528.5 94.9 %all-to-all-start.5 = ((bf16[8,2,128,128]{3,2,1,0:T(8,128)(2,1)}), bf16[8,2,128,128]{3,2,1,0:T(8,128)(2,1)}, u32[]{:S(2)}, u32[]{:S(2)}) async-start(bf16[8,2,128,128]{3,2,1,0:T(8,128)(2,1)} %bitcast.340), calls=%async_computation.5 | async-start | bytes 1048576 | tf_op jit(solution)/shard_map/all_to_all | solution.py:854
  561.0 4.6 copy-start.31
  623.4 56.5 %copy-start.25 = (bf16[2,128,4,2,128]{4,3,2,1,0:T(2,128)(2,1)S(1)}, bf16[2,128,4,2,128]{4,3,2,1,0:T(2,128)(2,1)}, u32[]{:S(2)}) copy-start(bf16[2,128,4,2,128]{4,3,2,1,0:T(2,128)(2,1)} %reshape.365) | copy-start | bytes 1572868
  674.5 70.9 %all-to-all-start.6 = ((bf16[8,2,128,128]{3,2,1,0:T(8,128)(2,1)}), bf16[8,2,128,128]{3,2,1,0:T(8,128)(2,1)}, u32[]{:S(2)}, u32[]{:S(2)}) async-start(bf16[8,2,128,128]{3,2,1,0:T(8,128)(2,1)} %get-tuple-element.69), calls=%async_computation.6 | async-start | bytes 1048576 | tf_op jit(solution)/shard_map/all_to_all | solution.py:854
  684.6 5.0 copy-start.4
  746.8 3.3 copy-start.10
  746.8 3.3 copy-start.26
  746.8 3.3 copy-start.30
  749.5 1.3 copy-start.6
  749.5 1.4 copy-start.16
  750.9 9.0 copy-start.12
  758.0 1.0 copy-start.7
  759.1 0.8 copy-start.17
  779.8 4.9 copy-start.35
  779.8 129.8 %all-to-all-start.9 = ((bf16[8,2,512,256]{3,2,1,0:T(8,128)(2,1)}), bf16[8,2,512,256]{3,2,1,0:T(8,128)(2,1)}, u32[]{:S(2)}, u32[]{:S(2)}) async-start(bf16[8,2,512,256]{3,2,1,0:T(8,128)(2,1)} %get-tuple-element.70), calls=%async_computation.9 | async-start | bytes 8388608 | tf_op jit(solution)/shard_map/all_to_all | solution.py:854
  785.1 1.9 copy-start.22
  786.2 1.3 copy-start.24
  909.6 108.8 %all-to-all-start.8 = ((bf16[8,2,128,384]{3,2,1,0:T(8,128)(2,1)}), bf16[8,2,128,384]{3,2,1,0:T(8,128)(2,1)}, u32[]{:S(2)}, u32[]{:S(2)}) async-start(bf16[8,2,128,384]{3,2,1,0:T(8,128)(2,1)} %constant_dynamic-update-slice_fusion), calls=%async_computation.8 | async-start | bytes 3145728 | tf_op jit(solution)/shard_map/all_to_all | solution.py:854
  925.3 6.0 copy-start.11
  935.5 3.3 copy-start.20
  937.2 1.9 copy-start.18
  955.8 7.5 copy-start.38
  963.3 6.0 copy-start.28
  963.3 6.0 copy-start.39
  1020.3 0.7 copy-start.43
  1020.3 0.7 copy-start.47
  1021.0 4.9 copy-start.51
  1021.0 5.0 copy-start.49
  1021.0 7.5 copy-start.29
  1025.9 1.2 copy-start.8
  1025.9 2.6 copy-start.27
  1091.3 16.8 %copy-start.9 = (f32[4,128,1024]{2,1,0:T(8,128)S(1)}, f32[4,128,1024]{2,1,0:T(8,128)}, u32[]{:S(2)}) copy-start(f32[4,128,1024]{2,1,0:T(8,128)} %param.18) | copy-start | bytes 6291460
  1108.0 6.9 copy-start.41
  1108.1 6.9 copy-start.44
  1108.1 6.9 copy-start.45

commit v3 on v2

--- a/solution.py
+++ b/solution.py
@@ -103,27 +103,26 @@
 
 def attend_forward(live, query_source, key_source, value_source, query_block, step_rows):
     (q_array, q_at), (k_array, k_at), (v_array, v_at) = query_source, key_source, value_source
-    groups, objects, q_rows, unused_width = q_array.shape
-    k_rows = k_array.shape[2]
-    width = q_at[1]
+    groups, unused_blocks, objects, q_rows, width = q_array.shape
+    k_rows = k_array.shape[3]
     heads = width // HD
     total_q = groups * q_rows
     per_q = query_block // q_rows
     grid = (objects, total_q // query_block)
-    whole = lambda index: (lambda o, j, live: (0, o, 0, index))
-    part = lambda index: (lambda o, j, live: (j, o, 0, index))
+    whole = lambda index: (lambda o, j, live: (0, index, o, 0, 0))
+    part = lambda index: (lambda o, j, live: (j, index, o, 0, 0))
     return pl.pallas_call(
         functools.partial(forward_body, step_rows),
         grid_spec=pltpu.PrefetchScalarGridSpec(
             num_scalar_prefetch=1,
             grid=grid,
             in_specs=[
-                pl.BlockSpec((per_q, 1, q_rows, width), part(q_at[0])),
-                pl.BlockSpec((groups, 1, k_rows, width), whole(k_at[0])),
-                pl.BlockSpec((groups, 1, k_rows, width), whole(v_at[0])),
+                pl.BlockSpec((per_q, None, 1, q_rows, width), part(q_at)),
+                pl.BlockSpec((groups, None, 1, k_rows, width), whole(k_at)),
+                pl.BlockSpec((groups, None, 1, k_rows, width), whole(v_at)),
             ],
             out_specs=[
-                pl.BlockSpec((per_q, 1, q_rows, width), part(0)),
+                pl.BlockSpec((per_q, 1, q_rows, width), lambda o, j, live: (j, o, 0, 0)),
                 pl.BlockSpec((1, heads, 1, query_block), lambda o, j, live: (o, 0, 0, j)),
             ],
         ),
@@ -189,8 +188,8 @@
         grad_q, grad_k, grad_v = backward_block(keys, values, lse_ref, qs, gs, delta)
         dq_acc[...] += grad_q
         shape = (k_ref.shape[0], 1, k_ref.shape[2], width)
-        dkv_ref[:, :, :, 0:width] = grad_k.astype(jnp.bfloat16).reshape(shape)
-        dkv_ref[:, :, :, width : 2 * width] = grad_v.astype(jnp.bfloat16).reshape(shape)
+        dkv_ref[:, 0] = grad_k.astype(jnp.bfloat16).reshape(shape)
+        dkv_ref[:, 1] = grad_v.astype(jnp.bfloat16).reshape(shape)
 
     @pl.when(jnp.logical_not(alive))
     def _():
@@ -203,31 +202,31 @@
 
 def attend_backward(live, query_source, key_source, value_source, outs, lse, grads, step_rows):
     (q_array, q_at), (k_array, k_at), (v_array, v_at) = query_source, key_source, value_source
-    groups, objects, q_rows, unused_width = q_array.shape
-    k_rows = k_array.shape[2]
-    width = q_at[1]
+    groups, unused_blocks, objects, q_rows, width = q_array.shape
+    k_rows = k_array.shape[3]
     heads = width // HD
     total_q = groups * q_rows
     per_k = max(step_rows // k_rows, 1)
     grid = (objects, groups // per_k)
-    whole = lambda index: (lambda o, j, live: (0, o, 0, index))
-    part = lambda index: (lambda o, j, live: (j, o, 0, index))
+    whole = lambda index: (lambda o, j, live: (0, index, o, 0, 0))
+    part = lambda index: (lambda o, j, live: (j, index, o, 0, 0))
+    tokens = pl.BlockSpec((groups, 1, q_rows, width), lambda o, j, live: (0, o, 0, 0))
     return pl.pallas_call(
         cross_backward_body,
         grid_spec=pltpu.PrefetchScalarGridSpec(
             num_scalar_prefetch=1,
             grid=grid,
             in_specs=[
-                pl.BlockSpec((groups, 1, q_rows, width), whole(q_at[0])),
-                pl.BlockSpec((per_k, 1, k_rows, width), part(k_at[0])),
-                pl.BlockSpec((per_k, 1, k_rows, width), part(v_at[0])),
-                pl.BlockSpec((groups, 1, q_rows, width), whole(0)),
+                pl.BlockSpec((groups, None, 1, q_rows, width), whole(q_at)),
+                pl.BlockSpec((per_k, None, 1, k_rows, width), part(k_at)),
+                pl.BlockSpec((per_k, None, 1, k_rows, width), part(v_at)),
+                tokens,
                 pl.BlockSpec((1, heads, 1, total_q), lambda o, j, live: (o, 0, 0, 0)),
-                pl.BlockSpec((groups, 1, q_rows, width), whole(0)),
+                pl.BlockSpec((groups, None, 1, q_rows, width), whole(0)),
             ],
             out_specs=[
-                pl.BlockSpec((groups, 1, q_rows, width), whole(0)),
-                pl.BlockSpec((per_k, 1, k_rows, 2 * width), part(0)),
+                tokens,
+                pl.BlockSpec((per_k, 2, 1, k_rows, width), part(0)),
             ],
             scratch_shapes=[
                 pltpu.VMEM((heads, total_q, width), jnp.bfloat16),
@@ -238,7 +237,7 @@
         ),
         out_shape=[
             jax.ShapeDtypeStruct((groups, objects, q_rows, width), jnp.bfloat16),
-            jax.ShapeDtypeStruct((groups, objects, k_rows, 2 * width), jnp.bfloat16),
+            jax.ShapeDtypeStruct((groups, 2, objects, k_rows, width), jnp.bfloat16),
         ],
         cost_estimate=pl.CostEstimate(
             flops=10 * objects * total_q * groups * k_rows * width,
@@ -247,7 +246,7 @@
         ),
     )(live, q_array, k_array, v_array, outs, lse, grads)
 
-CHUNKS = ((0, 1, 2), (5, 6), (3, 4, 7), (8, 9, 10, 11), (12, 13, 14, 15))
+CHUNKS = ((5, 6), (0, 1, 2), (3, 4, 7), (8, 9, 10, 11), (12, 13, 14, 15))
 EARLY = 8
 MOD_ROWS = 16
 MESH = pl.DeviceIdType.MESH
@@ -283,6 +282,93 @@
     )
     copy.start()
     return copy
+
+
+def columns(index):
+    return pl.ds(pl.multiple_of(index * LANES, LANES), LANES)
+
+
+def fsdp_peers(fsdp_index):
+    return [{"fsdp": (fsdp_index + shift) % 8} for shift in range(1, 8)]
+
+
+def mix_begin(kind, sources, target, scratch, fsdp_index):
+    sems, holds = scratch[0], scratch[1:]
+
+    def ends(place, peer):
+        if kind == "heads":
+            return sources[0].at[:, :, :, columns(peer)], target.at[fsdp_index]
+        mine = columns(fsdp_index)
+        if len(sources[place].shape) == 4:
+            return sources[place].at[peer], target.at[place, :, :, mine]
+        return sources[place].at[peer], target.at[place : place + 2, :, :, mine]
+
+    copies, stays = [], []
+    for shift in (4, 5, 3, 6, 2, 7, 1):
+        peer = (fsdp_index + shift) % 8
+        for place in range(len(sources)):
+            theirs, there = ends(place, peer)
+            copies.append(
+                remote(theirs, there, sems.at[0, place, shift], sems.at[1, place, shift], {"fsdp": peer})
+            )
+    for place in range(len(sources)):
+        ours, here = ends(place, fsdp_index)
+        load = pltpu.make_async_copy(ours, holds[place], sems.at[0, place, 0])
+        load.start()
+        stays.append((load, pltpu.make_async_copy(holds[place], here, sems.at[1, place, 0])))
+    return copies, stays
+
+
+def mix_own(moving):
+    for load, store in moving[1]:
+        load.wait()
+        store.start()
+
+
+def mix_end(moving):
+    for load, store in moving[1]:
+        store.wait()
+    for copy in moving[0]:
+        copy.wait()
+
+
+def mix_plan(mix):
+    kind, sources = mix
+    bf = jnp.bfloat16
+    holds, blocks = [], 0
+    for array in sources:
+        if kind == "heads":
+            holds.append(array.shape[:3] + (array.shape[3] // 8,))
+            result = (8,) + holds[0]
+        else:
+            holds.append(array.shape[1:])
+            blocks += 1 if len(array.shape) == 4 else array.shape[1]
+            result = (blocks,) + array.shape[-3:-1] + (8 * array.shape[-1],)
+    scratch = [pltpu.SemaphoreType.DMA((2, len(sources), 8))] + [pltpu.VMEM(hold, bf) for hold in holds]
+    return scratch, jax.ShapeDtypeStruct(result, bf)
+
+
+def mix_body(kind, amount, *refs):
+    sources, target, scratch = refs[:amount], refs[amount], refs[amount + 1 :]
+    fsdp_index = lax.axis_index("fsdp")
+    greet(fsdp_peers(fsdp_index))
+    moving = mix_begin(kind, sources, target, scratch, fsdp_index)
+    mix_own(moving)
+    mix_end(moving)
+
+
+def mix_alone(mix, collective):
+    kind, sources = mix
+    scratch, result = mix_plan(mix)
+    return pl.pallas_call(
+        functools.partial(mix_body, kind, len(sources)),
+        in_specs=[ANY] * len(sources),
+        out_specs=ANY,
+        scratch_shapes=scratch,
+        out_shape=result,
+        compiler_params=comm_params(collective),
+        cost_estimate=pl.CostEstimate(flops=0, bytes_accessed=30_000_000, transcendentals=0),
+    )(*sources)
 
 
 def send_z(unit, full, fsdp_index, dp_index, z_index, sems):
@@ -439,7 +525,12 @@
     )(index, narrow, mod_rows)
 
 
-def next_gather_body(tiles, start, zoned, source_ref, out_ref, full, load_sems, send_sems, recv_sems, out_sems):
+def next_gather_body(tiles, start, zoned, kind, amount, source_ref, *refs):
+    mix_sources, refs = refs[:amount], refs[amount:]
+    out_ref, refs = refs[0], refs[1:]
+    if amount:
+        mixed_ref, refs = refs[0], refs[1:]
+    full, load_sems, send_sems, recv_sems, out_sems = refs[:5]
     where = places()
     dp_index, fsdp_index, z_index, core = where
     loads = []
@@ -450,10 +541,15 @@
             load = pltpu.make_async_copy(source_ref.at[start + tile], full.at[tile, z_index, dp_index], load_sems.at[tile])
         load.start()
         loads.append(load)
-    peers = [dp_peer(dp_index, flip) for flip in (1, 2)] + [core_peer(fsdp_index)]
-    if not zoned:
-        peers += [z_peer(fsdp_index, shift) for shift in (1, 2, 3)]
+    peers = [dp_peer(dp_index, flip) for flip in (1, 2)]
+    if amount:
+        peers += fsdp_peers(fsdp_index)
+    else:
+        peers += [core_peer(fsdp_index)]
+        peers += [] if zoned else [z_peer(fsdp_index, shift) for shift in (1, 2, 3)]
     greet(peers)
+    if amount:
+        moving = mix_begin(kind, mix_sources, mixed_ref, refs[5:], fsdp_index)
     z_copies = {}
     for tile in range(tiles):
         if zoned:
@@ -461,6 +557,8 @@
         else:
             loads[tile].wait()
             z_copies[tile] = send_z(tile, full.at[tile], fsdp_index, dp_index, z_index, (send_sems, recv_sems))
+    if amount:
+        mix_own(moving)
     fulls = [full.at[tile] for tile in range(tiles)]
     outs = [out_ref.at[tile] for tile in range(tiles)]
     spread(tiles, fulls, outs, z_copies, zoned, (send_sems, recv_sems, out_sems), where)
@@ -468,26 +566,35 @@
         for tile in range(tiles):
             for copy in z_copies[tile]:
                 copy.wait_send()
-
-
-def next_gather(source, tiles, start, zoned, collective):
+    if amount:
+        mix_end(moving)
+
+
+def next_gather(source, tiles, start, zoned, mix, collective):
     rows, width = source.shape[-2:]
     bf = jnp.bfloat16
-    return pl.pallas_call(
-        functools.partial(next_gather_body, tiles, start, zoned),
-        in_specs=[ANY],
-        out_specs=ANY,
-        scratch_shapes=[
-            pltpu.VMEM((tiles, 4, 4, rows, width), bf),
-            pltpu.SemaphoreType.DMA((tiles,)),
-            pltpu.SemaphoreType.DMA((tiles, 10)),
-            pltpu.SemaphoreType.DMA((tiles, 10)),
-            pltpu.SemaphoreType.DMA((tiles,)),
-        ],
-        out_shape=jax.ShapeDtypeStruct((tiles, 4, 2, 4, rows, width), bf),
+    kind, mix_sources = mix if mix else (None, [])
+    out_shape = [jax.ShapeDtypeStruct((tiles, 4, 2, 4, rows, width), bf)]
+    scratch = [
+        pltpu.VMEM((tiles, 4, 4, rows, width), bf),
+        pltpu.SemaphoreType.DMA((tiles,)),
+        pltpu.SemaphoreType.DMA((tiles, 10)),
+        pltpu.SemaphoreType.DMA((tiles, 10)),
+        pltpu.SemaphoreType.DMA((tiles,)),
+    ]
+    if mix:
+        extra, result = mix_plan(mix)
+        scratch, out_shape = scratch + extra, out_shape + [result]
+    results = pl.pallas_call(
+        functools.partial(next_gather_body, tiles, start, zoned, kind, len(mix_sources)),
+        in_specs=[ANY] * (1 + len(mix_sources)),
+        out_specs=[ANY] * len(out_shape),
+        scratch_shapes=scratch,
+        out_shape=out_shape,
         compiler_params=comm_params(collective),
         cost_estimate=pl.CostEstimate(flops=0, bytes_accessed=tiles * 30_000_000, transcendentals=0),
-    )(source).reshape(tiles, 32 * rows, width)
+    )(source, *mix_sources)
+    return results[0].reshape(tiles, 32 * rows, width), (results[1] if mix else None)
 
 
 def fast_layout(master):
@@ -633,29 +740,41 @@
     return copies
 
 
-def reduce_body(counts, extra, *refs):
+def reduce_body(counts, extra, kind, amount, *refs):
     groups = len(counts)
     tiles = sum(counts)
-    theirs, refs = refs[:groups], refs[groups:]
-    ours, refs = refs[:groups], refs[groups:]
+    grads, refs = refs[:groups], refs[groups:]
     if extra:
-        mod_theirs, mod_ours, out_ref, mod_out_ref = refs[:4]
-        refs = refs[4:]
+        mod_grads, refs = refs[0], refs[1:]
+    mix_sources, refs = refs[:amount], refs[amount:]
+    out_ref, refs = refs[0], refs[1:]
+    if extra:
+        mod_out_ref, refs = refs[0], refs[1:]
+    if amount:
+        mixed_ref, refs = refs[0], refs[1:]
+    scratch, refs = refs[:10], refs[10:]
+    if extra:
+        mod_scratch, refs = refs[:10], refs[10:]
+    where = places()
+    dp_index, fsdp_index, core = where[0], where[1], where[3]
+    peers = [dp_peer(dp_index, flip) for flip in (1, 2)]
+    if amount:
+        peers += fsdp_peers(fsdp_index)
     else:
-        out_ref, refs = refs[0], refs[1:]
-    scratch, mod_scratch = refs[:10], refs[10:]
-    where = places()
-    dp_index, fsdp_index = where[0], where[1]
-    peers = [z_peer(fsdp_index, shift) for shift in (1, 2, 3)]
-    peers += [dp_peer(dp_index, flip) for flip in (1, 2)] + [core_peer(fsdp_index)]
+        peers += [z_peer(fsdp_index, shift) for shift in (1, 2, 3)] + [core_peer(fsdp_index)]
     greet(peers)
+    if amount:
+        moving = mix_begin(kind, mix_sources, mixed_ref, refs, fsdp_index)
     entries = [
-        (theirs[group].at[tile], ours[group].at[tile])
+        (grads[group].at[tile, :, 1 - core], grads[group].at[tile, :, core])
         for group in range(groups)
         for tile in range(counts[group])
     ]
-    mod_copies = core_copies([(mod_theirs, mod_ours)], mod_scratch, where) if extra else []
+    mod_entry = [(mod_grads.at[0, :, 1 - core], mod_grads.at[0, :, core])] if extra else []
+    mod_copies = core_copies(mod_entry, mod_scratch, where) if extra else []
     copies = core_copies(entries, scratch, where)
+    if amount:
+        mix_own(moving)
     stages = reduce_stages(tiles, scratch, out_ref, where)
     if extra:
         mod_stages = reduce_stages(1, mod_scratch, mod_out_ref, where)
@@ -697,6 +816,9 @@
     else:
         lax.fori_loop(0, tiles + 3, step, 0)
 
+    store = pltpu.make_async_copy(scratch[6], out_ref, scratch[-3].at[1, 0])
+    store.start()
+
     def close(tile, carried):
         stages[4](tile)
         return carried
@@ -704,29 +826,34 @@
     lax.fori_loop(0, tiles, close, 0)
     for away, load in copies:
         away.wait_send()
-    store = pltpu.make_async_copy(scratch[6], out_ref, scratch[-3].at[1, 0])
-    store.start()
     if extra:
         mod_store = pltpu.make_async_copy(mod_scratch[6], mod_out_ref, mod_scratch[-3].at[1, 0])
         mod_store.start()
         mod_store.wait()
     store.wait()
-
-
-def reduce_tiles(theirs, ours, mods, collective):
-    counts = tuple(part.shape[0] for part in theirs)
+    if amount:
+        mix_end(moving)
+
+
+def reduce_tiles(grads, mods, mix, collective):
+    counts = tuple(part.shape[0] for part in grads)
     tiles = sum(counts)
-    rows, width = theirs[0].shape[-2:]
+    rows, width = grads[0].shape[-2:]
     bf = jnp.bfloat16
-    operands = list(theirs) + list(ours)
+    kind, mix_sources = mix if mix else (None, [])
+    operands = list(grads)
     out_shape = [jax.ShapeDtypeStruct((tiles, rows, width), bf)]
     scratch = reduce_scratch(tiles, rows, width)
     if mods is not None:
-        operands += list(mods)
+        operands.append(mods)
         out_shape.append(jax.ShapeDtypeStruct((1, MOD_ROWS, width), bf))
         scratch = scratch + reduce_scratch(1, MOD_ROWS, width)
+    if mix:
+        operands += list(mix_sources)
+        extra, result = mix_plan(mix)
+        scratch, out_shape = scratch + extra, out_shape + [result]
     return pl.pallas_call(
-        functools.partial(reduce_body, counts, mods is not None),
+        functools.partial(reduce_body, counts, mods is not None, kind, len(mix_sources)),
         in_specs=[ANY] * len(operands),
         out_specs=[ANY] * len(out_shape),
         scratch_shapes=scratch,
@@ -797,27 +924,19 @@
     )(index, *sums)
 
 
-def half_sums(form, left, right):
-    core = lax.axis_index("fsdp") % 2
-    parts = left.reshape(left.shape[:-1] + (4, 2, left.shape[-1] // 8))
-    shape = parts.shape[:-3] + (left.shape[-1] // 2,)
-    halves = []
-    for side in (1 - core, core):
-        half = lax.dynamic_index_in_dim(parts, side, parts.ndim - 2, keepdims=False).reshape(shape)
-        total = contract(form, half, right).astype(jnp.bfloat16)
-        halves.append(total.reshape(-1, 4, 4, total.shape[-2] // 16, total.shape[-1]))
-    return halves
-
-
-def mod_halves(grad_modulation):
+def tile_sums(form, left, right):
+    total = contract(form, left, right).astype(jnp.bfloat16)
+    return total.reshape(-1, 4, 2, 4, total.shape[-2] // 32, total.shape[-1])
+
+
+def mod_sums(grad_modulation):
     rows, width = grad_modulation.shape
-    columns = width // 32
-    core = lax.axis_index("fsdp") % 2
-    blocks = grad_modulation.reshape(rows, 4, 4, 2, columns).transpose(3, 2, 1, 0, 4)
-    flat = blocks.astype(jnp.bfloat16).reshape(2, 4, 4, rows * columns)
-    flat = jnp.pad(flat, ((0, 0), (0, 0), (0, 0), (0, MOD_ROWS * 1024 - rows * columns)))
-    flat = flat.reshape(2, 4, 4, MOD_ROWS, 1024)
-    return [lax.dynamic_index_in_dim(flat, side, 0, keepdims=False) for side in (1 - core, core)]
+    columns_here = width // 32
+    blocks = grad_modulation.reshape(rows, 4, 4, 2, columns_here).transpose(2, 3, 1, 0, 4)
+    flat = blocks.astype(jnp.bfloat16).reshape(1, 4, 2, 4, rows * columns_here)
+    flat = jnp.pad(flat, ((0, 0),) * 4 + ((0, MOD_ROWS * 1024 - rows * columns_here),))
+    return flat.reshape(1, 4, 2, 4, MOD_ROWS, 1024)
+
 
 def after(value, *others):
     return lax.optimization_barrier((value,) + others)[0]
@@ -826,7 +945,7 @@
 def weight_source(master, modulation, tile_slots):
     if not fast_layout(master):
         chunks, mod_all = fetch_generic(master, modulation, tile_slots)
-        return (lambda number, *others: chunks[number]), mod_all
+        return (lambda number, mix, *others: (chunks[number], mix_generic(mix))), mod_all
     slots_here, row_count, width = master.shape
     dp_index = lax.axis_index("dp")
     narrow = master.astype(jnp.bfloat16).reshape(slots_here, 4, row_count // 4, width)
@@ -839,13 +958,15 @@
     flat = mods.reshape(8, 4, MOD_ROWS * width)[:, :, : mod_rows * mod_columns]
     mod_all = flat.reshape(8, 4, mod_rows, mod_columns).transpose(2, 1, 0, 3).reshape(mod_rows, -1)
 
-    def chunk(number, *others):
+    def chunk(number, mix, *others):
         tiles = len(CHUNKS[number])
         if number == 0:
-            return first.reshape(tiles, row_count * 8, width)
+            return first.reshape(tiles, row_count * 8, width), None
         if number < 3:
-            return next_gather(after(zoned, *others), tiles, (0, 2)[number - 1], True, number)
-        return next_gather(after(rest, *others), tiles, (0, 4)[number - 3], False, number)
+            held = after(zoned, *others) if others else zoned
+            return next_gather(held, tiles, (0, 3)[number - 1], True, mix, number)
+        held = after(rest, *others) if others else rest
+        return next_gather(held, tiles, (0, 4)[number - 3], False, mix, number)
 
     return chunk, mod_all
 
@@ -855,23 +976,24 @@
 
 
 def by_head(values, groups):
-    objects, rows, blocks, width = values.shape
-    share = width // groups
-    moved = values.reshape(objects, rows, blocks, groups, share).transpose(3, 0, 1, 2, 4)
-    return moved.reshape(groups, objects, rows, blocks * share)
-
-
-def from_head(pieces, blocks):
-    groups, objects, rows, share = pieces.shape
-    share = share // blocks
-    moved = pieces.reshape(groups, objects, rows, blocks, share).transpose(1, 2, 3, 0, 4)
-    return moved.reshape(objects, rows, blocks, groups * share)
-
-
-def source(array, index, width):
-    if width % LANES == 0:
-        return (array, (index, width))
-    return (array[..., index * width : (index + 1) * width], (0, width))
+    blocks, objects, rows, width = values.shape
+    moved = values.reshape(blocks, objects, rows, groups, width // groups)
+    return moved.transpose(3, 0, 1, 2, 4)
+
+
+def from_head(pieces):
+    groups, blocks, objects, rows, share = pieces.shape
+    return pieces.transpose(1, 2, 3, 0, 4).reshape(blocks, objects, rows, groups * share)
+
+
+def mix_generic(mix):
+    if mix is None:
+        return None
+    kind, sources = mix
+    if kind == "heads":
+        return exchange(by_head(sources[0], lax.axis_size("fsdp")))
+    parts = [array if array.ndim == 5 else array[:, None] for array in sources]
+    return from_head(exchange(jnp.concatenate(parts, axis=1)))
 
 
 def adamw(weights, grads, first, second, rate):
@@ -902,9 +1024,15 @@
     objects, tri_local, model_width = triplane.shape
     groups = lax.axis_size("fsdp")
     tri_total = tri_local * groups
-    head_width = model_width // groups
     fast = fast_layout(master)
-    partial_sums = half_sums if fast else contract
+    partial_sums = tile_sums if fast else contract
+
+    def reduced(grads, mods, mix, collective, *others):
+        if not fast:
+            return None, mix_generic(mix)
+        grads = list(after(tuple(grads), *others)) if others else grads
+        return reduce_tiles(grads, mods, mix, collective)
+
     chunk, mod_all = weight_source(master, modulation, tile_slots)
     mod_full = mod_all.astype(jnp.float32)
     modulations = (
@@ -915,40 +1043,30 @@
         modulations[:, position * model_width : (position + 1) * model_width][:, None, :]
         for position in range(9)
     ]
-    tiles_qkv = chunk(0)
+    tiles_pair, unused_mix = chunk(0, None)
+    image_pairs = contract("oid,kde->koie", image_tokens, tiles_pair).astype(jnp.bfloat16)
+    pair_sent = by_head(image_pairs, groups)
+    pair_heads = exchange(pair_sent)
+    tiles_qkv, unused_mix = chunk(1, None, pair_sent)
     residual_in = triplane.astype(jnp.float32)
     normed_one = modulate(residual_in, blocks[0], blocks[1]).astype(jnp.bfloat16)
-    triples = contract("otd,kde->otke", normed_one, tiles_qkv).astype(jnp.bfloat16)
-    triple_sent = by_head(triples, groups)
-    triple_heads = exchange(triple_sent)
-    tiles_pair = chunk(1, triple_sent)
-    triple_heads = after(triple_heads, tiles_pair)
-    image_pairs = contract("oid,kde->oike", image_tokens, tiles_pair).astype(jnp.bfloat16)
-    pair_sent = by_head(image_pairs, groups)
-    pair_heads = exchange(pair_sent)
-    triple_heads = after(triple_heads, pair_sent)
+    triples = contract("otd,kde->kote", normed_one, tiles_qkv).astype(jnp.bfloat16)
+    tiles_mixed, triple_heads = chunk(2, ("heads", [triples]))
+    tile_out_one, tile_query_two, tile_out_two = tiles_mixed[0], tiles_mixed[1], tiles_mixed[2]
     every_key = jnp.full((objects,), tri_total, jnp.int32)
-    self_sources = [source(triple_heads, index, head_width) for index in range(3)]
+    self_sources = [(triple_heads, index) for index in range(3)]
     self_result, self_logsum = attend_forward(every_key, *self_sources, tri_total, VIEW)
-    tiles_mixed = chunk(2, self_result, pair_sent)
-    tile_out_one, tile_query_two, tile_out_two = tiles_mixed[0], tiles_mixed[1], tiles_mixed[2]
-    merged_one = from_head(after(exchange(self_result), tiles_mixed), 1)[:, :, 0]
+    tiles_up, merged_one = chunk(3, ("tokens", [self_result]))
+    merged_one = merged_one[0]
     branch_one = contract("otd,de->ote", merged_one, tile_out_one)
     residual_mid = residual_in + blocks[2] * branch_one
     normed_two = modulate(residual_mid, blocks[3], blocks[4]).astype(jnp.bfloat16)
     cross_query = contract("otd,de->ote", normed_two, tile_query_two).astype(jnp.bfloat16)
-    query_sent = by_head(cross_query[:, :, None], groups)
-    query_heads = exchange(query_sent)
-    tiles_up = chunk(3, query_sent)
-    query_heads = after(query_heads, tiles_up)
-    cross_sources = [
-        source(query_heads, 0, head_width),
-        source(pair_heads, 0, head_width),
-        source(pair_heads, 1, head_width),
-    ]
+    tiles_down, query_heads = chunk(4, ("heads", [cross_query[None]]))
+    cross_sources = [(query_heads, 0), (pair_heads, 0), (pair_heads, 1)]
     cross_result, cross_logsum = attend_forward(view_tokens, *cross_sources, tri_total, VIEW)
-    tiles_down = chunk(4, cross_result)
-    merged_two = from_head(after(exchange(cross_result), tiles_down), 1)[:, :, 0]
+    cross_mix = ("tokens", [cross_result])
+    merged_two = (mix_alone(cross_mix, 11) if fast else mix_generic(cross_mix))[0]
     branch_two = contract("otd,de->ote", merged_two, tile_out_two)
     residual_late = residual_mid + blocks[5] * branch_two
     normed_three = modulate(residual_late, blocks[6], blocks[7]).astype(jnp.bfloat16)
@@ -970,25 +1088,16 @@
     grad_gate_two = jnp.sum(grad_late * branch_two, axis=1)
     grad_branch_two = (blocks[5] * grad_late).astype(jnp.bfloat16)
     grad_merged_two = contract("ote,de->otd", grad_branch_two, tile_out_two).astype(jnp.bfloat16)
-    grad_cross_sent = by_head(grad_merged_two[:, :, None], groups)
-    grad_cross_heads = exchange(grad_cross_sent)
     grad_down = partial_sums("otkd,ote->kde", hidden, grad_branch_three)
     grad_up = partial_sums("otd,otke->kde", normed_three, grad_pre)
     grad_out_two = partial_sums("otd,ote->de", merged_two, grad_branch_two)
-    if fast:
-        theirs, ours = after(tuple(grad_down), grad_cross_sent)
-        (sums_down,) = reduce_tiles([theirs], [ours], None, 5)
-        grad_cross_heads = after(grad_cross_heads, sums_down)
+    sums_down, grad_cross_heads = reduced([grad_down], None, ("heads", [grad_merged_two[None]]), 5)
     grad_query_heads, grad_pair_heads = attend_backward(
         view_tokens, *cross_sources, cross_result, cross_logsum, grad_cross_heads, VIEW
     )
-    grad_query_back = exchange(grad_query_heads)
     grad_pair_back = exchange(grad_pair_heads)
-    if fast:
-        theirs, ours = after(tuple(grad_up), grad_pair_heads, sums_down)
-        (sums_up,) = reduce_tiles([theirs], [ours], None, 6)
-        grad_query_back = after(grad_query_back, sums_up)
-    grad_query_two = from_head(grad_query_back, 1)[:, :, 0]
+    sums_up, grad_query_two = reduced([grad_up], None, ("tokens", [grad_query_heads]), 6, grad_pair_heads)
+    grad_query_two = grad_query_two[0]
     grad_tile_query = partial_sums("otd,ote->de", normed_two, grad_query_two)
     grad_normed_two = contract("ote,de->otd", grad_query_two, tile_query_two)
     grad_mid_norm, grad_shift_two, grad_scale_two = modulate_back(
@@ -998,30 +1107,21 @@
     grad_gate_one = jnp.sum(grad_mid * branch_one, axis=1)
     grad_branch_one = (blocks[2] * grad_mid).astype(jnp.bfloat16)
     grad_merged_one = contract("ote,de->otd", grad_branch_one, tile_out_one).astype(jnp.bfloat16)
-    grad_self_sent = by_head(grad_merged_one[:, :, None], groups)
-    grad_self_heads = exchange(grad_self_sent)
     grad_out_one = partial_sums("otd,ote->de", merged_one, grad_branch_one)
-    if fast:
-        halves = after(tuple(grad_out_two) + tuple(grad_tile_query), grad_self_sent, sums_up)
-        (sums_mid,) = reduce_tiles([halves[0], halves[2]], [halves[1], halves[3]], None, 7)
-        grad_self_heads = after(grad_self_heads, sums_mid)
+    sums_mid, grad_self_heads = reduced(
+        [grad_out_two, grad_tile_query], None, ("heads", [grad_merged_one[None]]), 7
+    )
     grad_self_query, grad_self_pair = attend_backward(
         every_key, *self_sources, self_result, self_logsum, grad_self_heads, VIEW
     )
-    grad_triple_heads = jnp.concatenate([grad_self_query, grad_self_pair], axis=-1)
-    grad_triple_back = exchange(grad_triple_heads)
-    if fast:
-        grad_pair_back = after(grad_pair_back, grad_triple_heads)
-    grad_pairs = from_head(grad_pair_back, 2)
-    grad_tiles_pair = partial_sums("oid,oike->kde", image_tokens, grad_pairs)
-    grad_image = contract("oike,kde->oid", grad_pairs, tiles_pair)
-    if fast:
-        halves = after(tuple(grad_tiles_pair) + tuple(grad_out_one), grad_triple_heads, sums_mid)
-        (sums_late,) = reduce_tiles([halves[0], halves[2]], [halves[1], halves[3]], None, 8)
-        grad_triple_back = after(grad_triple_back, sums_late)
-    grad_triples = from_head(grad_triple_back, 3)
-    grad_qkv = partial_sums("otd,otke->kde", normed_one, grad_triples)
-    grad_normed_one = contract("otke,kde->otd", grad_triples, tiles_qkv)
+    grad_pairs = from_head(after(grad_pair_back, grad_self_query))
+    grad_tiles_pair = partial_sums("oid,koie->kde", image_tokens, grad_pairs)
+    grad_image = contract("koie,kde->oid", grad_pairs, tiles_pair)
+    sums_late, grad_triples = reduced(
+        [grad_tiles_pair, grad_out_one], None, ("tokens", [grad_self_query, grad_self_pair]), 8
+    )
+    grad_qkv = partial_sums("otd,kote->kde", normed_one, grad_triples)
+    grad_normed_one = contract("kote,kde->otd", grad_triples, tiles_qkv)
     grad_in_norm, grad_shift_one, grad_scale_one = modulate_back(
         residual_in, blocks[0], blocks[1], grad_normed_one
     )
@@ -1047,8 +1147,7 @@
         [grad_mod_rows, jnp.sum(grad_mods, axis=0, keepdims=True)], axis=0
     )
     if fast:
-        theirs, ours = after(tuple(grad_qkv), sums_late)
-        sums_qkv, mod_sum = reduce_tiles([theirs], [ours], mod_halves(grad_modulation), 9)
+        sums_qkv, mod_sum = reduce_tiles([grad_qkv], mod_sums(grad_modulation), None, 9)
         sums = [sums_qkv, sums_late, sums_mid, sums_up, sums_down]
         order = (0, 1, 2, 5, 6, 3, 7, 4, 8, 9, 10, 11, 12, 13, 14, 15)
         tile_grad = to_owners(sums, order, tile_slots, 10).reshape(master.shape)

time: 1110 us -> 934 us (0.84)
  local copies, waits for them, and re-layouts: 141 us -> 35.2 us
  waiting for transfers between devices: 94 us -> 0.01 us
  Pallas kernels: 668 us -> 756 us
  blocking collectives: 38.5 us -> 0 us
  starting transfers between devices: 52.1 us -> 14.3 us
    pallas_call x9 -> x10, Pallas kernels: 464 us -> 598 us  [the longest x5 335 us: reduce_tiles(): pl.pallas_call(functools.partial(reduce_body, counts, mods is not None, k...]
    all_to_all x8 -> x2, waiting for transfers between devices: 94 us -> 0.01 us  [exchange(): lax.all_to_all(pieces, 'fsdp', split_axis=0, concat_axis=0, tiled=True)]
    reshape x13 -> x3, local copies, waits for them, and re-layouts: 49.4 us -> 9.49 us  [the longest x1 6.47 us: by_head(): moved = values.reshape(blocks, objects, rows, groups, width // groups)]
    all_to_all x2 -> x0, blocking collectives: 38.5 us -> none  [exchange(): lax.all_to_all(pieces, 'fsdp', split_axis=0, concat_axis=0, tiled=True)]
    all_to_all x8 -> x2, starting transfers between devices: 52.1 us -> 14.3 us  [exchange(): lax.all_to_all(pieces, 'fsdp', split_axis=0, concat_axis=0, tiled=True)]
    dynamic_slice x19 -> x0, local copies, waits for them, and re-layouts: 36.4 us -> none  [half_sums(): lax.dynamic_index_in_dim(parts, side, parts.ndim - 2, keepdims=False)]
    pallas_call x2, Pallas kernels: 66.5 us -> 46.6 us  [attend_backward(): pl.pallas_call(cross_backward_body, grid_spec=pltpu.PrefetchScalarGridSpe...]
    unnamed x126 -> x88, local copies, waits for them, and re-layouts: 21.8 us -> 4.26 us
  transfers between devices with their start and end apart: 8 -> 2, of which waited for: 1 -> 0; matrix products, arithmetic and copies ran while one was open for 13% -> 5% of each run, Pallas kernels for 39% -> 48%
where the time goes in v3:
time: 934 us; the launch traced here: 930 us
  Pallas kernels  756 us (81%)
  matrix products  101 us (11%)
  local copies, waits for them, and re-layouts  35.2 us (4%)
  other arithmetic  21.5 us (2%)
  starting transfers between devices  14.3 us (2%)
    pallas_call x5, Pallas kernels, reduce_tiles(): pl.pallas_call(functools.partial(reduce_body, counts, mods is not None, k...  335 us
    pallas_call x4, Pallas kernels, next_gather(): pl.pallas_call(functools.partial(next_gather_body, tiles, start, zoned, k...  247 us
    dot_general x21, matrix products, contract(): return jnp.einsum(form, left, right, preferred_element_type=jnp.float32)  100 us
    pallas_call x1, Pallas kernels, first_gather(): pl.pallas_call(functools.partial(first_gather_body, tiles, rows), grid_sp...  62.3 us
    pallas_call x2, Pallas kernels, attend_backward(): pl.pallas_call(cross_backward_body, grid_spec=pltpu.PrefetchScalarGridSpe...  46.6 us
    pallas_call x2, Pallas kernels, attend_forward(): pl.pallas_call(functools.partial(forward_body, step_rows), grid_spec=pltp...  34.1 us
  transfers between devices with their start and end apart: 2, of which 0 were waited for; matrix products, arithmetic and copies ran while one was open for 5% of the time, Pallas kernels for 48%

profile of v3, /device:TPU:0, one launch (start us, length us, event | category | flops | bytes accessed | tf_op | source)
XLA Modules:
  0.0 930.1 jit_solution(2691534070482250698)
XLA Ops:
  0.7 2.9 convert_element_type.115
  3.5 0.8 convert_element_type.116
  5.1 1.3 pad_clamp_fusion
  6.3 1.2 fusion.52
  7.5 1.2 gather_fusion
  8.7 62.3 %shard_map.213 = (bf16[2,4,2,4,32,1024]{5,4,3,2,1,0:T(8,128)(2,1)}, bf16[4,2,4,16,1024]{4,3,2,1,0:T(8,128)(2,1)}, bf16[4,6,32,1024]{3,2,1,0:T(8,128)(2,1)}, bf16[8,32,1024]{2,1,0:T(8,128)(2,1)}) custom-call(s32[16]{0:T(128)} %gather_fusion, bf16[4,4,32,1024]{3,2,1,0:T(8,128)(2,1)} %bitcast.194, bf16[16,1024]{1,0:T(8,128)(2,1)} %reshape.217.mod_ref), custom_call_target="tpu_custom_call" | custom-call | bytes 200000000 | tf_op jit(solution)/shard_map/pallas_call | solution.py:496
  71.0 8.4 convolution_convert_fusion.1
  79.4 6.5 copy.78
  85.9 9.5 %all-to-all-start = ((bf16[8,2,2,512,128]{4,3,2,1,0:T(8,128)(2,1)}), bf16[8,2,2,512,128]{4,3,2,1,0:T(8,128)(2,1)}, u32[]{:S(2)}, u32[]{:S(2)}) async-start(bf16[8,2,2,512,128]{4,3,2,1,0:T(8,128)(2,1)} %bitcast.183), calls=%async_computation | async-start | bytes 8388608 | tf_op jit(solution)/shard_map/all_to_all | solution.py:975
  95.4 1.9 reshape.218
  97.4 0.6 reshape.219
  98.9 32.5 %shard_map.214 = bf16[3,4,2,4,32,1024]{5,4,3,2,1,0:T(8,128)(2,1)} custom-call(bf16[4,6,32,1024]{3,2,1,0:T(8,128)(2,1)} %get-tuple-element.45.source_ref), custom_call_target="tpu_custom_call" | custom-call | bytes 90000000 | tf_op jit(solution)/shard_map/pallas_call | solution.py:588
  132.2 6.0 fusion.16.refs_0_
  138.2 80.9 %shard_map.215 = (bf16[3,4,2,4,32,1024]{5,4,3,2,1,0:T(8,128)(2,1)}, bf16[8,3,2,128,128]{4,3,2,1,0:T(8,128)(2,1)}) custom-call(bf16[4,6,32,1024]{3,2,1,0:T(8,128)(2,1)} %get-tuple-element.45.source_ref, bf16[3,2,128,1024]{3,2,1,0:T(8,128)(2,1)} %fusion.16.refs_0_), custom_call_target="tpu_custom_call" | custom-call | bytes 90000000 | tf_op jit(solution)/shard_map/pallas_call | solution.py:588
  219.7 13.1 %shard_map.216 = (bf16[8,2,128,128]{3,2,1,0:T(8,128)(2,1)}, f32[2,2,1,1024]{3,2,1,0:T(1,128)}) custom-call(s32[2]{0:T(128)} %broadcast_31_live_ref.2.live_ref, bf16[8,3,2,128,128]{4,3,2,1,0:T(8,128)(2,1)} %get-tuple-element.46.q_ref.k_ref.v_ref, bf16[8,3,2,128,128]{4,3,2,1,0:T(8,128)(2,1)} %get-tuple-element.46.q_ref.k_ref.v_ref, ...), custom_call_target="tpu_custom_call" | custom-call | flops 1073741824 | bytes 2097152 | tf_op jit(solution)/shard_map/pallas_call | solution.py:114
  232.8 68.0 %shard_map.217 = (bf16[4,4,2,4,32,1024]{5,4,3,2,1,0:T(8,128)(2,1)}, bf16[1,2,128,1024]{3,2,1,0:T(8,128)(2,1)}) custom-call(bf16[8,32,1024]{2,1,0:T(8,128)(2,1)} %get-tuple-element.42.source_ref, bf16[8,2,128,128]{3,2,1,0:T(8,128)(2,1)} %get-tuple-element.47.refs_0_.out_ref), custom_call_target="tpu_custom_call" | custom-call | bytes 120000000 | tf_op jit(solution)/shard_map/pallas_call | solution.py:588
  300.9 5.6 fusion.65
  306.5 2.2 fusion.64
  308.9 1.6 fusion.17.refs_0_
  310.5 65.5 %shard_map.218 = (bf16[4,4,2,4,32,1024]{5,4,3,2,1,0:T(8,128)(2,1)}, bf16[8,1,2,128,128]{4,3,2,1,0:T(8,128)(2,1)}) custom-call(bf16[8,32,1024]{2,1,0:T(8,128)(2,1)} %get-tuple-element.42.source_ref, bf16[1,2,128,1024]{3,2,1,0:T(8,128)(2,1)} %fusion.17.refs_0_), custom_call_target="tpu_custom_call" | custom-call | bytes 120000000 | tf_op jit(solution)/shard_map/pallas_call | solution.py:588
  376.0 21.0 %shard_map.219 = (bf16[8,2,128,128]{3,2,1,0:T(8,128)(2,1)}, f32[2,2,1,1024]{3,2,1,0:T(1,128)}) custom-call(s32[2]{0:T(128)} %live_ref.3, bf16[8,1,2,128,128]{4,3,2,1,0:T(8,128)(2,1)} %get-tuple-element.50.q_ref, bf16[8,2,2,512,128]{4,3,2,1,0:T(8,128)(2,1)} %all-to-all-done.k_ref.v_ref, bf16[8,2,2,512,128]{4,3,2,1,0:T(8,128)(2,1)} %all-to-all-done.k_ref.v_ref), custom_call_target="tpu_custom_call" | custom-call | flops 4294967296 | bytes 5242880 | tf_op jit(solution)/shard_map/pallas_call | solution.py:114
  397.0 15.8 %shard_map.220 = bf16[1,2,128,1024]{3,2,1,0:T(8,128)(2,1)} custom-call(bf16[8,2,128,128]{3,2,1,0:T(8,128)(2,1)} %get-tuple-element.51.refs_0_.out_ref), custom_call_target="tpu_custom_call" | custom-call | bytes 30000000 | tf_op jit(solution)/shard_map/pallas_call | solution.py:363
  412.8 3.5 fusion.63
  416.5 6.5 fusion.57
  423.0 5.8 bitcast_convert_fusion
  428.9 6.3 fusion.8
  435.2 1.3 copy-done.16
  436.5 6.3 multiply_reduce_fusion
  443.5 1.3 copy-done.14
  444.8 1.5 fusion.18.refs_1_
  446.3 64.3 %shard_map.221 = (bf16[4,32,1024]{2,1,0:T(8,128)(2,1)}, bf16[8,1,2,128,128]{4,3,2,1,0:T(8,128)(2,1)}) custom-call(bf16[4,4,2,4,32,1024]{5,4,3,2,1,0:T(8,128)(2,1)} %bitcast.184, bf16[1,2,128,1024]{3,2,1,0:T(8,128)(2,1)} %fusion.18.refs_1_), custom_call_target="tpu_custom_call" | custom-call | bytes 160000000 | tf_op jit(solution)/shard_map/pallas_call | solution.py:855
  510.6 30.6 %shard_map.222 = (bf16[8,2,128,128]{3,2,1,0:T(8,128)(2,1)}, bf16[8,2,2,512,128]{4,3,2,1,0:T(8,128)(2,1)}) custom-call(s32[2]{0:T(128)} %live_ref.3, bf16[8,1,2,128,128]{4,3,2,1,0:T(8,128)(2,1)} %get-tuple-element.50.q_ref, bf16[8,2,2,512,128]{4,3,2,1,0:T(8,128)(2,1)} %all-to-all-done.k_ref.v_ref, bf16[8,2,2,512,128]{4,3,2,1,0:T(8,128)(2,1)} %all-to-all-done.k_ref.v_ref, ...), custom_call_target="tpu_custom_call" | custom-call | flops 10737418240 | bytes 10485760 | tf_op jit(solution)/shard_map/pallas_call | solution.py:214
  541.3 4.8 all-to-all-start.1
  546.1 0.8 gather_fusion.1
  546.8 0.7 select_reduce_fusion.index_ref
  547.5 7.9 bitcast_convert_fusion.1
  555.4 129.9 %shard_map.223 = (bf16[4,32,1024]{2,1,0:T(8,128)(2,1)}, bf16[1,2,128,1024]{3,2,1,0:T(8,128)(2,1)}) custom-call(bf16[4,4,2,4,32,1024]{5,4,3,2,1,0:T(8,128)(2,1)} %bitcast.179, bf16[8,2,128,128]{3,2,1,0:T(8,128)(2,1)} %get-tuple-element.58.refs_1_), custom_call_target="tpu_custom_call" | custom-call | bytes 160000000 | tf_op jit(solution)/shard_map/pallas_call | solution.py:855
  685.3 2.1 multiply_reduce_fusion.4
  688.1 8.9 fusion.28
  697.0 1.5 fusion.19.refs_2_
  698.6 2.1 bitcast_convert_fusion.6
  700.7 2.2 bitcast_convert_fusion.5
  702.9 38.5 %shard_map.224 = (bf16[2,32,1024]{2,1,0:T(8,128)(2,1)}, bf16[8,1,2,128,128]{4,3,2,1,0:T(8,128)(2,1)}) custom-call(bf16[1,4,2,4,32,1024]{5,4,3,2,1,0:T(8,128)(2,1)} %bitcast.186, bf16[1,4,2,4,32,1024]{5,4,3,2,1,0:T(8,128)(2,1)} %bitcast.187, bf16[1,2,128,1024]{3,2,1,0:T(8,128)(2,1)} %fusion.19.refs_2_), custom_call_target="tpu_custom_call" | custom-call | bytes 80000000 | tf_op jit(solution)/shard_map/pallas_call | solution.py:855
  741.4 15.9 %shard_map.225 = (bf16[8,2,128,128]{3,2,1,0:T(8,128)(2,1)}, bf16[8,2,2,128,128]{4,3,2,1,0:T(8,128)(2,1)}) custom-call(s32[2]{0:T(128)} %broadcast_31_live_ref.2.live_ref, bf16[8,3,2,128,128]{4,3,2,1,0:T(8,128)(2,1)} %get-tuple-element.46.q_ref.k_ref.v_ref, bf16[8,3,2,128,128]{4,3,2,1,0:T(8,128)(2,1)} %get-tuple-element.46.q_ref.k_ref.v_ref, ...), custom_call_target="tpu_custom_call" | custom-call | flops 2684354560 | bytes 4194304 | tf_op jit(solution)/shard_map/pallas_call | solution.py:214
  757.3 3.1 bitcast_convert_fusion.4
  760.4 6.2 copy.85
  766.6 8.3 bitcast_convert_fusion.3
  774.9 55.8 %shard_map.226 = (bf16[3,32,1024]{2,1,0:T(8,128)(2,1)}, bf16[3,2,128,1024]{3,2,1,0:T(8,128)(2,1)}) custom-call(bf16[2,4,2,4,32,1024]{5,4,3,2,1,0:T(8,128)(2,1)} %bitcast.198, bf16[1,4,2,4,32,1024]{5,4,3,2,1,0:T(8,128)(2,1)} %bitcast.185, bf16[8,2,128,128]{3,2,1,0:T(8,128)(2,1)} %get-tuple-element.62.refs_2_, ...), custom_call_target="tpu_custom_call" | custom-call | bytes 120000000 | tf_op jit(solution)/shard_map/pallas_call | solution.py:855
  830.7 5.3 fusion.26
  836.1 5.1 bitcast_convert_fusion.2
  841.8 6.1 convolution_bitcast_fusion
  847.8 0.6 fusion.24
  848.6 0.7 fusion
  849.3 0.7 concatenate.13
  850.0 0.9 copy.91
  851.1 1.1 maximum_bitcast_fusion
  852.6 1.3 pad.9
  854.0 2.6 reshape.234.refs_1_
  856.5 46.5 %shard_map.227 = (bf16[3,32,1024]{2,1,0:T(8,128)(2,1)}, bf16[1,16,1024]{2,1,0:T(8,128)(2,1)}) custom-call(bf16[3,4,2,4,32,1024]{5,4,3,2,1,0:T(8,128)(2,1)} %bitcast.180, bf16[1,4,2,4,16,1024]{5,4,3,2,1,0:T(8,128)(2,1)} %reshape.234.refs_1_), custom_call_target="tpu_custom_call" | custom-call | bytes 120000000 | tf_op jit(solution)/shard_map/pallas_call | solution.py:855
  903.1 0.8 copy.122
  903.9 3.1 add_add_fusion.3
  907.0 15.5 %shard_map.228 = bf16[4,4,32,1024]{3,2,1,0:T(8,128)(2,1)} custom-call(s32[16]{0:T(128)} %select_reduce_fusion.index_ref, bf16[3,32,1024]{2,1,0:T(8,128)(2,1)} %get-tuple-element.66.refs_0_, bf16[3,32,1024]{2,1,0:T(8,128)(2,1)} %get-tuple-element.67.refs_1_, bf16[2,32,1024]{2,1,0:T(8,128)(2,1)} %get-tuple-element.68.refs_2_, ...), custom_call_target="tpu_custom_call" | custom-call | bytes 50000000 | tf_op jit(solution)/shard_map/pallas_call | solution.py:906
  922.5 6.7 fusion.60
  929.3 0.7 multiply_subtract_fusion.1
  (126 shorter events, 6.5 us)
Async XLA Ops:
  0.6 70.4 %copy-start = (bf16[2,512,1024]{2,1,0:T(8,128)(2,1)S(1)}, bf16[2,512,1024]{2,1,0:T(8,128)(2,1)}, u32[]{:S(2)}) copy-start(bf16[2,512,1024]{2,1,0:T(8,128)(2,1)} %param.15) | copy-start | bytes 6291460
  85.9 290.1 %all-to-all-start = ((bf16[8,2,2,512,128]{4,3,2,1,0:T(8,128)(2,1)}), bf16[8,2,2,512,128]{4,3,2,1,0:T(8,128)(2,1)}, u32[]{:S(2)}, u32[]{:S(2)}) async-start(bf16[8,2,2,512,128]{4,3,2,1,0:T(8,128)(2,1)} %bitcast.183), calls=%async_computation | async-start | bytes 8388608 | tf_op jit(solution)/shard_map/all_to_all | solution.py:975
  98.7 32.8 %copy-start.2 = (bf16[2,128,1024]{2,1,0:T(8,128)(2,1)S(1)}, bf16[2,128,1024]{2,1,0:T(8,128)(2,1)}, u32[]{:S(2)}) copy-start(bf16[2,128,1024]{2,1,0:T(8,128)(2,1)} %param.14) | copy-start | bytes 1572868
  98.9 33.0 %copy-start.33 = (f32[2,16]{1,0:T(2,128)S(1)}, f32[2,16]{1,0:T(2,128)}, u32[]{:S(2)}) copy-start(f32[2,16]{1,0:T(2,128)} %param.16) | copy-start | bytes 388
  300.8 5.6 copy-start.3
  300.8 5.6 copy-start.21
  306.4 2.2 copy-start.5
  306.4 2.5 copy-start.12
  416.2 26.6 %copy-start.7 = (f32[2,128,1024]{2,1,0:T(8,128)}, f32[2,128,1024]{2,1,0:T(8,128)S(1)}, u32[]{:S(2)}) copy-start(f32[2,128,1024]{2,1,0:T(8,128)S(1)} %get-tuple-element.95) | copy-start | bytes 3145732
  416.3 12.6 %slice-start = ((s8[8388608]{0:T(1024)(128)(4,1)}), s8[4194304]{0:T(1024)(128)(4,1)S(1)}, s32[]{:S(2)}) async-start(s8[8388608]{0:T(1024)(128)(4,1)} %bitcast.204), calls=%async_computation.2 | async-start | bytes 8388608
  416.5 6.5 copy-start.28
  416.5 12.3 %slice-start.1 = ((s8[8388608]{0:T(1024)(128)(4,1)}), s8[4194304]{0:T(1024)(128)(4,1)S(1)}, s32[]{:S(2)}) async-start(s8[8388608]{0:T(1024)(128)(4,1)} %bitcast.204), calls=%async_computation.3 | async-start | bytes 8388608
  423.0 5.8 copy-start.36
  435.2 1.3 copy-start.16
  442.8 2.0 copy-start.14
  443.3 3.1 copy-start.18
  444.8 1.5 copy-start.23
  541.3 4.8 copy-start.1
  541.3 5.6 copy-start.34
  541.3 219.1 %all-to-all-start.1 = ((bf16[8,2,2,512,128]{4,3,2,1,0:T(8,128)(2,1)}), bf16[8,2,2,512,128]{4,3,2,1,0:T(8,128)(2,1)}, u32[]{:S(2)}, u32[]{:S(2)}) async-start(bf16[8,2,2,512,128]{4,3,2,1,0:T(8,128)(2,1)} %get-tuple-element.56), calls=%async_computation.1 | async-start | bytes 8388608 | tf_op jit(solution)/shard_map/all_to_all | solution.py:975
  555.4 129.9 %copy-start.13 = (bf16[1,4,2,4,32,1024]{5,4,3,2,1,0:T(8,128)(2,1)S(1)}, bf16[1,4,2,4,32,1024]{5,4,3,2,1,0:T(8,128)(2,1)}, u32[]{:S(2)}) copy-start(bf16[1,4,2,4,32,1024]{5,4,3,2,1,0:T(8,128)(2,1)} %copy-done.12) | copy-start | bytes 6291460
  685.3 2.8 copy-start.8
  685.3 2.8 copy-start.19
  685.3 2.8 copy-start.26
  685.3 2.8 copy-start.27
  685.3 2.8 copy-start.29
  688.1 8.9 copy-start.6
  688.1 10.5 %copy-start.15 = (bf16[1,2,128,1024]{3,2,1,0:T(8,128)(2,1)S(1)}, bf16[1,2,128,1024]{3,2,1,0:T(8,128)(2,1)}, u32[]{:S(2)}) copy-start(bf16[1,2,128,1024]{3,2,1,0:T(8,128)(2,1)} %shard_map.220) | copy-start | bytes 1572868
  688.1 10.5 %copy-start.24 = (bf16[2,128,1024]{2,1,0:T(8,128)(2,1)S(1)}, bf16[2,128,1024]{2,1,0:T(8,128)(2,1)}, u32[]{:S(2)}) copy-start(bf16[2,128,1024]{2,1,0:T(8,128)(2,1)} %copy-done.23) | copy-start | bytes 1572868
  697.0 5.9 copy-start.9
  697.0 3.6 copy-start.22
  741.4 16.0 %copy-start.10 = (f32[2,128,1024]{2,1,0:T(8,128)S(1)}, f32[2,128,1024]{2,1,0:T(8,128)}, u32[]{:S(2)}) copy-start(f32[2,128,1024]{2,1,0:T(8,128)} %copy-done.9) | copy-start | bytes 3145732
  774.9 55.8 %copy-start.4 = (bf16[2,128,1024]{2,1,0:T(8,128)(2,1)S(1)}, bf16[2,128,1024]{2,1,0:T(8,128)(2,1)}, u32[]{:S(2)}) copy-start(bf16[2,128,1024]{2,1,0:T(8,128)(2,1)} %param.14) | copy-start | bytes 1572868
  830.7 5.3 copy-start.25
  836.1 11.8 %copy-start.20 = (f32[2,128,1024]{2,1,0:T(8,128)}, f32[2,128,1024]{2,1,0:T(8,128)S(1)}, u32[]{:S(2)}) copy-start(f32[2,128,1024]{2,1,0:T(8,128)S(1)} %get-tuple-element.119) | copy-start | bytes 3145732
  836.1 5.1 copy-start.17
  836.1 5.7 copy-start.35
  903.9 18.5 %copy-start.11 = (f32[4,128,1024]{2,1,0:T(8,128)S(1)}, f32[4,128,1024]{2,1,0:T(8,128)}, u32[]{:S(2)}) copy-start(f32[4,128,1024]{2,1,0:T(8,128)} %param.18) | copy-start | bytes 6291460
  922.5 6.8 copy-start.30
  922.5 6.7 copy-start.31
  922.5 6.7 copy-start.32

commit v4 on v3

--- a/solution.py
+++ b/solution.py
@@ -168,7 +168,7 @@
 
 
 def cross_backward_body(
-    live_ref, q_ref, k_ref, v_ref, out_ref, lse_ref, grad_ref, dq_ref, dkv_ref, qs, gs, delta, dq_acc
+    first_object, live_ref, q_ref, k_ref, v_ref, out_ref, lse_ref, grad_ref, dq_ref, dkv_ref, qs, gs, delta, dq_acc
 ):
     position = pl.program_id(1)
     width = q_ref.shape[3]
@@ -179,7 +179,7 @@
         backward_prepare(q_ref, out_ref, grad_ref, qs, gs, delta)
         dq_acc[...] = jnp.zeros_like(dq_acc)
 
-    alive = position * rows < live_ref[pl.program_id(0)]
+    alive = position * rows < live_ref[pl.program_id(0) + first_object]
 
     @pl.when(alive)
     def _():
@@ -200,19 +200,20 @@
         dq_ref[...] = (dq_acc[...] * 0.125).astype(jnp.bfloat16).reshape(dq_ref.shape)
 
 
-def attend_backward(live, query_source, key_source, value_source, outs, lse, grads, step_rows):
+def attend_backward(live, query_source, key_source, value_source, outs, lse, grads, step_rows, span):
     (q_array, q_at), (k_array, k_at), (v_array, v_at) = query_source, key_source, value_source
-    groups, unused_blocks, objects, q_rows, width = q_array.shape
+    groups, unused_blocks, unused_objects, q_rows, width = q_array.shape
+    first_object, objects = span
     k_rows = k_array.shape[3]
     heads = width // HD
     total_q = groups * q_rows
     per_k = max(step_rows // k_rows, 1)
     grid = (objects, groups // per_k)
-    whole = lambda index: (lambda o, j, live: (0, index, o, 0, 0))
-    part = lambda index: (lambda o, j, live: (j, index, o, 0, 0))
-    tokens = pl.BlockSpec((groups, 1, q_rows, width), lambda o, j, live: (0, o, 0, 0))
+    whole = lambda index: (lambda o, j, live: (0, index, o + first_object, 0, 0))
+    part = lambda index: (lambda o, j, live: (j, index, o + first_object, 0, 0))
+    tokens = pl.BlockSpec((groups, 1, q_rows, width), lambda o, j, live: (0, o + first_object, 0, 0))
     return pl.pallas_call(
-        cross_backward_body,
+        functools.partial(cross_backward_body, first_object),
         grid_spec=pltpu.PrefetchScalarGridSpec(
             num_scalar_prefetch=1,
             grid=grid,
@@ -221,12 +222,12 @@
                 pl.BlockSpec((per_k, None, 1, k_rows, width), part(k_at)),
                 pl.BlockSpec((per_k, None, 1, k_rows, width), part(v_at)),
                 tokens,
-                pl.BlockSpec((1, heads, 1, total_q), lambda o, j, live: (o, 0, 0, 0)),
+                pl.BlockSpec((1, heads, 1, total_q), lambda o, j, live: (o + first_object, 0, 0, 0)),
                 pl.BlockSpec((groups, None, 1, q_rows, width), whole(0)),
             ],
             out_specs=[
-                tokens,
-                pl.BlockSpec((per_k, 2, 1, k_rows, width), part(0)),
+                pl.BlockSpec((groups, 1, q_rows, width), lambda o, j, live: (0, o, 0, 0)),
+                pl.BlockSpec((per_k, 2, 1, k_rows, width), lambda o, j, live: (j, 0, o, 0, 0)),
             ],
             scratch_shapes=[
                 pltpu.VMEM((heads, total_q, width), jnp.bfloat16),
@@ -299,6 +300,8 @@
         if kind == "heads":
             return sources[0].at[:, :, :, columns(peer)], target.at[fsdp_index]
         mine = columns(fsdp_index)
+        if kind == "objects":
+            return sources[place].at[peer], target.at[0, place : place + 1, :, mine]
         if len(sources[place].shape) == 4:
             return sources[place].at[peer], target.at[place, :, :, mine]
         return sources[place].at[peer], target.at[place : place + 2, :, :, mine]
@@ -343,6 +346,9 @@
         else:
             holds.append(array.shape[1:])
             blocks += 1 if len(array.shape) == 4 else array.shape[1]
+            if kind == "objects":
+                result = (1, len(sources), array.shape[2], 8 * array.shape[3])
+                continue
             result = (blocks,) + array.shape[-3:-1] + (8 * array.shape[-1],)
     scratch = [pltpu.SemaphoreType.DMA((2, len(sources), 8))] + [pltpu.VMEM(hold, bf) for hold in holds]
     return scratch, jax.ShapeDtypeStruct(result, bf)
@@ -525,11 +531,14 @@
     )(index, narrow, mod_rows)
 
 
-def next_gather_body(tiles, start, zoned, kind, amount, source_ref, *refs):
+def next_gather_body(tiles, start, zoned, kind, amount, ahead, source_ref, *refs):
     mix_sources, refs = refs[:amount], refs[amount:]
     out_ref, refs = refs[0], refs[1:]
     if amount:
         mixed_ref, refs = refs[0], refs[1:]
+    if ahead:
+        zone_ref, refs = refs[0], refs[1:]
+        zone_hold, zone_sems, refs = refs[0], refs[1], refs[2:]
     full, load_sems, send_sems, recv_sems, out_sems = refs[:5]
     where = places()
     dp_index, fsdp_index, z_index, core = where
@@ -548,8 +557,6 @@
         peers += [core_peer(fsdp_index)]
         peers += [] if zoned else [z_peer(fsdp_index, shift) for shift in (1, 2, 3)]
     greet(peers)
-    if amount:
-        moving = mix_begin(kind, mix_sources, mixed_ref, refs[5:], fsdp_index)
     z_copies = {}
     for tile in range(tiles):
         if zoned:
@@ -558,7 +565,19 @@
             loads[tile].wait()
             z_copies[tile] = send_z(tile, full.at[tile], fsdp_index, dp_index, z_index, (send_sems, recv_sems))
     if amount:
+        moving = mix_begin(kind, mix_sources, mixed_ref, refs[5:], fsdp_index)
         mix_own(moving)
+    if ahead:
+        later = source_ref.at[pl.ds(ahead[0], ahead[1])]
+        zone = [
+            remote(later, zone_ref.at[z_index], zone_sems.at[0, shift], zone_sems.at[1, shift], z_peer(fsdp_index, shift))
+            for shift in (1, 2, 3)
+        ]
+        zone_load = pltpu.make_async_copy(later, zone_hold, zone_sems.at[0, 0])
+        zone_load.start()
+        zone_load.wait()
+        zone_store = pltpu.make_async_copy(zone_hold, zone_ref.at[z_index], zone_sems.at[1, 0])
+        zone_store.start()
     fulls = [full.at[tile] for tile in range(tiles)]
     outs = [out_ref.at[tile] for tile in range(tiles)]
     spread(tiles, fulls, outs, z_copies, zoned, (send_sems, recv_sems, out_sems), where)
@@ -568,9 +587,13 @@
                 copy.wait_send()
     if amount:
         mix_end(moving)
-
-
-def next_gather(source, tiles, start, zoned, mix, collective):
+    if ahead:
+        for copy in zone:
+            copy.wait()
+        zone_store.wait()
+
+
+def next_gather(source, tiles, start, zoned, mix, ahead, collective):
     rows, width = source.shape[-2:]
     bf = jnp.bfloat16
     kind, mix_sources = mix if mix else (None, [])
@@ -585,8 +608,11 @@
     if mix:
         extra, result = mix_plan(mix)
         scratch, out_shape = scratch + extra, out_shape + [result]
+    if ahead:
+        scratch = [pltpu.VMEM((ahead[1], rows, width), bf), pltpu.SemaphoreType.DMA((2, 4))] + scratch
+        out_shape = out_shape + [jax.ShapeDtypeStruct((4, ahead[1], rows, width), bf)]
     results = pl.pallas_call(
-        functools.partial(next_gather_body, tiles, start, zoned, kind, len(mix_sources)),
+        functools.partial(next_gather_body, tiles, start, zoned, kind, len(mix_sources), ahead),
         in_specs=[ANY] * (1 + len(mix_sources)),
         out_specs=[ANY] * len(out_shape),
         scratch_shapes=scratch,
@@ -594,7 +620,8 @@
         compiler_params=comm_params(collective),
         cost_estimate=pl.CostEstimate(flops=0, bytes_accessed=tiles * 30_000_000, transcendentals=0),
     )(source, *mix_sources)
-    return results[0].reshape(tiles, 32 * rows, width), (results[1] if mix else None)
+    mixed = results[1] if mix else None
+    return results[0].reshape(tiles, 32 * rows, width), mixed, (results[-1] if ahead else None)
 
 
 def fast_layout(master):
@@ -740,31 +767,35 @@
     return copies
 
 
-def reduce_body(counts, extra, kind, amount, *refs):
+def reduce_body(counts, extra, plans, *refs):
     groups = len(counts)
     tiles = sum(counts)
     grads, refs = refs[:groups], refs[groups:]
     if extra:
         mod_grads, refs = refs[0], refs[1:]
-    mix_sources, refs = refs[:amount], refs[amount:]
+    mix_sources = []
+    for unused_kind, amount in plans:
+        mix_sources.append(refs[:amount])
+        refs = refs[amount:]
     out_ref, refs = refs[0], refs[1:]
     if extra:
         mod_out_ref, refs = refs[0], refs[1:]
-    if amount:
-        mixed_ref, refs = refs[0], refs[1:]
+    mixed_refs, refs = refs[: len(plans)], refs[len(plans) :]
     scratch, refs = refs[:10], refs[10:]
     if extra:
         mod_scratch, refs = refs[:10], refs[10:]
     where = places()
     dp_index, fsdp_index, core = where[0], where[1], where[3]
     peers = [dp_peer(dp_index, flip) for flip in (1, 2)]
-    if amount:
+    if plans:
         peers += fsdp_peers(fsdp_index)
     else:
         peers += [z_peer(fsdp_index, shift) for shift in (1, 2, 3)] + [core_peer(fsdp_index)]
     greet(peers)
-    if amount:
-        moving = mix_begin(kind, mix_sources, mixed_ref, refs, fsdp_index)
+    movings = []
+    for place, (kind, amount) in enumerate(plans):
+        mix_scratch, refs = refs[: 1 + amount], refs[1 + amount :]
+        movings.append(mix_begin(kind, mix_sources[place], mixed_refs[place], mix_scratch, fsdp_index))
     entries = [
         (grads[group].at[tile, :, 1 - core], grads[group].at[tile, :, core])
         for group in range(groups)
@@ -773,7 +804,7 @@
     mod_entry = [(mod_grads.at[0, :, 1 - core], mod_grads.at[0, :, core])] if extra else []
     mod_copies = core_copies(mod_entry, mod_scratch, where) if extra else []
     copies = core_copies(entries, scratch, where)
-    if amount:
+    for moving in movings:
         mix_own(moving)
     stages = reduce_stages(tiles, scratch, out_ref, where)
     if extra:
@@ -831,16 +862,15 @@
         mod_store.start()
         mod_store.wait()
     store.wait()
-    if amount:
+    for moving in movings:
         mix_end(moving)
 
 
-def reduce_tiles(grads, mods, mix, collective):
+def reduce_tiles(grads, mods, mixes, collective):
     counts = tuple(part.shape[0] for part in grads)
     tiles = sum(counts)
     rows, width = grads[0].shape[-2:]
     bf = jnp.bfloat16
-    kind, mix_sources = mix if mix else (None, [])
     operands = list(grads)
     out_shape = [jax.ShapeDtypeStruct((tiles, rows, width), bf)]
     scratch = reduce_scratch(tiles, rows, width)
@@ -848,12 +878,13 @@
         operands.append(mods)
         out_shape.append(jax.ShapeDtypeStruct((1, MOD_ROWS, width), bf))
         scratch = scratch + reduce_scratch(1, MOD_ROWS, width)
-    if mix:
-        operands += list(mix_sources)
+    for mix in mixes:
+        operands += list(mix[1])
         extra, result = mix_plan(mix)
         scratch, out_shape = scratch + extra, out_shape + [result]
+    plans = tuple((kind, len(sources)) for kind, sources in mixes)
     return pl.pallas_call(
-        functools.partial(reduce_body, counts, mods is not None, kind, len(mix_sources)),
+        functools.partial(reduce_body, counts, mods is not None, plans),
         in_specs=[ANY] * len(operands),
         out_specs=[ANY] * len(out_shape),
         scratch_shapes=scratch,
@@ -958,15 +989,20 @@
     flat = mods.reshape(8, 4, MOD_ROWS * width)[:, :, : mod_rows * mod_columns]
     mod_all = flat.reshape(8, 4, mod_rows, mod_columns).transpose(2, 1, 0, 3).reshape(mod_rows, -1)
 
+    last_zone = []
+
     def chunk(number, mix, *others):
         tiles = len(CHUNKS[number])
         if number == 0:
             return first.reshape(tiles, row_count * 8, width), None
         if number < 3:
             held = after(zoned, *others) if others else zoned
-            return next_gather(held, tiles, (0, 3)[number - 1], True, mix, number)
-        held = after(rest, *others) if others else rest
-        return next_gather(held, tiles, (0, 4)[number - 3], False, mix, number)
+            return next_gather(held, tiles, (0, 3)[number - 1], True, mix, None, number)[:2]
+        if number == 3:
+            full, mixed, zone = next_gather(rest, tiles, 0, False, mix, (tiles, 16 - EARLY - tiles), number)
+            last_zone.append(zone)
+            return full, mixed
+        return next_gather(last_zone[0], tiles, 0, True, mix, None, number)[:2]
 
     return chunk, mod_all
 
@@ -992,6 +1028,8 @@
     kind, sources = mix
     if kind == "heads":
         return exchange(by_head(sources[0], lax.axis_size("fsdp")))
+    if kind == "objects":
+        sources = [jnp.concatenate(sources, axis=1)]
     parts = [array if array.ndim == 5 else array[:, None] for array in sources]
     return from_head(exchange(jnp.concatenate(parts, axis=1)))
 
@@ -1027,11 +1065,10 @@
     fast = fast_layout(master)
     partial_sums = tile_sums if fast else contract
 
-    def reduced(grads, mods, mix, collective, *others):
+    def reduced(grads, mods, mixes, collective):
         if not fast:
-            return None, mix_generic(mix)
-        grads = list(after(tuple(grads), *others)) if others else grads
-        return reduce_tiles(grads, mods, mix, collective)
+            return [None] + [mix_generic(mix) for mix in mixes]
+        return reduce_tiles(grads, mods, mixes, collective)
 
     chunk, mod_all = weight_source(master, modulation, tile_slots)
     mod_full = mod_all.astype(jnp.float32)
@@ -1091,12 +1128,19 @@
     grad_down = partial_sums("otkd,ote->kde", hidden, grad_branch_three)
     grad_up = partial_sums("otd,otke->kde", normed_three, grad_pre)
     grad_out_two = partial_sums("otd,ote->de", merged_two, grad_branch_two)
-    sums_down, grad_cross_heads = reduced([grad_down], None, ("heads", [grad_merged_two[None]]), 5)
-    grad_query_heads, grad_pair_heads = attend_backward(
-        view_tokens, *cross_sources, cross_result, cross_logsum, grad_cross_heads, VIEW
-    )
-    grad_pair_back = exchange(grad_pair_heads)
-    sums_up, grad_query_two = reduced([grad_up], None, ("tokens", [grad_query_heads]), 6, grad_pair_heads)
+    sums_down, grad_cross_heads = reduced([grad_down], None, [("heads", [grad_merged_two[None]])], 5)
+    grad_query_heads, grad_pair_heads = [], []
+    for place in range(objects):
+        query_part, pair_part = attend_backward(
+            view_tokens, *cross_sources, cross_result, cross_logsum, grad_cross_heads, VIEW, (place, 1)
+        )
+        grad_query_heads.append(query_part)
+        grad_pair_heads.append(pair_part)
+    half = objects // 2
+    pair_mixes = [("tokens", [part]) for part in grad_pair_heads]
+    sums_up, grad_query_two, *grad_pairs = reduced(
+        [grad_up], None, [("objects", grad_query_heads)] + pair_mixes[:half], 6
+    )
     grad_query_two = grad_query_two[0]
     grad_tile_query = partial_sums("otd,ote->de", normed_two, grad_query_two)
     grad_normed_two = contract("ote,de->otd", grad_query_two, tile_query_two)
@@ -1108,17 +1152,17 @@
     grad_branch_one = (blocks[2] * grad_mid).astype(jnp.bfloat16)
     grad_merged_one = contract("ote,de->otd", grad_branch_one, tile_out_one).astype(jnp.bfloat16)
     grad_out_one = partial_sums("otd,ote->de", merged_one, grad_branch_one)
-    sums_mid, grad_self_heads = reduced(
-        [grad_out_two, grad_tile_query], None, ("heads", [grad_merged_one[None]]), 7
+    sums_mid, grad_self_heads, *more_pairs = reduced(
+        [grad_out_two, grad_tile_query], None, [("heads", [grad_merged_one[None]])] + pair_mixes[half:], 7
     )
     grad_self_query, grad_self_pair = attend_backward(
-        every_key, *self_sources, self_result, self_logsum, grad_self_heads, VIEW
-    )
-    grad_pairs = from_head(after(grad_pair_back, grad_self_query))
+        every_key, *self_sources, self_result, self_logsum, grad_self_heads, VIEW, (0, objects)
+    )
+    grad_pairs = jnp.concatenate(grad_pairs + more_pairs, axis=1)
     grad_tiles_pair = partial_sums("oid,koie->kde", image_tokens, grad_pairs)
     grad_image = contract("koie,kde->oid", grad_pairs, tiles_pair)
     sums_late, grad_triples = reduced(
-        [grad_tiles_pair, grad_out_one], None, ("tokens", [grad_self_query, grad_self_pair]), 8
+        [grad_tiles_pair, grad_out_one], None, [("tokens", [grad_self_query, grad_self_pair])], 8
     )
     grad_qkv = partial_sums("otd,kote->kde", normed_one, grad_triples)
     grad_normed_one = contract("kote,kde->otd", grad_triples, tiles_qkv)
@@ -1147,7 +1191,7 @@
         [grad_mod_rows, jnp.sum(grad_mods, axis=0, keepdims=True)], axis=0
     )
     if fast:
-        sums_qkv, mod_sum = reduce_tiles([grad_qkv], mod_sums(grad_modulation), None, 9)
+        sums_qkv, mod_sum = reduce_tiles([grad_qkv], mod_sums(grad_modulation), [], 9)
         sums = [sums_qkv, sums_late, sums_mid, sums_up, sums_down]
         order = (0, 1, 2, 5, 6, 3, 7, 4, 8, 9, 10, 11, 12, 13, 14, 15)
         tile_grad = to_owners(sums, order, tile_slots, 10).reshape(master.shape)

time: 934 us -> 896 us (0.959)
  Pallas kernels: 756 us -> 731 us
    pallas_call x4, Pallas kernels: 247 us -> 221 us  [next_gather(): pl.pallas_call(functools.partial(next_gather_body, tiles, start, zoned, k...]
    pallas_call x7 -> x8, Pallas kernels: 382 us -> 378 us  [the longest x5 320 us: reduce_tiles(): pl.pallas_call(functools.partial(reduce_body, counts, mods is not None, p...]
  transfers between devices with their start and end apart: 2 -> 1, of which waited for: 0 -> 0; matrix products, arithmetic and copies ran while one was open for 5% -> 2% of each run, Pallas kernels for 48% -> 26%
where the time goes in v4:
time: 896 us; the launch traced here: 894 us
  Pallas kernels  731 us (82%)
  matrix products  97.6 us (11%)
  local copies, waits for them, and re-layouts  32.3 us (4%)
  other arithmetic  22 us (2%)
  starting transfers between devices  9.52 us (1%)
    pallas_call x5, Pallas kernels, reduce_tiles(): pl.pallas_call(functools.partial(reduce_body, counts, mods is not None, p...  320 us
    pallas_call x4, Pallas kernels, next_gather(): pl.pallas_call(functools.partial(next_gather_body, tiles, start, zoned, k...  221 us
    dot_general x21, matrix products, contract(): return jnp.einsum(form, left, right, preferred_element_type=jnp.float32)  96.7 us
    pallas_call x1, Pallas kernels, first_gather(): pl.pallas_call(functools.partial(first_gather_body, tiles, rows), grid_sp...  62.3 us
    pallas_call x3, Pallas kernels, attend_backward(): pl.pallas_call(functools.partial(cross_backward_body, first_object), grid...  57.8 us
    pallas_call x2, Pallas kernels, attend_forward(): pl.pallas_call(functools.partial(forward_body, step_rows), grid_spec=pltp...  41.8 us
  transfers between devices with their start and end apart: 1, of which 0 were waited for; matrix products, arithmetic and copies ran while one was open for 2% of the time, Pallas kernels for 26%

profile of v4, /device:TPU:0, one launch (start us, length us, event | category | flops | bytes accessed | tf_op | source)
XLA Modules:
  0.0 894.3 jit_solution(17178431015731880388)
XLA Ops:
  0.7 2.9 convert_element_type.115
  3.5 0.8 convert_element_type.116
  5.1 1.3 pad_clamp_fusion
  6.3 1.2 fusion.52
  7.5 1.2 gather_fusion
  8.7 62.3 %shard_map.213 = (bf16[2,4,2,4,32,1024]{5,4,3,2,1,0:T(8,128)(2,1)}, bf16[4,2,4,16,1024]{4,3,2,1,0:T(8,128)(2,1)}, bf16[4,6,32,1024]{3,2,1,0:T(8,128)(2,1)}, bf16[8,32,1024]{2,1,0:T(8,128)(2,1)}) custom-call(s32[16]{0:T(128)} %gather_fusion, bf16[4,4,32,1024]{3,2,1,0:T(8,128)(2,1)} %bitcast.192, bf16[16,1024]{1,0:T(8,128)(2,1)} %reshape.214.mod_ref), custom_call_target="tpu_custom_call" | custom-call | bytes 200000000 | tf_op jit(solution)/shard_map/pallas_call | solution.py:502
  71.0 8.4 convolution_convert_fusion.1
  79.3 6.5 copy.73
  85.8 9.5 %all-to-all-start = ((bf16[8,2,2,512,128]{4,3,2,1,0:T(8,128)(2,1)}), bf16[8,2,2,512,128]{4,3,2,1,0:T(8,128)(2,1)}, u32[]{:S(2)}, u32[]{:S(2)}) async-start(bf16[8,2,2,512,128]{4,3,2,1,0:T(8,128)(2,1)} %bitcast.181), calls=%async_computation | async-start | bytes 8388608 | tf_op jit(solution)/shard_map/all_to_all | solution.py:1011
  95.3 1.9 reshape.215
  97.4 0.6 reshape.216
  98.9 32.5 %shard_map.214 = bf16[3,4,2,4,32,1024]{5,4,3,2,1,0:T(8,128)(2,1)} custom-call(bf16[4,6,32,1024]{3,2,1,0:T(8,128)(2,1)} %get-tuple-element.48.source_ref), custom_call_target="tpu_custom_call" | custom-call | bytes 90000000 | tf_op jit(solution)/shard_map/pallas_call | solution.py:614
  132.2 6.0 fusion.16.refs_0_
  138.2 80.9 %shard_map.215 = (bf16[3,4,2,4,32,1024]{5,4,3,2,1,0:T(8,128)(2,1)}, bf16[8,3,2,128,128]{4,3,2,1,0:T(8,128)(2,1)}) custom-call(bf16[4,6,32,1024]{3,2,1,0:T(8,128)(2,1)} %get-tuple-element.48.source_ref, bf16[3,2,128,1024]{3,2,1,0:T(8,128)(2,1)} %fusion.16.refs_0_), custom_call_target="tpu_custom_call" | custom-call | bytes 90000000 | tf_op jit(solution)/shard_map/pallas_call | solution.py:614
  219.1 0.8 gather_fusion.1
  220.3 13.1 %shard_map.216 = (bf16[8,2,128,128]{3,2,1,0:T(8,128)(2,1)}, f32[2,2,1,1024]{3,2,1,0:T(1,128)}) custom-call(s32[2]{0:T(128)} %broadcast_31_live_ref.2.live_ref, bf16[8,3,2,128,128]{4,3,2,1,0:T(8,128)(2,1)} %get-tuple-element.49.q_ref.k_ref.v_ref, bf16[8,3,2,128,128]{4,3,2,1,0:T(8,128)(2,1)} %get-tuple-element.49.q_ref.k_ref.v_ref, ...), custom_call_target="tpu_custom_call" | custom-call | flops 1073741824 | bytes 2097152 | tf_op jit(solution)/shard_map/pallas_call | solution.py:114
  233.5 60.0 %shard_map.217 = (bf16[4,4,2,4,32,1024]{5,4,3,2,1,0:T(8,128)(2,1)}, bf16[1,2,128,1024]{3,2,1,0:T(8,128)(2,1)}, bf16[4,4,32,1024]{3,2,1,0:T(8,128)(2,1)}) custom-call(bf16[8,32,1024]{2,1,0:T(8,128)(2,1)} %get-tuple-element.45.source_ref, bf16[8,2,128,128]{3,2,1,0:T(8,128)(2,1)} %get-tuple-element.50.refs_0_.out_ref), custom_call_target="tpu_custom_call" | custom-call | bytes 120000000 | tf_op jit(solution)/shard_map/pallas_call | solution.py:614
  293.4 5.6 fusion.65
  299.0 2.2 fusion.64
  301.5 1.6 fusion.17.refs_0_
  303.1 47.4 %shard_map.218 = (bf16[4,4,2,4,32,1024]{5,4,3,2,1,0:T(8,128)(2,1)}, bf16[8,1,2,128,128]{4,3,2,1,0:T(8,128)(2,1)}) custom-call(bf16[4,4,32,1024]{3,2,1,0:T(8,128)(2,1)} %get-tuple-element.53.source_ref, bf16[1,2,128,1024]{3,2,1,0:T(8,128)(2,1)} %fusion.17.refs_0_), custom_call_target="tpu_custom_call" | custom-call | bytes 120000000 | tf_op jit(solution)/shard_map/pallas_call | solution.py:614
  350.5 0.7 select_reduce_fusion.index_ref
  351.2 28.7 %shard_map.219 = (bf16[8,2,128,128]{3,2,1,0:T(8,128)(2,1)}, f32[2,2,1,1024]{3,2,1,0:T(1,128)}) custom-call(s32[2]{0:T(128)} %live_ref.5, bf16[8,1,2,128,128]{4,3,2,1,0:T(8,128)(2,1)} %get-tuple-element.54.q_ref, bf16[8,2,2,512,128]{4,3,2,1,0:T(8,128)(2,1)} %all-to-all-done.k_ref.v_ref, bf16[8,2,2,512,128]{4,3,2,1,0:T(8,128)(2,1)} %all-to-all-done.k_ref.v_ref), custom_call_target="tpu_custom_call" | custom-call | flops 4294967296 | bytes 5242880 | tf_op jit(solution)/shard_map/pallas_call | solution.py:114
  379.9 13.6 %shard_map.220 = bf16[1,2,128,1024]{3,2,1,0:T(8,128)(2,1)} custom-call(bf16[8,2,128,128]{3,2,1,0:T(8,128)(2,1)} %get-tuple-element.55.refs_0_.out_ref), custom_call_target="tpu_custom_call" | custom-call | bytes 30000000 | tf_op jit(solution)/shard_map/pallas_call | solution.py:369
  393.5 3.5 fusion.63
  397.2 6.5 fusion.57
  403.7 5.9 bitcast_convert_fusion
  409.6 6.3 fusion.8
  415.9 6.3 multiply_reduce_fusion
  422.3 6.1 bitcast_convert_fusion.1
  429.0 1.3 copy-done.13
  430.3 1.5 fusion.18.refs_1_
  431.8 55.4 %shard_map.221 = (bf16[4,32,1024]{2,1,0:T(8,128)(2,1)}, bf16[8,1,2,128,128]{4,3,2,1,0:T(8,128)(2,1)}) custom-call(bf16[4,4,2,4,32,1024]{5,4,3,2,1,0:T(8,128)(2,1)} %bitcast.182, bf16[1,2,128,1024]{3,2,1,0:T(8,128)(2,1)} %fusion.18.refs_1_), custom_call_target="tpu_custom_call" | custom-call | bytes 160000000 | tf_op jit(solution)/shard_map/pallas_call | solution.py:886
  487.2 21.2 %shard_map.223 = (bf16[8,1,128,128]{3,2,1,0:T(8,128)(2,1)}, bf16[8,2,1,512,128]{4,3,2,1,0:T(8,128)(2,1)}) custom-call(s32[2]{0:T(128)} %live_ref.5, bf16[8,1,2,128,128]{4,3,2,1,0:T(8,128)(2,1)} %get-tuple-element.54.q_ref, bf16[8,2,2,512,128]{4,3,2,1,0:T(8,128)(2,1)} %all-to-all-done.k_ref.v_ref, bf16[8,2,2,512,128]{4,3,2,1,0:T(8,128)(2,1)} %all-to-all-done.k_ref.v_ref, ...), custom_call_target="tpu_custom_call" | custom-call | flops 5368709120 | bytes 5242880 | tf_op jit(solution)/shard_map/pallas_call | solution.py:215
  508.4 21.0 %shard_map.222 = (bf16[8,1,128,128]{3,2,1,0:T(8,128)(2,1)}, bf16[8,2,1,512,128]{4,3,2,1,0:T(8,128)(2,1)}) custom-call(s32[2]{0:T(128)} %live_ref.5, bf16[8,1,2,128,128]{4,3,2,1,0:T(8,128)(2,1)} %get-tuple-element.54.q_ref, bf16[8,2,2,512,128]{4,3,2,1,0:T(8,128)(2,1)} %all-to-all-done.k_ref.v_ref, bf16[8,2,2,512,128]{4,3,2,1,0:T(8,128)(2,1)} %all-to-all-done.k_ref.v_ref, ...), custom_call_target="tpu_custom_call" | custom-call | flops 5368709120 | bytes 5242880 | tf_op jit(solution)/shard_map/pallas_call | solution.py:215
  529.4 85.5 %shard_map.224 = (bf16[4,32,1024]{2,1,0:T(8,128)(2,1)}, bf16[1,2,128,1024]{3,2,1,0:T(8,128)(2,1)}, bf16[2,1,512,1024]{3,2,1,0:T(8,128)(2,1)}) custom-call(bf16[4,4,2,4,32,1024]{5,4,3,2,1,0:T(8,128)(2,1)} %bitcast.177, bf16[8,1,128,128]{3,2,1,0:T(8,128)(2,1)} %get-tuple-element.60.refs_1_, bf16[8,1,128,128]{3,2,1,0:T(8,128)(2,1)} %get-tuple-element.61.refs_2_, ...), custom_call_target="tpu_custom_call" | custom-call | bytes 160000000 | tf_op jit(solution)/shard_map/pallas_call | solution.py:886
  615.0 2.0 multiply_reduce_fusion.4
  617.1 2.2 bitcast_convert_fusion.5
  619.3 2.1 bitcast_convert_fusion.6
  622.2 7.7 fusion.28
  629.8 1.5 fusion.19.refs_2_
  631.4 2.1 bitcast_convert_fusion.4
  633.5 1.5 constant_dynamic-update-slice_fusion.1
  635.0 74.2 %shard_map.225 = (bf16[2,32,1024]{2,1,0:T(8,128)(2,1)}, bf16[8,1,2,128,128]{4,3,2,1,0:T(8,128)(2,1)}, bf16[2,1,512,1024]{3,2,1,0:T(8,128)(2,1)}) custom-call(bf16[1,4,2,4,32,1024]{5,4,3,2,1,0:T(8,128)(2,1)} %bitcast.184, bf16[1,4,2,4,32,1024]{5,4,3,2,1,0:T(8,128)(2,1)} %bitcast.183, bf16[1,2,128,1024]{3,2,1,0:T(8,128)(2,1)} %fusion.19.refs_2_, ...), custom_call_target="tpu_custom_call" | custom-call | bytes 80000000 | tf_op jit(solution)/shard_map/pallas_call | solution.py:886
  709.1 3.1 constant_dynamic-update-slice_fusion
  712.2 8.3 bitcast_convert_fusion.3
  720.5 15.6 %shard_map.226 = (bf16[8,2,128,128]{3,2,1,0:T(8,128)(2,1)}, bf16[8,2,2,128,128]{4,3,2,1,0:T(8,128)(2,1)}) custom-call(s32[2]{0:T(128)} %broadcast_31_live_ref.2.live_ref, bf16[8,3,2,128,128]{4,3,2,1,0:T(8,128)(2,1)} %get-tuple-element.49.q_ref.k_ref.v_ref, bf16[8,3,2,128,128]{4,3,2,1,0:T(8,128)(2,1)} %get-tuple-element.49.q_ref.k_ref.v_ref, ...), custom_call_target="tpu_custom_call" | custom-call | flops 2684354560 | bytes 4194304 | tf_op jit(solution)/shard_map/pallas_call | solution.py:215
  736.1 56.5 %shard_map.227 = (bf16[3,32,1024]{2,1,0:T(8,128)(2,1)}, bf16[3,2,128,1024]{3,2,1,0:T(8,128)(2,1)}) custom-call(bf16[2,4,2,4,32,1024]{5,4,3,2,1,0:T(8,128)(2,1)} %bitcast.194, bf16[1,4,2,4,32,1024]{5,4,3,2,1,0:T(8,128)(2,1)} %bitcast.185, bf16[8,2,128,128]{3,2,1,0:T(8,128)(2,1)} %get-tuple-element.69.refs_2_, ...), custom_call_target="tpu_custom_call" | custom-call | bytes 120000000 | tf_op jit(solution)/shard_map/pallas_call | solution.py:886
  792.6 5.3 fusion.26
  798.0 5.1 bitcast_convert_fusion.2
  803.7 6.3 convolution_bitcast_fusion
  809.9 1.2 fusion.24
  811.2 0.7 fusion
  811.9 0.7 concatenate.17
  812.6 0.9 copy.83
  813.7 1.1 maximum_bitcast_fusion
  815.3 1.3 pad.9
  816.6 2.6 reshape.230.refs_1_
  819.2 48.8 %shard_map.228 = (bf16[3,32,1024]{2,1,0:T(8,128)(2,1)}, bf16[1,16,1024]{2,1,0:T(8,128)(2,1)}) custom-call(bf16[3,4,2,4,32,1024]{5,4,3,2,1,0:T(8,128)(2,1)} %bitcast.178, bf16[1,4,2,4,16,1024]{5,4,3,2,1,0:T(8,128)(2,1)} %reshape.230.refs_1_), custom_call_target="tpu_custom_call" | custom-call | bytes 120000000 | tf_op jit(solution)/shard_map/pallas_call | solution.py:886
  868.0 0.8 copy.112
  868.8 3.1 add_add_fusion.3
  871.9 14.7 %shard_map.229 = bf16[4,4,32,1024]{3,2,1,0:T(8,128)(2,1)} custom-call(s32[16]{0:T(128)} %select_reduce_fusion.index_ref, bf16[3,32,1024]{2,1,0:T(8,128)(2,1)} %get-tuple-element.72.refs_0_, bf16[3,32,1024]{2,1,0:T(8,128)(2,1)} %get-tuple-element.73.refs_1_, bf16[2,32,1024]{2,1,0:T(8,128)(2,1)} %get-tuple-element.74.refs_2_, ...), custom_call_target="tpu_custom_call" | custom-call | bytes 50000000 | tf_op jit(solution)/shard_map/pallas_call | solution.py:937
  886.7 6.7 fusion.60
  893.4 0.7 multiply_subtract_fusion.1
  (130 shorter events, 6.5 us)
Async XLA Ops:
  0.6 70.3 %copy-start = (bf16[2,512,1024]{2,1,0:T(8,128)(2,1)S(1)}, bf16[2,512,1024]{2,1,0:T(8,128)(2,1)}, u32[]{:S(2)}) copy-start(bf16[2,512,1024]{2,1,0:T(8,128)(2,1)} %param.15) | copy-start | bytes 6291460
  85.8 265.3 %all-to-all-start = ((bf16[8,2,2,512,128]{4,3,2,1,0:T(8,128)(2,1)}), bf16[8,2,2,512,128]{4,3,2,1,0:T(8,128)(2,1)}, u32[]{:S(2)}, u32[]{:S(2)}) async-start(bf16[8,2,2,512,128]{4,3,2,1,0:T(8,128)(2,1)} %bitcast.181), calls=%async_computation | async-start | bytes 8388608 | tf_op jit(solution)/shard_map/all_to_all | solution.py:1011
  98.6 32.8 %copy-start.2 = (bf16[2,128,1024]{2,1,0:T(8,128)(2,1)S(1)}, bf16[2,128,1024]{2,1,0:T(8,128)(2,1)}, u32[]{:S(2)}) copy-start(bf16[2,128,1024]{2,1,0:T(8,128)(2,1)} %param.14) | copy-start | bytes 1572868
  98.9 33.0 %copy-start.33 = (f32[2,16]{1,0:T(2,128)S(1)}, f32[2,16]{1,0:T(2,128)}, u32[]{:S(2)}) copy-start(f32[2,16]{1,0:T(2,128)} %param.16) | copy-start | bytes 388
  132.2 86.9 %copy-start.1 = (s32[16]{0:T(128)S(1)}, s32[16]{0:T(128)}, u32[]{:S(2)}) copy-start(s32[16]{0:T(128)} %param.21) | copy-start | bytes 196
  293.4 5.6 copy-start.3
  293.4 5.6 copy-start.18
  299.0 4.0 copy-start.5
  299.0 4.0 copy-start.11
  301.2 49.2 %copy-start.35 = (s32[16]{0:T(128)S(1)}, s32[16]{0:T(128)}, u32[]{:S(2)}) copy-start(s32[16]{0:T(128)} %get-tuple-element.126) | copy-start | bytes 196
  397.0 31.4 %copy-start.7 = (f32[2,128,1024]{2,1,0:T(8,128)}, f32[2,128,1024]{2,1,0:T(8,128)S(1)}, u32[]{:S(2)}) copy-start(f32[2,128,1024]{2,1,0:T(8,128)S(1)} %get-tuple-element.101) | copy-start | bytes 3145732
  397.0 12.7 %slice-start = ((s8[8388608]{0:T(1024)(128)(4,1)}), s8[4194304]{0:T(1024)(128)(4,1)S(1)}, s32[]{:S(2)}) async-start(s8[8388608]{0:T(1024)(128)(4,1)} %bitcast.200), calls=%async_computation.1 | async-start | bytes 8388608
  397.2 6.5 copy-start.28
  397.2 12.4 %slice-start.1 = ((s8[8388608]{0:T(1024)(128)(4,1)}), s8[4194304]{0:T(1024)(128)(4,1)S(1)}, s32[]{:S(2)}) async-start(s8[8388608]{0:T(1024)(128)(4,1)} %bitcast.200), calls=%async_computation.2 | async-start | bytes 8388608
  403.7 5.9 copy-start.37
  428.3 2.0 copy-start.13
  428.8 3.1 copy-start.15
  430.3 1.5 copy-start.22
  529.4 85.5 %copy-start.12 = (bf16[1,4,2,4,32,1024]{5,4,3,2,1,0:T(8,128)(2,1)S(1)}, bf16[1,4,2,4,32,1024]{5,4,3,2,1,0:T(8,128)(2,1)}, u32[]{:S(2)}) copy-start(bf16[1,4,2,4,32,1024]{5,4,3,2,1,0:T(8,128)(2,1)} %copy-done.11) | copy-start | bytes 6291460
  614.9 2.1 copy-start.20
  614.9 4.4 copy-start.14
  615.0 4.4 copy-start.23
  617.0 5.0 copy-start.8
  617.0 5.0 copy-start.16
  617.0 5.0 copy-start.25
  617.0 5.0 copy-start.27
  617.1 5.0 copy-start.29
  617.1 5.1 copy-start.38
  622.1 7.7 copy-start.6
  622.1 9.2 %copy-start.19 = (bf16[1,2,128,1024]{3,2,1,0:T(8,128)(2,1)S(1)}, bf16[1,2,128,1024]{3,2,1,0:T(8,128)(2,1)}, u32[]{:S(2)}) copy-start(bf16[1,2,128,1024]{3,2,1,0:T(8,128)(2,1)} %get-tuple-element.51) | copy-start | bytes 1572868
  629.8 5.1 copy-start.9
  629.8 3.6 copy-start.21
  736.1 56.5 %copy-start.4 = (bf16[2,128,1024]{2,1,0:T(8,128)(2,1)S(1)}, bf16[2,128,1024]{2,1,0:T(8,128)(2,1)}, u32[]{:S(2)}) copy-start(bf16[2,128,1024]{2,1,0:T(8,128)(2,1)} %param.14) | copy-start | bytes 1572868
  792.6 5.3 copy-start.24
  798.0 12.0 %copy-start.17 = (f32[2,128,1024]{2,1,0:T(8,128)}, f32[2,128,1024]{2,1,0:T(8,128)S(1)}, u32[]{:S(2)}) copy-start(f32[2,128,1024]{2,1,0:T(8,128)S(1)} %get-tuple-element.125) | copy-start | bytes 3145732
  798.0 5.1 copy-start.26
  798.0 5.7 copy-start.36
  819.2 49.6 %copy-start.34 = (f32[2,128]{1,0:T(2,128)S(1)}, f32[2,128]{1,0:T(2,128)}, u32[]{:S(2)}) copy-start(f32[2,128]{1,0:T(2,128)} %get-tuple-element.83) | copy-start | bytes 3076
  868.8 17.8 %copy-start.10 = (f32[4,128,1024]{2,1,0:T(8,128)S(1)}, f32[4,128,1024]{2,1,0:T(8,128)}, u32[]{:S(2)}) copy-start(f32[4,128,1024]{2,1,0:T(8,128)} %param.18) | copy-start | bytes 6291460
  886.6 6.8 copy-start.30
  886.7 6.7 copy-start.31
  886.7 6.7 copy-start.32

commit v5 on v4

--- a/solution.py
+++ b/solution.py
@@ -249,6 +249,7 @@
 
 CHUNKS = ((5, 6), (0, 1, 2), (3, 4, 7), (8, 9, 10, 11), (12, 13, 14, 15))
 EARLY = 8
+GATHER_PARTS = 1
 MOD_ROWS = 16
 MESH = pl.DeviceIdType.MESH
 
@@ -375,6 +376,12 @@
         compiler_params=comm_params(collective),
         cost_estimate=pl.CostEstimate(flops=0, bytes_accessed=30_000_000, transcendentals=0),
     )(*sources)
+
+
+def part_of(ref, unit, dims):
+    tile, part = unit // GATHER_PARTS, unit % GATHER_PARTS
+    rows = ref.shape[-2] // GATHER_PARTS
+    return ref.at[(tile,) + (slice(None),) * dims + (pl.ds(part * rows, rows),)]
 
 
 def send_z(unit, full, fsdp_index, dp_index, z_index, sems):
@@ -444,13 +451,15 @@
     mod_load = pltpu.make_async_copy(mod_ref, mod_full.at[z_index, dp_index], load_sems.at[1])
     mod_load.start()
     mod_load.wait()
-    z_copies = {tiles: send_z(tiles, mod_full, fsdp_index, dp_index, z_index, (send_sems, recv_sems))}
+    units = tiles * GATHER_PARTS
+    z_copies = {units: send_z(units, mod_full, fsdp_index, dp_index, z_index, (send_sems, recv_sems))}
     own.wait()
     for swap in swaps:
         swap.wait()
     for tile in range(tiles):
         full[tile, z_index, dp_index] = stacked[index_ref[tile]]
-        z_copies[tile] = send_z(tile, full.at[tile], fsdp_index, dp_index, z_index, (send_sems, recv_sems))
+        for unit in range(tile * GATHER_PARTS, (tile + 1) * GATHER_PARTS):
+            z_copies[unit] = send_z(unit, part_of(full, unit, 2), fsdp_index, dp_index, z_index, (send_sems, recv_sems))
 
     def take(position, carried):
         mine[position] = stacked[index_ref[position + tiles]]
@@ -466,10 +475,10 @@
     zone_own.start()
     rest = pltpu.make_async_copy(mine.at[pl.ds(early, 16 - EARLY)], rest_ref, load_sems.at[3])
     rest.start()
-    fulls = [full.at[tile] for tile in range(tiles)] + [mod_full]
-    outs = [out_ref.at[tile] for tile in range(tiles)] + [mod_out_ref]
-    spread(tiles + 1, fulls, outs, z_copies, False, (send_sems, recv_sems, out_sems), where)
-    for unit in range(tiles + 1):
+    fulls = [part_of(full, unit, 2) for unit in range(units)] + [mod_full]
+    outs = [part_of(out_ref, unit, 3) for unit in range(units)] + [mod_out_ref]
+    spread(units + 1, fulls, outs, z_copies, False, (send_sems, recv_sems, out_sems), where)
+    for unit in range(units + 1):
         for copy in z_copies[unit]:
             copy.wait_send()
     for copy in zone:
@@ -514,9 +523,9 @@
                 pltpu.VMEM((4, EARLY - tiles, rows, width), bf),
                 pltpu.SemaphoreType.DMA((2, 4)),
                 pltpu.SemaphoreType.DMA((8,)),
-                pltpu.SemaphoreType.DMA((tiles + 1, 10)),
-                pltpu.SemaphoreType.DMA((tiles + 1, 10)),
-                pltpu.SemaphoreType.DMA((tiles + 1,)),
+                pltpu.SemaphoreType.DMA((tiles * GATHER_PARTS + 1, 10)),
+                pltpu.SemaphoreType.DMA((tiles * GATHER_PARTS + 1, 10)),
+                pltpu.SemaphoreType.DMA((tiles * GATHER_PARTS + 1,)),
                 pltpu.SemaphoreType.DMA((2, 3)),
             ],
         ),
@@ -550,6 +559,7 @@
             load = pltpu.make_async_copy(source_ref.at[start + tile], full.at[tile, z_index, dp_index], load_sems.at[tile])
         load.start()
         loads.append(load)
+    units = tiles * GATHER_PARTS
     peers = [dp_peer(dp_index, flip) for flip in (1, 2)]
     if amount:
         peers += fsdp_peers(fsdp_index)
@@ -559,11 +569,14 @@
     greet(peers)
     z_copies = {}
     for tile in range(tiles):
+        near = range(tile * GATHER_PARTS, (tile + 1) * GATHER_PARTS)
         if zoned:
-            z_copies[tile] = [loads[tile]]
+            for unit in near:
+                z_copies[unit] = [loads[tile]] if unit == near[0] else []
         else:
             loads[tile].wait()
-            z_copies[tile] = send_z(tile, full.at[tile], fsdp_index, dp_index, z_index, (send_sems, recv_sems))
+            for unit in near:
+                z_copies[unit] = send_z(unit, part_of(full, unit, 2), fsdp_index, dp_index, z_index, (send_sems, recv_sems))
     if amount:
         moving = mix_begin(kind, mix_sources, mixed_ref, refs[5:], fsdp_index)
         mix_own(moving)
@@ -578,12 +591,12 @@
         zone_load.wait()
         zone_store = pltpu.make_async_copy(zone_hold, zone_ref.at[z_index], zone_sems.at[1, 0])
         zone_store.start()
-    fulls = [full.at[tile] for tile in range(tiles)]
-    outs = [out_ref.at[tile] for tile in range(tiles)]
-    spread(tiles, fulls, outs, z_copies, zoned, (send_sems, recv_sems, out_sems), where)
+    fulls = [part_of(full, unit, 2) for unit in range(units)]
+    outs = [part_of(out_ref, unit, 3) for unit in range(units)]
+    spread(units, fulls, outs, z_copies, zoned, (send_sems, recv_sems, out_sems), where)
     if not zoned:
-        for tile in range(tiles):
-            for copy in z_copies[tile]:
+        for unit in range(units):
+            for copy in z_copies[unit]:
                 copy.wait_send()
     if amount:
         mix_end(moving)
@@ -601,9 +614,9 @@
     scratch = [
         pltpu.VMEM((tiles, 4, 4, rows, width), bf),
         pltpu.SemaphoreType.DMA((tiles,)),
-        pltpu.SemaphoreType.DMA((tiles, 10)),
-        pltpu.SemaphoreType.DMA((tiles, 10)),
-        pltpu.SemaphoreType.DMA((tiles,)),
+        pltpu.SemaphoreType.DMA((tiles * GATHER_PARTS, 10)),
+        pltpu.SemaphoreType.DMA((tiles * GATHER_PARTS, 10)),
+        pltpu.SemaphoreType.DMA((tiles * GATHER_PARTS,)),
     ]
     if mix:
         extra, result = mix_plan(mix)
@@ -767,9 +780,9 @@
     return copies
 
 
-def reduce_body(counts, extra, plans, *refs):
+def reduce_body(counts, extra, plans, parts, *refs):
     groups = len(counts)
-    tiles = sum(counts)
+    tiles = sum(counts) * parts
     grads, refs = refs[:groups], refs[groups:]
     if extra:
         mod_grads, refs = refs[0], refs[1:]
@@ -796,10 +809,12 @@
     for place, (kind, amount) in enumerate(plans):
         mix_scratch, refs = refs[: 1 + amount], refs[1 + amount :]
         movings.append(mix_begin(kind, mix_sources[place], mixed_refs[place], mix_scratch, fsdp_index))
+    rows = out_ref.shape[1]
     entries = [
-        (grads[group].at[tile, :, 1 - core], grads[group].at[tile, :, core])
+        tuple(grads[group].at[tile, :, side, :, pl.ds(part * rows, rows)] for side in (1 - core, core))
         for group in range(groups)
         for tile in range(counts[group])
+        for part in range(parts)
     ]
     mod_entry = [(mod_grads.at[0, :, 1 - core], mod_grads.at[0, :, core])] if extra else []
     mod_copies = core_copies(mod_entry, mod_scratch, where) if extra else []
@@ -866,10 +881,11 @@
         mix_end(moving)
 
 
-def reduce_tiles(grads, mods, mixes, collective):
+def reduce_tiles(grads, mods, mixes, collective, parts=1):
     counts = tuple(part.shape[0] for part in grads)
-    tiles = sum(counts)
+    tiles = sum(counts) * parts
     rows, width = grads[0].shape[-2:]
+    rows = rows // parts
     bf = jnp.bfloat16
     operands = list(grads)
     out_shape = [jax.ShapeDtypeStruct((tiles, rows, width), bf)]
@@ -883,15 +899,16 @@
         extra, result = mix_plan(mix)
         scratch, out_shape = scratch + extra, out_shape + [result]
     plans = tuple((kind, len(sources)) for kind, sources in mixes)
-    return pl.pallas_call(
-        functools.partial(reduce_body, counts, mods is not None, plans),
+    results = pl.pallas_call(
+        functools.partial(reduce_body, counts, mods is not None, plans, parts),
         in_specs=[ANY] * len(operands),
         out_specs=[ANY] * len(out_shape),
         scratch_shapes=scratch,
         out_shape=out_shape,
         compiler_params=comm_params(collective),
-        cost_estimate=pl.CostEstimate(flops=0, bytes_accessed=tiles * 40_000_000, transcendentals=0),
+        cost_estimate=pl.CostEstimate(flops=0, bytes_accessed=tiles * 20_000_000, transcendentals=0),
     )(*operands)
+    return [results[0].reshape(-1, rows * parts, width)] + list(results[1:])
 
 
 def owner_body(counts, index_ref, *refs):
@@ -1007,6 +1024,34 @@
     return chunk, mod_all
 
 
+def pair_body(x_ref, w_ref, out_ref):
+    objects, rows, width = x_ref.shape
+    values = dot(x_ref[...].reshape(objects * rows, width), w_ref[0], NN).astype(jnp.bfloat16)
+    for side in range(2):
+        part = values[:, side * LANES : (side + 1) * LANES]
+        out_ref[side, 0] = part.reshape(objects, rows, LANES)
+
+
+def project_pairs(tokens, tiles):
+    objects, rows, width = tokens.shape
+    blocks = tiles.shape[0]
+    return pl.pallas_call(
+        pair_body,
+        grid=(blocks, 4),
+        in_specs=[
+            pl.BlockSpec((objects, rows, width), lambda k, g: (0, 0, 0)),
+            pl.BlockSpec((1, width, 2 * LANES), lambda k, g: (k, 0, g)),
+        ],
+        out_specs=pl.BlockSpec((2, 1, objects, rows, LANES), lambda k, g: (g, k, 0, 0, 0)),
+        out_shape=jax.ShapeDtypeStruct((8, blocks, objects, rows, LANES), jnp.bfloat16),
+        cost_estimate=pl.CostEstimate(
+            flops=2 * objects * rows * width * blocks * 8 * LANES,
+            bytes_accessed=2 * objects * rows * (width + blocks * 8 * LANES),
+            transcendentals=0,
+        ),
+    )(tokens, tiles)
+
+
 def exchange(pieces):
     return lax.all_to_all(pieces, "fsdp", split_axis=0, concat_axis=0, tiled=True)
 
@@ -1065,10 +1110,10 @@
     fast = fast_layout(master)
     partial_sums = tile_sums if fast else contract
 
-    def reduced(grads, mods, mixes, collective):
+    def reduced(grads, mods, mixes, collective, parts=1):
         if not fast:
             return [None] + [mix_generic(mix) for mix in mixes]
-        return reduce_tiles(grads, mods, mixes, collective)
+        return reduce_tiles(grads, mods, mixes, collective, parts)
 
     chunk, mod_all = weight_source(master, modulation, tile_slots)
     mod_full = mod_all.astype(jnp.float32)
@@ -1081,8 +1126,11 @@
         for position in range(9)
     ]
     tiles_pair, unused_mix = chunk(0, None)
-    image_pairs = contract("oid,kde->koie", image_tokens, tiles_pair).astype(jnp.bfloat16)
-    pair_sent = by_head(image_pairs, groups)
+    if fast:
+        pair_sent = project_pairs(image_tokens, tiles_pair)
+    else:
+        image_pairs = contract("oid,kde->koie", image_tokens, tiles_pair).astype(jnp.bfloat16)
+        pair_sent = by_head(image_pairs, groups)
     pair_heads = exchange(pair_sent)
     tiles_qkv, unused_mix = chunk(1, None, pair_sent)
     residual_in = triplane.astype(jnp.float32)
@@ -1128,7 +1176,7 @@
     grad_down = partial_sums("otkd,ote->kde", hidden, grad_branch_three)
     grad_up = partial_sums("otd,otke->kde", normed_three, grad_pre)
     grad_out_two = partial_sums("otd,ote->de", merged_two, grad_branch_two)
-    sums_down, grad_cross_heads = reduced([grad_down], None, [("heads", [grad_merged_two[None]])], 5)
+    sums_down, grad_cross_heads = reduced([grad_down], None, [("heads", [grad_merged_two[None]])], 5, 2)
     grad_query_heads, grad_pair_heads = [], []
     for place in range(objects):
         query_part, pair_part = attend_backward(
@@ -1191,7 +1239,7 @@
         [grad_mod_rows, jnp.sum(grad_mods, axis=0, keepdims=True)], axis=0
     )
     if fast:
-        sums_qkv, mod_sum = reduce_tiles([grad_qkv], mod_sums(grad_modulation), [], 9)
+        sums_qkv, mod_sum = reduce_tiles([grad_qkv], mod_sums(grad_modulation), [], 9, 2)
         sums = [sums_qkv, sums_late, sums_mid, sums_up, sums_down]
         order = (0, 1, 2, 5, 6, 3, 7, 4, 8, 9, 10, 11, 12, 13, 14, 15)
         tile_grad = to_owners(sums, order, tile_slots, 10).reshape(master.shape)

time: 896 us -> 890 us (level); the launches traced: 894 us -> 875 us
  local copies, waits for them, and re-layouts: 32.3 us -> 21.3 us
    pallas_call x0 -> x1, Pallas kernels: none -> 10 us  [project_pairs(): pl.pallas_call(pair_body, grid=(blocks, 4), in_specs=[pl.BlockSpec((objec...]
    dot_general x21 -> x20, matrix products: 96.7 us -> 90.4 us  [contract(): return jnp.einsum(form, left, right, preferred_element_type=jnp.float32)]
  transfers between devices with their start and end apart: 1 -> 1, of which waited for: 0 -> 0; matrix products, arithmetic and copies ran while one was open for 2% -> 2% of each run, Pallas kernels for 26% -> 27%
where the time goes in v5:
time: 890 us; the launch traced here: 875 us
  Pallas kernels  733 us (82%)
  matrix products  91.4 us (10%)
  local copies, waits for them, and re-layouts  21.3 us (2%)
  other arithmetic  17.7 us (2%)
  starting transfers between devices  9.39 us (1%)
    pallas_call x5, Pallas kernels, reduce_tiles(): pl.pallas_call(functools.partial(reduce_body, counts, mods is not None, p...  312 us
    pallas_call x4, Pallas kernels, next_gather(): pl.pallas_call(functools.partial(next_gather_body, tiles, start, zoned, k...  222 us
    dot_general x20, matrix products, contract(): return jnp.einsum(form, left, right, preferred_element_type=jnp.float32)  90.4 us
    pallas_call x1, Pallas kernels, first_gather(): pl.pallas_call(functools.partial(first_gather_body, tiles, rows), grid_sp...  62.3 us
    pallas_call x3, Pallas kernels, attend_backward(): pl.pallas_call(functools.partial(cross_backward_body, first_object), grid...  59.1 us
    pallas_call x2, Pallas kernels, attend_forward(): pl.pallas_call(functools.partial(forward_body, step_rows), grid_spec=pltp...  41.7 us
  transfers between devices with their start and end apart: 1, of which 0 were waited for; matrix products, arithmetic and copies ran while one was open for 2% of the time, Pallas kernels for 27%

profile of v5, /device:TPU:0, one launch (start us, length us, event | category | flops | bytes accessed | tf_op | source)
XLA Modules:
  0.0 874.6 jit_solution(5236941171363278480)
XLA Ops:
  0.7 2.7 convert_element_type.109
  3.4 0.8 convert_element_type.110
  4.3 0.6 reshape.217.mod_ref
  4.9 0.7 pad_clamp_fusion
  5.6 0.7 fusion.51
  6.3 1.2 gather_fusion
  7.4 62.3 %shard_map.213 = (bf16[2,4,2,4,32,1024]{5,4,3,2,1,0:T(8,128)(2,1)}, bf16[4,2,4,16,1024]{4,3,2,1,0:T(8,128)(2,1)}, bf16[4,6,32,1024]{3,2,1,0:T(8,128)(2,1)}, bf16[8,32,1024]{2,1,0:T(8,128)(2,1)}) custom-call(s32[16]{0:T(128)} %gather_fusion, bf16[4,4,32,1024]{3,2,1,0:T(8,128)(2,1)} %bitcast.182, bf16[16,1024]{1,0:T(8,128)(2,1)} %reshape.217.mod_ref), custom_call_target="tpu_custom_call" | custom-call | bytes 200000000 | tf_op jit(solution)/shard_map/pallas_call | solution.py:511
  69.7 10.0 %shard_map.214 = bf16[8,2,2,512,128]{4,3,2,1,0:T(8,128)(2,1)} custom-call(bf16[2,512,1024]{2,1,0:T(8,128)(2,1)} %x_ref.1, bf16[2,1024,1024]{2,1,0:T(8,128)(2,1)} %bitcast.196), custom_call_target="tpu_custom_call" | custom-call | flops 4294967296 | bytes 6291456 | tf_op jit(solution)/shard_map/pallas_call | solution.py:1038
  79.8 9.4 %all-to-all-start = ((bf16[8,2,2,512,128]{4,3,2,1,0:T(8,128)(2,1)}), bf16[8,2,2,512,128]{4,3,2,1,0:T(8,128)(2,1)}, u32[]{:S(2)}, u32[]{:S(2)}) async-start(bf16[8,2,2,512,128]{4,3,2,1,0:T(8,128)(2,1)} %shard_map.214), calls=%async_computation | async-start | bytes 8388608 | tf_op jit(solution)/shard_map/all_to_all | solution.py:1056
  89.2 0.8 reshape.218
  90.2 0.6 reshape.219
  90.9 0.5 slice.58
  91.7 32.5 %shard_map.215 = bf16[3,4,2,4,32,1024]{5,4,3,2,1,0:T(8,128)(2,1)} custom-call(bf16[4,6,32,1024]{3,2,1,0:T(8,128)(2,1)} %get-tuple-element.48.source_ref), custom_call_target="tpu_custom_call" | custom-call | bytes 90000000 | tf_op jit(solution)/shard_map/pallas_call | solution.py:627
  125.0 6.0 fusion.15.refs_0_
  131.0 82.0 %shard_map.216 = (bf16[3,4,2,4,32,1024]{5,4,3,2,1,0:T(8,128)(2,1)}, bf16[8,3,2,128,128]{4,3,2,1,0:T(8,128)(2,1)}) custom-call(bf16[4,6,32,1024]{3,2,1,0:T(8,128)(2,1)} %get-tuple-element.48.source_ref, bf16[3,2,128,1024]{3,2,1,0:T(8,128)(2,1)} %fusion.15.refs_0_), custom_call_target="tpu_custom_call" | custom-call | bytes 90000000 | tf_op jit(solution)/shard_map/pallas_call | solution.py:627
  212.9 0.7 gather_fusion.1
  213.6 0.5 broadcast_31_live_ref.2.live_ref
  214.1 12.9 %shard_map.217 = (bf16[8,2,128,128]{3,2,1,0:T(8,128)(2,1)}, f32[2,2,1,1024]{3,2,1,0:T(1,128)}) custom-call(s32[2]{0:T(128)} %broadcast_31_live_ref.2.live_ref, bf16[8,3,2,128,128]{4,3,2,1,0:T(8,128)(2,1)} %get-tuple-element.49.q_ref.k_ref.v_ref, bf16[8,3,2,128,128]{4,3,2,1,0:T(8,128)(2,1)} %get-tuple-element.49.q_ref.k_ref.v_ref, ...), custom_call_target="tpu_custom_call" | custom-call | flops 1073741824 | bytes 2097152 | tf_op jit(solution)/shard_map/pallas_call | solution.py:114
  227.0 60.0 %shard_map.218 = (bf16[4,4,2,4,32,1024]{5,4,3,2,1,0:T(8,128)(2,1)}, bf16[1,2,128,1024]{3,2,1,0:T(8,128)(2,1)}, bf16[4,4,32,1024]{3,2,1,0:T(8,128)(2,1)}) custom-call(bf16[8,32,1024]{2,1,0:T(8,128)(2,1)} %get-tuple-element.45.source_ref, bf16[8,2,128,128]{3,2,1,0:T(8,128)(2,1)} %get-tuple-element.50.refs_0_.out_ref), custom_call_target="tpu_custom_call" | custom-call | bytes 120000000 | tf_op jit(solution)/shard_map/pallas_call | solution.py:627
  287.0 5.6 fusion.64
  292.6 2.2 fusion.63
  295.0 1.6 fusion.16.refs_0_
  296.6 47.4 %shard_map.219 = (bf16[4,4,2,4,32,1024]{5,4,3,2,1,0:T(8,128)(2,1)}, bf16[8,1,2,128,128]{4,3,2,1,0:T(8,128)(2,1)}) custom-call(bf16[4,4,32,1024]{3,2,1,0:T(8,128)(2,1)} %get-tuple-element.53.source_ref, bf16[1,2,128,1024]{3,2,1,0:T(8,128)(2,1)} %fusion.16.refs_0_), custom_call_target="tpu_custom_call" | custom-call | bytes 120000000 | tf_op jit(solution)/shard_map/pallas_call | solution.py:627
  344.0 0.8 select_reduce_fusion.index_ref
  344.8 28.8 %shard_map.220 = (bf16[8,2,128,128]{3,2,1,0:T(8,128)(2,1)}, f32[2,2,1,1024]{3,2,1,0:T(1,128)}) custom-call(s32[2]{0:T(128)} %live_ref.5, bf16[8,1,2,128,128]{4,3,2,1,0:T(8,128)(2,1)} %get-tuple-element.54.q_ref, bf16[8,2,2,512,128]{4,3,2,1,0:T(8,128)(2,1)} %all-to-all-done.k_ref.v_ref, bf16[8,2,2,512,128]{4,3,2,1,0:T(8,128)(2,1)} %all-to-all-done.k_ref.v_ref), custom_call_target="tpu_custom_call" | custom-call | flops 4294967296 | bytes 5242880 | tf_op jit(solution)/shard_map/pallas_call | solution.py:114
  373.5 13.6 %shard_map.221 = bf16[1,2,128,1024]{3,2,1,0:T(8,128)(2,1)} custom-call(bf16[8,2,128,128]{3,2,1,0:T(8,128)(2,1)} %get-tuple-element.55.refs_0_.out_ref), custom_call_target="tpu_custom_call" | custom-call | bytes 30000000 | tf_op jit(solution)/shard_map/pallas_call | solution.py:370
  387.2 3.5 fusion.62
  390.9 6.0 fusion.56
  397.0 6.0 bitcast_convert_fusion
  403.0 4.9 fusion.8
  408.0 6.3 multiply_reduce_fusion
  414.3 6.1 bitcast_convert_fusion.1
  420.8 1.0 copy-done.12
  422.3 1.5 fusion.17.refs_1_
  423.9 51.2 %shard_map.222 = (bf16[8,16,1024]{2,1,0:T(8,128)(2,1)}, bf16[8,1,2,128,128]{4,3,2,1,0:T(8,128)(2,1)}) custom-call(bf16[4,4,2,4,32,1024]{5,4,3,2,1,0:T(8,128)(2,1)} %bitcast.172, bf16[1,2,128,1024]{3,2,1,0:T(8,128)(2,1)} %fusion.17.refs_1_), custom_call_target="tpu_custom_call" | custom-call | bytes 160000000 | tf_op jit(solution)/shard_map/pallas_call | solution.py:902
  475.1 26.9 %shard_map.224 = (bf16[8,1,128,128]{3,2,1,0:T(8,128)(2,1)}, bf16[8,2,1,512,128]{4,3,2,1,0:T(8,128)(2,1)}) custom-call(s32[2]{0:T(128)} %live_ref.5, bf16[8,1,2,128,128]{4,3,2,1,0:T(8,128)(2,1)} %get-tuple-element.54.q_ref, bf16[8,2,2,512,128]{4,3,2,1,0:T(8,128)(2,1)} %all-to-all-done.k_ref.v_ref, bf16[8,2,2,512,128]{4,3,2,1,0:T(8,128)(2,1)} %all-to-all-done.k_ref.v_ref, ...), custom_call_target="tpu_custom_call" | custom-call | flops 5368709120 | bytes 5242880 | tf_op jit(solution)/shard_map/pallas_call | solution.py:215
  502.0 16.4 %shard_map.223 = (bf16[8,1,128,128]{3,2,1,0:T(8,128)(2,1)}, bf16[8,2,1,512,128]{4,3,2,1,0:T(8,128)(2,1)}) custom-call(s32[2]{0:T(128)} %live_ref.5, bf16[8,1,2,128,128]{4,3,2,1,0:T(8,128)(2,1)} %get-tuple-element.54.q_ref, bf16[8,2,2,512,128]{4,3,2,1,0:T(8,128)(2,1)} %all-to-all-done.k_ref.v_ref, bf16[8,2,2,512,128]{4,3,2,1,0:T(8,128)(2,1)} %all-to-all-done.k_ref.v_ref, ...), custom_call_target="tpu_custom_call" | custom-call | flops 5368709120 | bytes 5242880 | tf_op jit(solution)/shard_map/pallas_call | solution.py:215
  518.5 85.0 %shard_map.225 = (bf16[4,32,1024]{2,1,0:T(8,128)(2,1)}, bf16[1,2,128,1024]{3,2,1,0:T(8,128)(2,1)}, bf16[2,1,512,1024]{3,2,1,0:T(8,128)(2,1)}) custom-call(bf16[4,4,2,4,32,1024]{5,4,3,2,1,0:T(8,128)(2,1)} %bitcast.168, bf16[8,1,128,128]{3,2,1,0:T(8,128)(2,1)} %get-tuple-element.60.refs_1_, bf16[8,1,128,128]{3,2,1,0:T(8,128)(2,1)} %get-tuple-element.61.refs_2_, ...), custom_call_target="tpu_custom_call" | custom-call | bytes 80000000 | tf_op jit(solution)/shard_map/pallas_call | solution.py:902
  603.5 2.1 multiply_reduce_fusion.4
  605.7 2.2 bitcast_convert_fusion.5
  608.0 2.1 bitcast_convert_fusion.6
  610.0 0.6 multiply_reduce_fusion.2
  610.7 7.7 fusion.27
  618.4 1.5 fusion.18.refs_2_
  620.0 2.1 bitcast_convert_fusion.4
  622.1 1.6 constant_dynamic-update-slice_fusion.1
  623.7 73.1 %shard_map.226 = (bf16[2,32,1024]{2,1,0:T(8,128)(2,1)}, bf16[8,1,2,128,128]{4,3,2,1,0:T(8,128)(2,1)}, bf16[2,1,512,1024]{3,2,1,0:T(8,128)(2,1)}) custom-call(bf16[1,4,2,4,32,1024]{5,4,3,2,1,0:T(8,128)(2,1)} %bitcast.174, bf16[1,4,2,4,32,1024]{5,4,3,2,1,0:T(8,128)(2,1)} %bitcast.173, bf16[1,2,128,1024]{3,2,1,0:T(8,128)(2,1)} %fusion.18.refs_2_, ...), custom_call_target="tpu_custom_call" | custom-call | bytes 40000000 | tf_op jit(solution)/shard_map/pallas_call | solution.py:902
  696.8 3.1 constant_dynamic-update-slice_fusion
  699.9 8.4 bitcast_convert_fusion.3
  708.3 15.8 %shard_map.227 = (bf16[8,2,128,128]{3,2,1,0:T(8,128)(2,1)}, bf16[8,2,2,128,128]{4,3,2,1,0:T(8,128)(2,1)}) custom-call(s32[2]{0:T(128)} %broadcast_31_live_ref.2.live_ref, bf16[8,3,2,128,128]{4,3,2,1,0:T(8,128)(2,1)} %get-tuple-element.49.q_ref.k_ref.v_ref, bf16[8,3,2,128,128]{4,3,2,1,0:T(8,128)(2,1)} %get-tuple-element.49.q_ref.k_ref.v_ref, ...), custom_call_target="tpu_custom_call" | custom-call | flops 2684354560 | bytes 4194304 | tf_op jit(solution)/shard_map/pallas_call | solution.py:215
  724.1 56.1 %shard_map.228 = (bf16[3,32,1024]{2,1,0:T(8,128)(2,1)}, bf16[3,2,128,1024]{3,2,1,0:T(8,128)(2,1)}) custom-call(bf16[2,4,2,4,32,1024]{5,4,3,2,1,0:T(8,128)(2,1)} %bitcast.183, bf16[1,4,2,4,32,1024]{5,4,3,2,1,0:T(8,128)(2,1)} %bitcast.175, bf16[8,2,128,128]{3,2,1,0:T(8,128)(2,1)} %get-tuple-element.69.refs_2_, ...), custom_call_target="tpu_custom_call" | custom-call | bytes 60000000 | tf_op jit(solution)/shard_map/pallas_call | solution.py:902
  780.3 5.3 fusion.25
  785.6 4.7 bitcast_convert_fusion.2
  790.3 0.6 fusion.23
  791.1 0.7 fusion
  791.7 0.7 concatenate.17
  793.7 1.6 reshape.232.refs_1_
  795.3 46.1 %shard_map.229 = (bf16[6,16,1024]{2,1,0:T(8,128)(2,1)}, bf16[1,16,1024]{2,1,0:T(8,128)(2,1)}) custom-call(bf16[3,4,2,4,32,1024]{5,4,3,2,1,0:T(8,128)(2,1)} %bitcast.169, bf16[1,4,2,4,16,1024]{5,4,3,2,1,0:T(8,128)(2,1)} %reshape.232.refs_1_), custom_call_target="tpu_custom_call" | custom-call | bytes 120000000 | tf_op jit(solution)/shard_map/pallas_call | solution.py:902
  841.4 0.8 copy.102
  842.3 10.1 %convolution_bitcast_fusion = f32[2,512,1024]{2,1,0:T(8,128)} fusion(bf16[2,2,512,1024]{3,2,1,0:T(8,128)(2,1)} %constant_dynamic-update-slice_fusion, bf16[2,1024,1024,1]{2,1,3,0:T(8,128)(2,1)} %bitcast.197), kind=kOutput, calls=%fused_computation.25 | convolution fusion | flops 4294967296 | bytes 12582912 | tf_op jit(solution)/shard_map/koie,kde->oid/dot_general | solution.py:27
  852.4 1.4 add_add_fusion.3
  853.7 13.1 %shard_map.230 = bf16[4,4,32,1024]{3,2,1,0:T(8,128)(2,1)} custom-call(s32[16]{0:T(128)} %select_reduce_fusion.index_ref, bf16[3,32,1024]{2,1,0:T(8,128)(2,1)} %bitcast.187, bf16[3,32,1024]{2,1,0:T(8,128)(2,1)} %get-tuple-element.73.refs_1_, bf16[2,32,1024]{2,1,0:T(8,128)(2,1)} %get-tuple-element.74.refs_2_, bf16[4,32,1024]{2,1,0:T(8,128)(2,1)} %get-tuple-element.75.refs_3_, ...), custom_call_target="tpu_custom_call" | custom-call | bytes 50000000 | tf_op jit(solution)/shard_map/pallas_call | solution.py:954
  866.9 6.9 fusion.59
  873.8 0.7 multiply_subtract_fusion.1
  (113 shorter events, 4.4 us)
Async XLA Ops:
  0.6 124.0 %copy-start = (f32[2,16]{1,0:T(2,128)S(1)}, f32[2,16]{1,0:T(2,128)}, u32[]{:S(2)}) copy-start(f32[2,16]{1,0:T(2,128)} %param.16) | copy-start | bytes 388
  79.8 9.4 %copy-start.21 = (bf16[4,2,4,16,1024]{4,3,2,1,0:T(8,128)(2,1)S(1)}, bf16[4,2,4,16,1024]{4,3,2,1,0:T(8,128)(2,1)}, u32[]{:S(2)}) copy-start(bf16[4,2,4,16,1024]{4,3,2,1,0:T(8,128)(2,1)} %get-tuple-element.44) | copy-start | bytes 3145732
  79.8 265.0 %all-to-all-start = ((bf16[8,2,2,512,128]{4,3,2,1,0:T(8,128)(2,1)}), bf16[8,2,2,512,128]{4,3,2,1,0:T(8,128)(2,1)}, u32[]{:S(2)}, u32[]{:S(2)}) async-start(bf16[8,2,2,512,128]{4,3,2,1,0:T(8,128)(2,1)} %shard_map.214), calls=%async_computation | async-start | bytes 8388608 | tf_op jit(solution)/shard_map/all_to_all | solution.py:1056
  91.4 32.8 %copy-start.2 = (bf16[2,128,1024]{2,1,0:T(8,128)(2,1)S(1)}, bf16[2,128,1024]{2,1,0:T(8,128)(2,1)}, u32[]{:S(2)}) copy-start(bf16[2,128,1024]{2,1,0:T(8,128)(2,1)} %param.14) | copy-start | bytes 1572868
  124.9 88.0 %copy-start.1 = (s32[16]{0:T(128)S(1)}, s32[16]{0:T(128)}, u32[]{:S(2)}) copy-start(s32[16]{0:T(128)} %param.21) | copy-start | bytes 196
  287.0 5.6 copy-start.14
  292.6 4.1 copy-start.3
  292.6 4.1 copy-start.8
  390.7 12.4 %slice-start = ((s8[8388608]{0:T(1024)(128)(4,1)}), s8[4194304]{0:T(1024)(128)(4,1)S(1)}, s32[]{:S(2)}) async-start(s8[8388608]{0:T(1024)(128)(4,1)} %bitcast.191), calls=%async_computation.1 | async-start | bytes 8388608
  390.9 6.0 copy-start.23
  390.9 12.1 %slice-start.1 = ((s8[8388608]{0:T(1024)(128)(4,1)}), s8[4194304]{0:T(1024)(128)(4,1)S(1)}, s32[]{:S(2)}) async-start(s8[8388608]{0:T(1024)(128)(4,1)} %bitcast.191), calls=%async_computation.2 | async-start | bytes 8388608
  396.9 6.1 copy-start.29
  420.3 2.0 copy-start.10
  420.8 1.0 copy-start.12
  422.3 1.5 copy-start.17
  518.5 85.1 %copy-start.9 = (bf16[1,4,2,4,32,1024]{5,4,3,2,1,0:T(8,128)(2,1)S(1)}, bf16[1,4,2,4,32,1024]{5,4,3,2,1,0:T(8,128)(2,1)}, u32[]{:S(2)}) copy-start(bf16[1,4,2,4,32,1024]{5,4,3,2,1,0:T(8,128)(2,1)} %copy-done.8) | copy-start | bytes 6291460
  603.5 2.1 copy-start.15
  603.5 4.4 copy-start.11
  603.5 4.4 copy-start.18
  605.6 5.0 copy-start.13
  605.7 5.0 copy-start.20
  605.7 5.0 copy-start.22
  605.7 5.0 copy-start.24
  605.7 5.0 copy-start.30
  610.7 7.7 copy-start.4
  618.4 5.3 copy-start.5
  618.4 3.7 copy-start.16
  623.7 76.2 %copy-start.28 = (bf16[2,512,1024]{2,1,0:T(8,128)(2,1)S(1)}, bf16[2,512,1024]{2,1,0:T(8,128)(2,1)}, u32[]{:S(2)}) copy-start(bf16[2,512,1024]{2,1,0:T(8,128)(2,1)} %x_ref.1) | copy-start | bytes 6291460
  780.3 5.3 copy-start.19
  842.3 10.1 %copy-start.6 = (f32[2,128,1024]{2,1,0:T(8,128)S(1)}, f32[2,128,1024]{2,1,0:T(8,128)}, u32[]{:S(2)}) copy-start(f32[2,128,1024]{2,1,0:T(8,128)} %copy-done.5) | copy-start | bytes 3145732
  852.3 14.5 %copy-start.7 = (f32[4,128,1024]{2,1,0:T(8,128)S(1)}, f32[4,128,1024]{2,1,0:T(8,128)}, u32[]{:S(2)}) copy-start(f32[4,128,1024]{2,1,0:T(8,128)} %param.18) | copy-start | bytes 6291460
  866.9 6.9 copy-start.25
  866.9 6.9 copy-start.26
  866.9 6.9 copy-start.27

commit v6 on v5

--- a/solution.py
+++ b/solution.py
@@ -67,11 +67,11 @@
     return block.reshape(block.shape[0] * block.shape[1], block.shape[2])
 
 
-def forward_body(step_rows, live_ref, q_ref, k_ref, v_ref, out_ref, lse_ref):
+def forward_body(step_rows, first_object, live_ref, q_ref, k_ref, v_ref, out_ref, lse_ref):
     key_groups, unused_one, key_rows, width = k_ref.shape
     heads = width // HD
     per_block = step_rows // key_rows
-    blocks = live_ref[pl.program_id(0)] // step_rows
+    blocks = live_ref[pl.program_id(0) + first_object] // step_rows
     queries = rows_of(q_ref, 0, q_ref.shape[0]) * jnp.bfloat16(0.125)
     result = jnp.zeros(queries.shape, jnp.float32)
     for head in range(heads):
@@ -101,18 +101,19 @@
     out_ref[...] = result.astype(jnp.bfloat16).reshape(out_ref.shape)
 
 
-def attend_forward(live, query_source, key_source, value_source, query_block, step_rows):
-    (q_array, q_at), (k_array, k_at), (v_array, v_at) = query_source, key_source, value_source
-    groups, unused_blocks, objects, q_rows, width = q_array.shape
+def attend_forward(live, query_source, key_source, value_source, query_block, step_rows, span):
+    (q_array, *q_at), (k_array, *k_at), (v_array, *v_at) = query_source, key_source, value_source
+    groups, unused_blocks, unused_objects, q_rows, width = q_array.shape
+    first_object, objects = span
     k_rows = k_array.shape[3]
     heads = width // HD
     total_q = groups * q_rows
     per_q = query_block // q_rows
     grid = (objects, total_q // query_block)
-    whole = lambda index: (lambda o, j, live: (0, index, o, 0, 0))
-    part = lambda index: (lambda o, j, live: (j, index, o, 0, 0))
+    whole = lambda at: (lambda o, j, live: (0, at[0], o + at[1], 0, 0))
+    part = lambda at: (lambda o, j, live: (j, at[0], o + at[1], 0, 0))
     return pl.pallas_call(
-        functools.partial(forward_body, step_rows),
+        functools.partial(forward_body, step_rows, first_object),
         grid_spec=pltpu.PrefetchScalarGridSpec(
             num_scalar_prefetch=1,
             grid=grid,
@@ -201,7 +202,7 @@
 
 
 def attend_backward(live, query_source, key_source, value_source, outs, lse, grads, step_rows, span):
-    (q_array, q_at), (k_array, k_at), (v_array, v_at) = query_source, key_source, value_source
+    (q_array, *q_at), (k_array, *k_at), (v_array, *v_at) = query_source, key_source, value_source
     groups, unused_blocks, unused_objects, q_rows, width = q_array.shape
     first_object, objects = span
     k_rows = k_array.shape[3]
@@ -209,9 +210,9 @@
     total_q = groups * q_rows
     per_k = max(step_rows // k_rows, 1)
     grid = (objects, groups // per_k)
-    whole = lambda index: (lambda o, j, live: (0, index, o + first_object, 0, 0))
-    part = lambda index: (lambda o, j, live: (j, index, o + first_object, 0, 0))
-    tokens = pl.BlockSpec((groups, 1, q_rows, width), lambda o, j, live: (0, o + first_object, 0, 0))
+    whole = lambda at: (lambda o, j, live: (0, at[0], o + at[1], 0, 0))
+    part = lambda at: (lambda o, j, live: (j, at[0], o + at[1], 0, 0))
+    tokens = pl.BlockSpec((groups, 1, q_rows, width), lambda o, j, live: (0, o, 0, 0))
     return pl.pallas_call(
         functools.partial(cross_backward_body, first_object),
         grid_spec=pltpu.PrefetchScalarGridSpec(
@@ -222,8 +223,8 @@
                 pl.BlockSpec((per_k, None, 1, k_rows, width), part(k_at)),
                 pl.BlockSpec((per_k, None, 1, k_rows, width), part(v_at)),
                 tokens,
-                pl.BlockSpec((1, heads, 1, total_q), lambda o, j, live: (o + first_object, 0, 0, 0)),
-                pl.BlockSpec((groups, None, 1, q_rows, width), whole(0)),
+                pl.BlockSpec((1, heads, 1, total_q), lambda o, j, live: (o, 0, 0, 0)),
+                pl.BlockSpec((groups, None, 1, q_rows, width), whole((0, first_object))),
             ],
             out_specs=[
                 pl.BlockSpec((groups, 1, q_rows, width), lambda o, j, live: (0, o, 0, 0)),
@@ -540,15 +541,17 @@
     )(index, narrow, mod_rows)
 
 
-def next_gather_body(tiles, start, zoned, kind, amount, ahead, source_ref, *refs):
-    mix_sources, refs = refs[:amount], refs[amount:]
+def next_gather_body(tiles, start, zoned, plans, ahead, source_ref, *refs):
+    mix_sources = []
+    for unused_kind, amount in plans:
+        mix_sources.append(refs[:amount])
+        refs = refs[amount:]
     out_ref, refs = refs[0], refs[1:]
-    if amount:
-        mixed_ref, refs = refs[0], refs[1:]
+    mixed_refs, refs = refs[: len(plans)], refs[len(plans) :]
     if ahead:
         zone_ref, refs = refs[0], refs[1:]
         zone_hold, zone_sems, refs = refs[0], refs[1], refs[2:]
-    full, load_sems, send_sems, recv_sems, out_sems = refs[:5]
+    (full, load_sems, send_sems, recv_sems, out_sems), refs = refs[:5], refs[5:]
     where = places()
     dp_index, fsdp_index, z_index, core = where
     loads = []
@@ -561,7 +564,7 @@
         loads.append(load)
     units = tiles * GATHER_PARTS
     peers = [dp_peer(dp_index, flip) for flip in (1, 2)]
-    if amount:
+    if plans:
         peers += fsdp_peers(fsdp_index)
     else:
         peers += [core_peer(fsdp_index)]
@@ -577,8 +580,11 @@
             loads[tile].wait()
             for unit in near:
                 z_copies[unit] = send_z(unit, part_of(full, unit, 2), fsdp_index, dp_index, z_index, (send_sems, recv_sems))
-    if amount:
-        moving = mix_begin(kind, mix_sources, mixed_ref, refs[5:], fsdp_index)
+    movings = []
+    for place, (kind, amount) in enumerate(plans):
+        mix_scratch, refs = refs[: 1 + amount], refs[1 + amount :]
+        movings.append(mix_begin(kind, mix_sources[place], mixed_refs[place], mix_scratch, fsdp_index))
+    for moving in movings:
         mix_own(moving)
     if ahead:
         later = source_ref.at[pl.ds(ahead[0], ahead[1])]
@@ -598,7 +604,7 @@
         for unit in range(units):
             for copy in z_copies[unit]:
                 copy.wait_send()
-    if amount:
+    for moving in movings:
         mix_end(moving)
     if ahead:
         for copy in zone:
@@ -606,10 +612,10 @@
         zone_store.wait()
 
 
-def next_gather(source, tiles, start, zoned, mix, ahead, collective):
+def next_gather(source, tiles, start, zoned, mixes, ahead, collective):
     rows, width = source.shape[-2:]
     bf = jnp.bfloat16
-    kind, mix_sources = mix if mix else (None, [])
+    operands = [source]
     out_shape = [jax.ShapeDtypeStruct((tiles, 4, 2, 4, rows, width), bf)]
     scratch = [
         pltpu.VMEM((tiles, 4, 4, rows, width), bf),
@@ -618,23 +624,24 @@
         pltpu.SemaphoreType.DMA((tiles * GATHER_PARTS, 10)),
         pltpu.SemaphoreType.DMA((tiles * GATHER_PARTS,)),
     ]
-    if mix:
+    for mix in mixes:
+        operands += list(mix[1])
         extra, result = mix_plan(mix)
         scratch, out_shape = scratch + extra, out_shape + [result]
+    plans = tuple((kind, len(sources)) for kind, sources in mixes)
     if ahead:
         scratch = [pltpu.VMEM((ahead[1], rows, width), bf), pltpu.SemaphoreType.DMA((2, 4))] + scratch
         out_shape = out_shape + [jax.ShapeDtypeStruct((4, ahead[1], rows, width), bf)]
     results = pl.pallas_call(
-        functools.partial(next_gather_body, tiles, start, zoned, kind, len(mix_sources), ahead),
-        in_specs=[ANY] * (1 + len(mix_sources)),
+        functools.partial(next_gather_body, tiles, start, zoned, plans, ahead),
+        in_specs=[ANY] * len(operands),
         out_specs=[ANY] * len(out_shape),
         scratch_shapes=scratch,
         out_shape=out_shape,
         compiler_params=comm_params(collective),
         cost_estimate=pl.CostEstimate(flops=0, bytes_accessed=tiles * 30_000_000, transcendentals=0),
-    )(source, *mix_sources)
-    mixed = results[1] if mix else None
-    return results[0].reshape(tiles, 32 * rows, width), mixed, (results[-1] if ahead else None)
+    )(*operands)
+    return [results[0].reshape(tiles, 32 * rows, width)] + list(results[1:])
 
 
 def fast_layout(master):
@@ -993,7 +1000,8 @@
 def weight_source(master, modulation, tile_slots):
     if not fast_layout(master):
         chunks, mod_all = fetch_generic(master, modulation, tile_slots)
-        return (lambda number, mix, *others: (chunks[number], mix_generic(mix))), mod_all
+        generic = lambda number, mixes, *others: [chunks[number]] + [mix_generic(mix) for mix in mixes]
+        return generic, mod_all
     slots_here, row_count, width = master.shape
     dp_index = lax.axis_index("dp")
     narrow = master.astype(jnp.bfloat16).reshape(slots_here, 4, row_count // 4, width)
@@ -1008,18 +1016,18 @@
 
     last_zone = []
 
-    def chunk(number, mix, *others):
+    def chunk(number, mixes, *others):
         tiles = len(CHUNKS[number])
         if number == 0:
-            return first.reshape(tiles, row_count * 8, width), None
+            return [first.reshape(tiles, row_count * 8, width)]
         if number < 3:
             held = after(zoned, *others) if others else zoned
-            return next_gather(held, tiles, (0, 3)[number - 1], True, mix, None, number)[:2]
+            return next_gather(held, tiles, (0, 3)[number - 1], True, mixes, None, number)
         if number == 3:
-            full, mixed, zone = next_gather(rest, tiles, 0, False, mix, (tiles, 16 - EARLY - tiles), number)
+            *results, zone = next_gather(rest, tiles, 0, False, mixes, (tiles, 16 - EARLY - tiles), number)
             last_zone.append(zone)
-            return full, mixed
-        return next_gather(last_zone[0], tiles, 0, True, mix, None, number)[:2]
+            return results
+        return next_gather(last_zone[0], tiles, 0, True, mixes, None, number)
 
     return chunk, mod_all
 
@@ -1032,8 +1040,8 @@
         out_ref[side, 0] = part.reshape(objects, rows, LANES)
 
 
-def project_pairs(tokens, tiles):
-    objects, rows, width = tokens.shape
+def project_pairs(tokens, objects, tiles):
+    unused_objects, rows, width = tokens.shape
     blocks = tiles.shape[0]
     return pl.pallas_call(
         pair_body,
@@ -1125,32 +1133,40 @@
         modulations[:, position * model_width : (position + 1) * model_width][:, None, :]
         for position in range(9)
     ]
-    tiles_pair, unused_mix = chunk(0, None)
+    half = objects // 2
+    (tiles_pair,) = chunk(0, [])
     if fast:
-        pair_sent = project_pairs(image_tokens, tiles_pair)
+        pair_sent = project_pairs(image_tokens, half, tiles_pair)
     else:
-        image_pairs = contract("oid,kde->koie", image_tokens, tiles_pair).astype(jnp.bfloat16)
+        image_pairs = contract("oid,kde->koie", image_tokens[:half], tiles_pair).astype(jnp.bfloat16)
         pair_sent = by_head(image_pairs, groups)
-    pair_heads = exchange(pair_sent)
-    tiles_qkv, unused_mix = chunk(1, None, pair_sent)
+    pair_early = exchange(pair_sent)
+    (tiles_qkv,) = chunk(1, [], pair_sent)
+    pairs_late = contract("oid,kde->koie", image_tokens[half:], tiles_pair).astype(jnp.bfloat16)
     residual_in = triplane.astype(jnp.float32)
     normed_one = modulate(residual_in, blocks[0], blocks[1]).astype(jnp.bfloat16)
     triples = contract("otd,kde->kote", normed_one, tiles_qkv).astype(jnp.bfloat16)
-    tiles_mixed, triple_heads = chunk(2, ("heads", [triples]))
+    tiles_mixed, triple_heads = chunk(2, [("heads", [triples])])
     tile_out_one, tile_query_two, tile_out_two = tiles_mixed[0], tiles_mixed[1], tiles_mixed[2]
     every_key = jnp.full((objects,), tri_total, jnp.int32)
-    self_sources = [(triple_heads, index) for index in range(3)]
-    self_result, self_logsum = attend_forward(every_key, *self_sources, tri_total, VIEW)
-    tiles_up, merged_one = chunk(3, ("tokens", [self_result]))
+    self_sources = [(triple_heads, index, 0) for index in range(3)]
+    self_result, self_logsum = attend_forward(every_key, *self_sources, tri_total, VIEW, (0, objects))
+    tiles_up, merged_one = chunk(3, [("tokens", [self_result])])
     merged_one = merged_one[0]
     branch_one = contract("otd,de->ote", merged_one, tile_out_one)
     residual_mid = residual_in + blocks[2] * branch_one
     normed_two = modulate(residual_mid, blocks[3], blocks[4]).astype(jnp.bfloat16)
     cross_query = contract("otd,de->ote", normed_two, tile_query_two).astype(jnp.bfloat16)
-    tiles_down, query_heads = chunk(4, ("heads", [cross_query[None]]))
-    cross_sources = [(query_heads, 0), (pair_heads, 0), (pair_heads, 1)]
-    cross_result, cross_logsum = attend_forward(view_tokens, *cross_sources, tri_total, VIEW)
-    cross_mix = ("tokens", [cross_result])
+    tiles_down, query_heads, pair_late = chunk(4, [("heads", [cross_query[None]]), ("heads", [pairs_late])])
+    cross_sources, cross_result, cross_logsum = [], [], []
+    for place in range(objects):
+        pair_heads, shift = (pair_early, place) if place < half else (pair_late, place - half)
+        sources = [(query_heads, 0, place), (pair_heads, 0, shift), (pair_heads, 1, shift)]
+        result, logsum = attend_forward(view_tokens, *sources, tri_total, VIEW, (place, 1))
+        cross_sources.append(sources)
+        cross_result.append(result)
+        cross_logsum.append(logsum)
+    cross_mix = ("objects", cross_result)
     merged_two = (mix_alone(cross_mix, 11) if fast else mix_generic(cross_mix))[0]
     branch_two = contract("otd,de->ote", merged_two, tile_out_two)
     residual_late = residual_mid + blocks[5] * branch_two
@@ -1180,11 +1196,10 @@
     grad_query_heads, grad_pair_heads = [], []
     for place in range(objects):
         query_part, pair_part = attend_backward(
-            view_tokens, *cross_sources, cross_result, cross_logsum, grad_cross_heads, VIEW, (place, 1)
+            view_tokens, *cross_sources[place], cross_result[place], cross_logsum[place], grad_cross_heads, VIEW, (place, 1)
         )
         grad_query_heads.append(query_part)
         grad_pair_heads.append(pair_part)
-    half = objects // 2
     pair_mixes = [("tokens", [part]) for part in grad_pair_heads]
     sums_up, grad_query_two, *grad_pairs = reduced(
         [grad_up], None, [("objects", grad_query_heads)] + pair_mixes[:half], 6

time: 890 us -> 881 us (0.990); the launches traced: 875 us -> 878 us
    pallas_call x6 -> x7, Pallas kernels: 263 us -> 250 us  [the longest x4 189 us: next_gather(): pl.pallas_call(functools.partial(next_gather_body, tiles, start, zoned, p...]
    dot_general x20 -> x21, matrix products: 90.4 us -> 93.7 us  [contract(): return jnp.einsum(form, left, right, preferred_element_type=jnp.float32)]
  transfers between devices with their start and end apart: 1 -> 1, of which waited for: 0 -> 0; matrix products, arithmetic and copies ran while one was open for 2% -> 3% of each run, Pallas kernels for 27% -> 26%
where the time goes in v6:
time: 881 us; the launch traced here: 878 us
  Pallas kernels  732 us (83%)
  matrix products  94.6 us (11%)
  local copies, waits for them, and re-layouts  22.7 us (3%)
  other arithmetic  17.6 us (2%)
  starting transfers between devices  9.38 us (1%)
    pallas_call x5, Pallas kernels, reduce_tiles(): pl.pallas_call(functools.partial(reduce_body, counts, mods is not None, p...  315 us
    pallas_call x4, Pallas kernels, next_gather(): pl.pallas_call(functools.partial(next_gather_body, tiles, start, zoned, p...  189 us
    dot_general x21, matrix products, contract(): return jnp.einsum(form, left, right, preferred_element_type=jnp.float32)  93.7 us
    pallas_call x3, Pallas kernels, attend_backward(): pl.pallas_call(functools.partial(cross_backward_body, first_object), grid...  63.6 us
    pallas_call x1, Pallas kernels, first_gather(): pl.pallas_call(functools.partial(first_gather_body, tiles, rows), grid_sp...  62.3 us
    pallas_call x3, Pallas kernels, attend_forward(): pl.pallas_call(functools.partial(forward_body, step_rows, first_object),...  60.8 us
    pallas_call x1, Pallas kernels, mix_alone(): pl.pallas_call(functools.partial(mix_body, kind, len(sources)), in_specs=...  19.4 us
  transfers between devices with their start and end apart: 1, of which 0 were waited for; matrix products, arithmetic and copies ran while one was open for 3% of the time, Pallas kernels for 26%

profile of v6, /device:TPU:0, one launch (start us, length us, event | category | flops | bytes accessed | tf_op | source)
XLA Modules:
  0.0 877.6 jit_solution(3368434042024413754)
XLA Ops:
  0.7 2.7 convert_element_type.116
  3.4 0.8 convert_element_type.117
  4.3 0.6 reshape.222.mod_ref
  4.9 0.7 pad_clamp_fusion
  5.6 0.7 fusion.53
  6.3 1.2 gather_fusion
  7.4 62.3 %shard_map.213 = (bf16[2,4,2,4,32,1024]{5,4,3,2,1,0:T(8,128)(2,1)}, bf16[4,2,4,16,1024]{4,3,2,1,0:T(8,128)(2,1)}, bf16[4,6,32,1024]{3,2,1,0:T(8,128)(2,1)}, bf16[8,32,1024]{2,1,0:T(8,128)(2,1)}) custom-call(s32[16]{0:T(128)} %gather_fusion, bf16[4,4,32,1024]{3,2,1,0:T(8,128)(2,1)} %bitcast.191, bf16[16,1024]{1,0:T(8,128)(2,1)} %reshape.222.mod_ref), custom_call_target="tpu_custom_call" | custom-call | bytes 200000000 | tf_op jit(solution)/shard_map/pallas_call | solution.py:512
  69.7 8.0 shard_map.214
  77.8 9.4 %all-to-all-start = ((bf16[8,2,1,512,128]{4,3,2,1,0:T(8,128)(2,1)}), bf16[8,2,1,512,128]{4,3,2,1,0:T(8,128)(2,1)}, u32[]{:S(2)}, u32[]{:S(2)}) async-start(bf16[8,2,1,512,128]{4,3,2,1,0:T(8,128)(2,1)} %shard_map.214), calls=%async_computation | async-start | bytes 4194304 | tf_op jit(solution)/shard_map/all_to_all | solution.py:1064
  87.2 0.8 reshape.223
  88.1 0.6 reshape.224
  89.6 32.5 %shard_map.215 = bf16[3,4,2,4,32,1024]{5,4,3,2,1,0:T(8,128)(2,1)} custom-call(bf16[4,6,32,1024]{3,2,1,0:T(8,128)(2,1)} %get-tuple-element.51.source_ref), custom_call_target="tpu_custom_call" | custom-call | bytes 90000000 | tf_op jit(solution)/shard_map/pallas_call | solution.py:635
  122.9 6.0 fusion.15.refs_0_
  128.9 37.0 %shard_map.216 = (bf16[3,4,2,4,32,1024]{5,4,3,2,1,0:T(8,128)(2,1)}, bf16[8,3,2,128,128]{4,3,2,1,0:T(8,128)(2,1)}) custom-call(bf16[4,6,32,1024]{3,2,1,0:T(8,128)(2,1)} %get-tuple-element.51.source_ref, bf16[3,2,128,1024]{3,2,1,0:T(8,128)(2,1)} %fusion.15.refs_0_), custom_call_target="tpu_custom_call" | custom-call | bytes 90000000 | tf_op jit(solution)/shard_map/pallas_call | solution.py:635
  166.0 0.7 gather_fusion.1
  167.2 25.4 %shard_map.217 = (bf16[8,2,128,128]{3,2,1,0:T(8,128)(2,1)}, f32[2,2,1,1024]{3,2,1,0:T(1,128)}) custom-call(s32[2]{0:T(128)} %broadcast_31_live_ref.2.live_ref, bf16[8,3,2,128,128]{4,3,2,1,0:T(8,128)(2,1)} %get-tuple-element.52.q_ref.k_ref.v_ref, bf16[8,3,2,128,128]{4,3,2,1,0:T(8,128)(2,1)} %get-tuple-element.52.q_ref.k_ref.v_ref, ...), custom_call_target="tpu_custom_call" | custom-call | flops 1073741824 | bytes 2097152 | tf_op jit(solution)/shard_map/pallas_call | solution.py:115
  192.7 60.0 %shard_map.218 = (bf16[4,4,2,4,32,1024]{5,4,3,2,1,0:T(8,128)(2,1)}, bf16[1,2,128,1024]{3,2,1,0:T(8,128)(2,1)}, bf16[4,4,32,1024]{3,2,1,0:T(8,128)(2,1)}) custom-call(bf16[8,32,1024]{2,1,0:T(8,128)(2,1)} %get-tuple-element.48.source_ref, bf16[8,2,128,128]{3,2,1,0:T(8,128)(2,1)} %get-tuple-element.53.refs_0_.out_ref), custom_call_target="tpu_custom_call" | custom-call | bytes 120000000 | tf_op jit(solution)/shard_map/pallas_call | solution.py:635
  252.6 5.6 fusion.66
  258.2 1.7 fusion.65
  260.2 1.6 fusion.16.refs_0_
  262.4 0.7 copy-done.18
  263.1 3.7 convert_bitcast_fusion.refs_1_
  266.8 59.7 %shard_map.219 = (bf16[4,4,2,4,32,1024]{5,4,3,2,1,0:T(8,128)(2,1)}, bf16[8,1,2,128,128]{4,3,2,1,0:T(8,128)(2,1)}, bf16[8,2,1,512,128]{4,3,2,1,0:T(8,128)(2,1)}) custom-call(bf16[4,4,32,1024]{3,2,1,0:T(8,128)(2,1)} %get-tuple-element.56.source_ref, bf16[1,2,128,1024]{3,2,1,0:T(8,128)(2,1)} %fusion.16.refs_0_, ...), custom_call_target="tpu_custom_call" | custom-call | bytes 120000000 | tf_op jit(solution)/shard_map/pallas_call | solution.py:635
  326.5 0.7 select_reduce_fusion.index_ref
  327.2 15.8 %shard_map.221 = (bf16[8,1,128,128]{3,2,1,0:T(8,128)(2,1)}, f32[1,2,1,1024]{3,2,1,0:T(1,128)}) custom-call(s32[2]{0:T(128)} %live_ref.7, bf16[8,1,2,128,128]{4,3,2,1,0:T(8,128)(2,1)} %get-tuple-element.57.q_ref, bf16[8,2,1,512,128]{4,3,2,1,0:T(8,128)(2,1)} %get-tuple-element.59.k_ref.v_ref, bf16[8,2,1,512,128]{4,3,2,1,0:T(8,128)(2,1)} %get-tuple-element.59.k_ref.v_ref), custom_call_target="tpu_custom_call" | custom-call | flops 2147483648 | bytes 2621440 | tf_op jit(solution)/shard_map/pallas_call | solution.py:115
  343.0 19.6 %shard_map.220 = (bf16[8,1,128,128]{3,2,1,0:T(8,128)(2,1)}, f32[1,2,1,1024]{3,2,1,0:T(1,128)}) custom-call(s32[2]{0:T(128)} %live_ref.7, bf16[8,1,2,128,128]{4,3,2,1,0:T(8,128)(2,1)} %get-tuple-element.57.q_ref, bf16[8,2,1,512,128]{4,3,2,1,0:T(8,128)(2,1)} %all-to-all-done.k_ref.v_ref, bf16[8,2,1,512,128]{4,3,2,1,0:T(8,128)(2,1)} %all-to-all-done.k_ref.v_ref), custom_call_target="tpu_custom_call" | custom-call | flops 2147483648 | bytes 2621440 | tf_op jit(solution)/shard_map/pallas_call | solution.py:115
  362.6 19.4 %shard_map.222 = bf16[1,2,128,1024]{3,2,1,0:T(8,128)(2,1)} custom-call(bf16[8,1,128,128]{3,2,1,0:T(8,128)(2,1)} %get-tuple-element.58.refs_0_.out_ref, bf16[8,1,128,128]{3,2,1,0:T(8,128)(2,1)} %get-tuple-element.60.refs_1_.out_ref), custom_call_target="tpu_custom_call" | custom-call | bytes 30000000 | tf_op jit(solution)/shard_map/pallas_call | solution.py:371
  382.1 3.5 fusion.64
  385.8 6.0 fusion.58
  391.9 6.1 bitcast_convert_fusion
  397.9 4.9 fusion.8
  402.9 6.3 multiply_reduce_fusion
  409.2 6.1 bitcast_convert_fusion.1
  415.7 1.0 copy-done.13
  417.2 1.5 fusion.17.refs_1_
  418.8 52.1 %shard_map.223 = (bf16[8,16,1024]{2,1,0:T(8,128)(2,1)}, bf16[8,1,2,128,128]{4,3,2,1,0:T(8,128)(2,1)}) custom-call(bf16[4,4,2,4,32,1024]{5,4,3,2,1,0:T(8,128)(2,1)} %bitcast.181, bf16[1,2,128,1024]{3,2,1,0:T(8,128)(2,1)} %fusion.17.refs_1_), custom_call_target="tpu_custom_call" | custom-call | bytes 160000000 | tf_op jit(solution)/shard_map/pallas_call | solution.py:909
  470.8 21.2 %shard_map.225 = (bf16[8,1,128,128]{3,2,1,0:T(8,128)(2,1)}, bf16[8,2,1,512,128]{4,3,2,1,0:T(8,128)(2,1)}) custom-call(s32[2]{0:T(128)} %live_ref.7, bf16[8,1,2,128,128]{4,3,2,1,0:T(8,128)(2,1)} %get-tuple-element.57.q_ref, bf16[8,2,1,512,128]{4,3,2,1,0:T(8,128)(2,1)} %get-tuple-element.59.k_ref.v_ref, ...), custom_call_target="tpu_custom_call" | custom-call | flops 5368709120 | bytes 5242880 | tf_op jit(solution)/shard_map/pallas_call | solution.py:216
  492.0 26.7 %shard_map.224 = (bf16[8,1,128,128]{3,2,1,0:T(8,128)(2,1)}, bf16[8,2,1,512,128]{4,3,2,1,0:T(8,128)(2,1)}) custom-call(s32[2]{0:T(128)} %live_ref.7, bf16[8,1,2,128,128]{4,3,2,1,0:T(8,128)(2,1)} %get-tuple-element.57.q_ref, bf16[8,2,1,512,128]{4,3,2,1,0:T(8,128)(2,1)} %all-to-all-done.k_ref.v_ref, bf16[8,2,1,512,128]{4,3,2,1,0:T(8,128)(2,1)} %all-to-all-done.k_ref.v_ref, ...), custom_call_target="tpu_custom_call" | custom-call | flops 5368709120 | bytes 5242880 | tf_op jit(solution)/shard_map/pallas_call | solution.py:216
  518.7 87.4 %shard_map.226 = (bf16[4,32,1024]{2,1,0:T(8,128)(2,1)}, bf16[1,2,128,1024]{3,2,1,0:T(8,128)(2,1)}, bf16[2,1,512,1024]{3,2,1,0:T(8,128)(2,1)}) custom-call(bf16[4,4,2,4,32,1024]{5,4,3,2,1,0:T(8,128)(2,1)} %bitcast.177, bf16[8,1,128,128]{3,2,1,0:T(8,128)(2,1)} %get-tuple-element.65.refs_1_, bf16[8,1,128,128]{3,2,1,0:T(8,128)(2,1)} %get-tuple-element.67.refs_2_, ...), custom_call_target="tpu_custom_call" | custom-call | bytes 80000000 | tf_op jit(solution)/shard_map/pallas_call | solution.py:909
  606.1 2.1 multiply_reduce_fusion.4
  608.3 2.2 bitcast_convert_fusion.5
  610.5 2.1 bitcast_convert_fusion.6
  613.3 7.7 fusion.27
  621.0 1.5 fusion.18.refs_2_
  622.6 2.1 bitcast_convert_fusion.4
  624.7 1.6 constant_dynamic-update-slice_fusion.1
  626.3 73.5 %shard_map.227 = (bf16[2,32,1024]{2,1,0:T(8,128)(2,1)}, bf16[8,1,2,128,128]{4,3,2,1,0:T(8,128)(2,1)}, bf16[2,1,512,1024]{3,2,1,0:T(8,128)(2,1)}) custom-call(bf16[1,4,2,4,32,1024]{5,4,3,2,1,0:T(8,128)(2,1)} %bitcast.183, bf16[1,4,2,4,32,1024]{5,4,3,2,1,0:T(8,128)(2,1)} %bitcast.182, bf16[1,2,128,1024]{3,2,1,0:T(8,128)(2,1)} %fusion.18.refs_2_, ...), custom_call_target="tpu_custom_call" | custom-call | bytes 40000000 | tf_op jit(solution)/shard_map/pallas_call | solution.py:909
  699.8 3.1 constant_dynamic-update-slice_fusion
  702.8 8.4 bitcast_convert_fusion.3
  711.2 15.8 %shard_map.228 = (bf16[8,2,128,128]{3,2,1,0:T(8,128)(2,1)}, bf16[8,2,2,128,128]{4,3,2,1,0:T(8,128)(2,1)}) custom-call(s32[2]{0:T(128)} %broadcast_31_live_ref.2.live_ref, bf16[8,3,2,128,128]{4,3,2,1,0:T(8,128)(2,1)} %get-tuple-element.52.q_ref.k_ref.v_ref, bf16[8,3,2,128,128]{4,3,2,1,0:T(8,128)(2,1)} %get-tuple-element.52.q_ref.k_ref.v_ref, ...), custom_call_target="tpu_custom_call" | custom-call | flops 2684354560 | bytes 4194304 | tf_op jit(solution)/shard_map/pallas_call | solution.py:216
  727.0 55.8 %shard_map.229 = (bf16[3,32,1024]{2,1,0:T(8,128)(2,1)}, bf16[3,2,128,1024]{3,2,1,0:T(8,128)(2,1)}) custom-call(bf16[2,4,2,4,32,1024]{5,4,3,2,1,0:T(8,128)(2,1)} %bitcast.195, bf16[1,4,2,4,32,1024]{5,4,3,2,1,0:T(8,128)(2,1)} %bitcast.184, bf16[8,2,128,128]{3,2,1,0:T(8,128)(2,1)} %get-tuple-element.75.refs_2_, ...), custom_call_target="tpu_custom_call" | custom-call | bytes 60000000 | tf_op jit(solution)/shard_map/pallas_call | solution.py:909
  782.8 5.3 fusion.25
  788.2 4.7 bitcast_convert_fusion.2
  792.9 0.6 fusion.23
  793.6 0.7 fusion
  794.3 0.7 concatenate.17
  796.3 1.6 reshape.238.refs_1_
  797.9 46.2 %shard_map.230 = (bf16[6,16,1024]{2,1,0:T(8,128)(2,1)}, bf16[1,16,1024]{2,1,0:T(8,128)(2,1)}) custom-call(bf16[3,4,2,4,32,1024]{5,4,3,2,1,0:T(8,128)(2,1)} %bitcast.178, bf16[1,4,2,4,16,1024]{5,4,3,2,1,0:T(8,128)(2,1)} %reshape.238.refs_1_), custom_call_target="tpu_custom_call" | custom-call | bytes 120000000 | tf_op jit(solution)/shard_map/pallas_call | solution.py:909
  844.1 0.8 copy.112
  844.9 10.1 %convolution_bitcast_fusion = f32[2,512,1024]{2,1,0:T(8,128)} fusion(bf16[2,2,512,1024]{3,2,1,0:T(8,128)(2,1)} %constant_dynamic-update-slice_fusion, bf16[2,1024,1024,1]{2,1,3,0:T(8,128)(2,1)} %bitcast.193), kind=kOutput, calls=%fused_computation.25 | convolution fusion | flops 4294967296 | bytes 12582912 | tf_op jit(solution)/shard_map/koie,kde->oid/dot_general | solution.py:27
  855.0 1.4 add_add_fusion.3
  856.4 13.4 %shard_map.231 = bf16[4,4,32,1024]{3,2,1,0:T(8,128)(2,1)} custom-call(s32[16]{0:T(128)} %select_reduce_fusion.index_ref, bf16[3,32,1024]{2,1,0:T(8,128)(2,1)} %bitcast.199, bf16[3,32,1024]{2,1,0:T(8,128)(2,1)} %get-tuple-element.79.refs_1_, bf16[2,32,1024]{2,1,0:T(8,128)(2,1)} %get-tuple-element.80.refs_2_, bf16[4,32,1024]{2,1,0:T(8,128)(2,1)} %get-tuple-element.81.refs_3_, ...), custom_call_target="tpu_custom_call" | custom-call | bytes 50000000 | tf_op jit(solution)/shard_map/pallas_call | solution.py:961
  869.9 6.9 fusion.61
  876.7 0.7 multiply_subtract_fusion.1
  (119 shorter events, 6.7 us)
Async XLA Ops:
  0.6 122.0 %copy-start = (f32[2,16]{1,0:T(2,128)S(1)}, f32[2,16]{1,0:T(2,128)}, u32[]{:S(2)}) copy-start(f32[2,16]{1,0:T(2,128)} %param.16) | copy-start | bytes 388
  77.8 9.4 %copy-start.24 = (bf16[4,2,4,16,1024]{4,3,2,1,0:T(8,128)(2,1)S(1)}, bf16[4,2,4,16,1024]{4,3,2,1,0:T(8,128)(2,1)}, u32[]{:S(2)}) copy-start(bf16[4,2,4,16,1024]{4,3,2,1,0:T(8,128)(2,1)} %get-tuple-element.47) | copy-start | bytes 3145732
  77.8 265.2 %all-to-all-start = ((bf16[8,2,1,512,128]{4,3,2,1,0:T(8,128)(2,1)}), bf16[8,2,1,512,128]{4,3,2,1,0:T(8,128)(2,1)}, u32[]{:S(2)}, u32[]{:S(2)}) async-start(bf16[8,2,1,512,128]{4,3,2,1,0:T(8,128)(2,1)} %shard_map.214), calls=%async_computation | async-start | bytes 4194304 | tf_op jit(solution)/shard_map/all_to_all | solution.py:1064
  89.0 33.1 %copy-start.2 = (bf16[2,128,1024]{2,1,0:T(8,128)(2,1)S(1)}, bf16[2,128,1024]{2,1,0:T(8,128)(2,1)}, u32[]{:S(2)}) copy-start(bf16[2,128,1024]{2,1,0:T(8,128)(2,1)} %param.14) | copy-start | bytes 1572868
  122.9 43.0 %copy-start.1 = (s32[16]{0:T(128)S(1)}, s32[16]{0:T(128)}, u32[]{:S(2)}) copy-start(s32[16]{0:T(128)} %param.21) | copy-start | bytes 196
  252.6 5.6 copy-start.15
  258.2 3.6 copy-start.3
  258.2 3.6 copy-start.8
  258.2 4.2 copy-start.12
  258.2 4.9 copy-start.18
  385.5 12.4 %slice-start = ((s8[8388608]{0:T(1024)(128)(4,1)}), s8[4194304]{0:T(1024)(128)(4,1)S(1)}, s32[]{:S(2)}) async-start(s8[8388608]{0:T(1024)(128)(4,1)} %bitcast.203), calls=%async_computation.1 | async-start | bytes 8388608
  385.8 6.0 copy-start.26
  385.8 12.1 %slice-start.1 = ((s8[8388608]{0:T(1024)(128)(4,1)}), s8[4194304]{0:T(1024)(128)(4,1)S(1)}, s32[]{:S(2)}) async-start(s8[8388608]{0:T(1024)(128)(4,1)} %bitcast.203), calls=%async_computation.2 | async-start | bytes 8388608
  391.8 6.1 copy-start.31
  415.3 2.0 copy-start.10
  415.7 1.0 copy-start.13
  417.2 1.5 copy-start.20
  518.7 87.4 %copy-start.9 = (bf16[1,4,2,4,32,1024]{5,4,3,2,1,0:T(8,128)(2,1)S(1)}, bf16[1,4,2,4,32,1024]{5,4,3,2,1,0:T(8,128)(2,1)}, u32[]{:S(2)}) copy-start(bf16[1,4,2,4,32,1024]{5,4,3,2,1,0:T(8,128)(2,1)} %copy-done.8) | copy-start | bytes 6291460
  606.1 2.1 copy-start.16
  606.1 4.4 copy-start.11
  606.1 4.4 copy-start.21
  608.2 5.0 copy-start.14
  608.2 5.0 copy-start.23
  608.2 5.0 copy-start.25
  608.3 5.0 copy-start.27
  608.3 5.0 copy-start.32
  613.3 7.7 copy-start.4
  621.0 5.3 copy-start.5
  621.0 3.7 copy-start.17
  626.3 76.5 %copy-start.19 = (bf16[2,512,1024]{2,1,0:T(8,128)(2,1)S(1)}, bf16[2,512,1024]{2,1,0:T(8,128)(2,1)}, u32[]{:S(2)}) copy-start(bf16[2,512,1024]{2,1,0:T(8,128)(2,1)} %x_ref.1) | copy-start | bytes 6291460
  782.8 5.3 copy-start.22
  844.9 10.1 %copy-start.6 = (f32[2,128,1024]{2,1,0:T(8,128)S(1)}, f32[2,128,1024]{2,1,0:T(8,128)}, u32[]{:S(2)}) copy-start(f32[2,128,1024]{2,1,0:T(8,128)} %copy-done.5) | copy-start | bytes 3145732
  855.0 14.8 %copy-start.7 = (f32[4,128,1024]{2,1,0:T(8,128)S(1)}, f32[4,128,1024]{2,1,0:T(8,128)}, u32[]{:S(2)}) copy-start(f32[4,128,1024]{2,1,0:T(8,128)} %param.18) | copy-start | bytes 6291460
  869.8 6.9 copy-start.28
  869.9 6.9 copy-start.29
  869.9 6.9 copy-start.30

commit v7 on v6

--- a/solution.py
+++ b/solution.py
@@ -503,6 +503,16 @@
     return pltpu.CompilerParams(
         collective_id=collective, has_side_effects=True, vmem_limit_bytes=58 * 1024 * 1024
     )
+
+
+def reorder(values, order):
+    runs = []
+    for spot in order:
+        if runs and runs[-1][1] == spot:
+            runs[-1][1] = spot + 1
+        else:
+            runs.append([spot, spot + 1])
+    return jnp.concatenate([values[start:end] for start, end in runs])
 
 
 def first_gather(narrow, mod_rows, index):
@@ -954,7 +964,7 @@
     dp_index = lax.axis_index("dp")
     spots = jnp.arange(16, dtype=jnp.int32)
     wanted = ((spots // 4) ^ dp_index) * 4 + spots % 4
-    slots = tile_slots[jnp.array(order, jnp.int32)]
+    slots = reorder(tile_slots, order)
     matches = slots[None, :] == wanted[:, None]
     index = jnp.sum(jnp.where(matches, spots[None, :], 0), axis=1).astype(jnp.int32)
     bf = jnp.bfloat16
@@ -1006,7 +1016,7 @@
     dp_index = lax.axis_index("dp")
     narrow = master.astype(jnp.bfloat16).reshape(slots_here, 4, row_count // 4, width)
     index = ((tile_slots // slots_here) ^ dp_index) * slots_here + tile_slots % slots_here
-    index = index[jnp.array([tile for chunk in CHUNKS for tile in chunk], jnp.int32)]
+    index = reorder(index, [tile for chunk in CHUNKS for tile in chunk])
     mod_rows, mod_columns = modulation.shape
     mod_flat = modulation.astype(jnp.bfloat16).reshape(-1)
     mod_flat = jnp.pad(mod_flat, (0, MOD_ROWS * width - mod_flat.shape[0])).reshape(MOD_ROWS, width)

time: 881 us -> 867 us (0.984)
  Pallas kernels: 732 us -> 712 us
    pallas_call x5, Pallas kernels: 315 us -> 304 us  [reduce_tiles(): pl.pallas_call(functools.partial(reduce_body, counts, mods is not None, p...]
  transfers between devices with their start and end apart: 1 -> 1, of which waited for: 0 -> 0; matrix products, arithmetic and copies ran while one was open for 3% -> 3% of each run, Pallas kernels for 26% -> 27%
where the time goes in v7:
time: 867 us; the launch traced here: 859 us
  Pallas kernels  712 us (82%)
  matrix products  94.5 us (11%)
  local copies, waits for them, and re-layouts  23.7 us (3%)
  other arithmetic  17.6 us (2%)
  starting transfers between devices  9.38 us (1%)
    pallas_call x5, Pallas kernels, reduce_tiles(): pl.pallas_call(functools.partial(reduce_body, counts, mods is not None, p...  304 us
    pallas_call x4, Pallas kernels, next_gather(): pl.pallas_call(functools.partial(next_gather_body, tiles, start, zoned, p...  189 us
    dot_general x21, matrix products, contract(): return jnp.einsum(form, left, right, preferred_element_type=jnp.float32)  93.6 us
    pallas_call x1, Pallas kernels, first_gather(): pl.pallas_call(functools.partial(first_gather_body, tiles, rows), grid_sp...  62.3 us
    pallas_call x3, Pallas kernels, attend_backward(): pl.pallas_call(functools.partial(cross_backward_body, first_object), grid...  57.9 us
    pallas_call x3, Pallas kernels, attend_forward(): pl.pallas_call(functools.partial(forward_body, step_rows, first_object),...  57 us
    pallas_call x1, Pallas kernels, mix_alone(): pl.pallas_call(functools.partial(mix_body, kind, len(sources)), in_specs=...  19.4 us
  transfers between devices with their start and end apart: 1, of which 0 were waited for; matrix products, arithmetic and copies ran while one was open for 3% of the time, Pallas kernels for 27%

profile of v7, /device:TPU:0, one launch (start us, length us, event | category | flops | bytes accessed | tf_op | source)
XLA Modules:
  0.0 858.8 jit_solution(4755520124157856803)
XLA Ops:
  0.7 0.7 fusion.53
  1.5 2.7 convert_element_type.116
  4.2 0.8 convert_element_type.117
  5.1 0.6 reshape.222.mod_ref
  6.3 62.3 %shard_map.195 = (bf16[2,4,2,4,32,1024]{5,4,3,2,1,0:T(8,128)(2,1)}, bf16[4,2,4,16,1024]{4,3,2,1,0:T(8,128)(2,1)}, bf16[4,6,32,1024]{3,2,1,0:T(8,128)(2,1)}, bf16[8,32,1024]{2,1,0:T(8,128)(2,1)}) custom-call(s32[16]{0:T(128)} %pad_add_fusion.index_ref, bf16[4,4,32,1024]{3,2,1,0:T(8,128)(2,1)} %bitcast.193, bf16[16,1024]{1,0:T(8,128)(2,1)} %reshape.222.mod_ref), custom_call_target="tpu_custom_call" | custom-call | bytes 200000000 | tf_op jit(solution)/shard_map/pallas_call | solution.py:522
  68.6 8.0 shard_map.196
  76.7 9.4 %all-to-all-start = ((bf16[8,2,1,512,128]{4,3,2,1,0:T(8,128)(2,1)}), bf16[8,2,1,512,128]{4,3,2,1,0:T(8,128)(2,1)}, u32[]{:S(2)}, u32[]{:S(2)}) async-start(bf16[8,2,1,512,128]{4,3,2,1,0:T(8,128)(2,1)} %shard_map.196), calls=%async_computation | async-start | bytes 4194304 | tf_op jit(solution)/shard_map/all_to_all | solution.py:1074
  86.1 0.8 reshape.223
  87.1 0.6 reshape.224
  89.5 32.5 %shard_map.197 = bf16[3,4,2,4,32,1024]{5,4,3,2,1,0:T(8,128)(2,1)} custom-call(bf16[4,6,32,1024]{3,2,1,0:T(8,128)(2,1)} %get-tuple-element.51.source_ref), custom_call_target="tpu_custom_call" | custom-call | bytes 90000000 | tf_op jit(solution)/shard_map/pallas_call | solution.py:645
  122.0 6.0 fusion.15.refs_0_
  128.0 36.9 %shard_map.198 = (bf16[3,4,2,4,32,1024]{5,4,3,2,1,0:T(8,128)(2,1)}, bf16[8,3,2,128,128]{4,3,2,1,0:T(8,128)(2,1)}) custom-call(bf16[4,6,32,1024]{3,2,1,0:T(8,128)(2,1)} %get-tuple-element.51.source_ref, bf16[3,2,128,1024]{3,2,1,0:T(8,128)(2,1)} %fusion.15.refs_0_), custom_call_target="tpu_custom_call" | custom-call | bytes 90000000 | tf_op jit(solution)/shard_map/pallas_call | solution.py:645
  165.4 25.4 %shard_map.199 = (bf16[8,2,128,128]{3,2,1,0:T(8,128)(2,1)}, f32[2,2,1,1024]{3,2,1,0:T(1,128)}) custom-call(s32[2]{0:T(128)} %broadcast_29_live_ref.2.live_ref, bf16[8,3,2,128,128]{4,3,2,1,0:T(8,128)(2,1)} %get-tuple-element.52.q_ref.k_ref.v_ref, bf16[8,3,2,128,128]{4,3,2,1,0:T(8,128)(2,1)} %get-tuple-element.52.q_ref.k_ref.v_ref, ...), custom_call_target="tpu_custom_call" | custom-call | flops 1073741824 | bytes 2097152 | tf_op jit(solution)/shard_map/pallas_call | solution.py:115
  190.9 60.0 %shard_map.200 = (bf16[4,4,2,4,32,1024]{5,4,3,2,1,0:T(8,128)(2,1)}, bf16[1,2,128,1024]{3,2,1,0:T(8,128)(2,1)}, bf16[4,4,32,1024]{3,2,1,0:T(8,128)(2,1)}) custom-call(bf16[8,32,1024]{2,1,0:T(8,128)(2,1)} %get-tuple-element.48.source_ref, bf16[8,2,128,128]{3,2,1,0:T(8,128)(2,1)} %get-tuple-element.53.refs_0_.out_ref), custom_call_target="tpu_custom_call" | custom-call | bytes 120000000 | tf_op jit(solution)/shard_map/pallas_call | solution.py:645
  250.9 5.6 fusion.66
  256.5 1.7 fusion.65
  258.5 1.6 fusion.16.refs_0_
  260.1 0.6 copy-done.11
  260.7 0.7 copy-done.17
  261.4 3.7 convert_bitcast_fusion.refs_1_
  265.0 59.7 %shard_map.201 = (bf16[4,4,2,4,32,1024]{5,4,3,2,1,0:T(8,128)(2,1)}, bf16[8,1,2,128,128]{4,3,2,1,0:T(8,128)(2,1)}, bf16[8,2,1,512,128]{4,3,2,1,0:T(8,128)(2,1)}) custom-call(bf16[4,4,32,1024]{3,2,1,0:T(8,128)(2,1)} %get-tuple-element.56.source_ref, bf16[1,2,128,1024]{3,2,1,0:T(8,128)(2,1)} %fusion.16.refs_0_, ...), custom_call_target="tpu_custom_call" | custom-call | bytes 120000000 | tf_op jit(solution)/shard_map/pallas_call | solution.py:645
  325.3 2.0 concatenate.23
  327.3 0.7 select_reduce_fusion.index_ref
  328.1 15.8 %shard_map.203 = (bf16[8,1,128,128]{3,2,1,0:T(8,128)(2,1)}, f32[1,2,1,1024]{3,2,1,0:T(1,128)}) custom-call(s32[2]{0:T(128)} %live_ref.7, bf16[8,1,2,128,128]{4,3,2,1,0:T(8,128)(2,1)} %get-tuple-element.57.q_ref, bf16[8,2,1,512,128]{4,3,2,1,0:T(8,128)(2,1)} %get-tuple-element.59.k_ref.v_ref, bf16[8,2,1,512,128]{4,3,2,1,0:T(8,128)(2,1)} %get-tuple-element.59.k_ref.v_ref), custom_call_target="tpu_custom_call" | custom-call | flops 2147483648 | bytes 2621440 | tf_op jit(solution)/shard_map/pallas_call | solution.py:115
  343.8 15.8 %shard_map.202 = (bf16[8,1,128,128]{3,2,1,0:T(8,128)(2,1)}, f32[1,2,1,1024]{3,2,1,0:T(1,128)}) custom-call(s32[2]{0:T(128)} %live_ref.7, bf16[8,1,2,128,128]{4,3,2,1,0:T(8,128)(2,1)} %get-tuple-element.57.q_ref, bf16[8,2,1,512,128]{4,3,2,1,0:T(8,128)(2,1)} %all-to-all-done.k_ref.v_ref, bf16[8,2,1,512,128]{4,3,2,1,0:T(8,128)(2,1)} %all-to-all-done.k_ref.v_ref), custom_call_target="tpu_custom_call" | custom-call | flops 2147483648 | bytes 2621440 | tf_op jit(solution)/shard_map/pallas_call | solution.py:115
  359.6 19.4 %shard_map.204 = bf16[1,2,128,1024]{3,2,1,0:T(8,128)(2,1)} custom-call(bf16[8,1,128,128]{3,2,1,0:T(8,128)(2,1)} %get-tuple-element.58.refs_0_.out_ref, bf16[8,1,128,128]{3,2,1,0:T(8,128)(2,1)} %get-tuple-element.60.refs_1_.out_ref), custom_call_target="tpu_custom_call" | custom-call | bytes 30000000 | tf_op jit(solution)/shard_map/pallas_call | solution.py:371
  379.1 3.5 fusion.64
  382.8 6.0 fusion.58
  388.9 6.1 bitcast_convert_fusion
  395.0 4.8 fusion.8
  399.8 6.3 multiply_reduce_fusion
  406.1 6.1 bitcast_convert_fusion.1
  412.6 1.0 copy-done.12
  414.1 1.5 fusion.17.refs_1_
  415.7 47.9 %shard_map.205 = (bf16[8,16,1024]{2,1,0:T(8,128)(2,1)}, bf16[8,1,2,128,128]{4,3,2,1,0:T(8,128)(2,1)}) custom-call(bf16[4,4,2,4,32,1024]{5,4,3,2,1,0:T(8,128)(2,1)} %bitcast.183, bf16[1,2,128,1024]{3,2,1,0:T(8,128)(2,1)} %fusion.17.refs_1_), custom_call_target="tpu_custom_call" | custom-call | bytes 160000000 | tf_op jit(solution)/shard_map/pallas_call | solution.py:919
  463.6 21.1 %shard_map.207 = (bf16[8,1,128,128]{3,2,1,0:T(8,128)(2,1)}, bf16[8,2,1,512,128]{4,3,2,1,0:T(8,128)(2,1)}) custom-call(s32[2]{0:T(128)} %live_ref.7, bf16[8,1,2,128,128]{4,3,2,1,0:T(8,128)(2,1)} %get-tuple-element.57.q_ref, bf16[8,2,1,512,128]{4,3,2,1,0:T(8,128)(2,1)} %get-tuple-element.59.k_ref.v_ref, ...), custom_call_target="tpu_custom_call" | custom-call | flops 5368709120 | bytes 5242880 | tf_op jit(solution)/shard_map/pallas_call | solution.py:216
  484.8 21.0 %shard_map.206 = (bf16[8,1,128,128]{3,2,1,0:T(8,128)(2,1)}, bf16[8,2,1,512,128]{4,3,2,1,0:T(8,128)(2,1)}) custom-call(s32[2]{0:T(128)} %live_ref.7, bf16[8,1,2,128,128]{4,3,2,1,0:T(8,128)(2,1)} %get-tuple-element.57.q_ref, bf16[8,2,1,512,128]{4,3,2,1,0:T(8,128)(2,1)} %all-to-all-done.k_ref.v_ref, bf16[8,2,1,512,128]{4,3,2,1,0:T(8,128)(2,1)} %all-to-all-done.k_ref.v_ref, ...), custom_call_target="tpu_custom_call" | custom-call | flops 5368709120 | bytes 5242880 | tf_op jit(solution)/shard_map/pallas_call | solution.py:216
  505.7 84.1 %shard_map.208 = (bf16[4,32,1024]{2,1,0:T(8,128)(2,1)}, bf16[1,2,128,1024]{3,2,1,0:T(8,128)(2,1)}, bf16[2,1,512,1024]{3,2,1,0:T(8,128)(2,1)}) custom-call(bf16[4,4,2,4,32,1024]{5,4,3,2,1,0:T(8,128)(2,1)} %bitcast.179, bf16[8,1,128,128]{3,2,1,0:T(8,128)(2,1)} %get-tuple-element.65.refs_1_, bf16[8,1,128,128]{3,2,1,0:T(8,128)(2,1)} %get-tuple-element.67.refs_2_, ...), custom_call_target="tpu_custom_call" | custom-call | bytes 80000000 | tf_op jit(solution)/shard_map/pallas_call | solution.py:919
  589.9 2.1 multiply_reduce_fusion.4
  592.0 2.2 bitcast_convert_fusion.5
  594.3 2.1 bitcast_convert_fusion.6
  596.4 0.6 multiply_reduce_fusion.2
  597.0 7.7 fusion.27
  604.8 1.5 fusion.18.refs_2_
  606.3 2.1 bitcast_convert_fusion.4
  608.4 1.6 constant_dynamic-update-slice_fusion.1
  610.0 72.5 %shard_map.209 = (bf16[2,32,1024]{2,1,0:T(8,128)(2,1)}, bf16[8,1,2,128,128]{4,3,2,1,0:T(8,128)(2,1)}, bf16[2,1,512,1024]{3,2,1,0:T(8,128)(2,1)}) custom-call(bf16[1,4,2,4,32,1024]{5,4,3,2,1,0:T(8,128)(2,1)} %bitcast.185, bf16[1,4,2,4,32,1024]{5,4,3,2,1,0:T(8,128)(2,1)} %bitcast.184, bf16[1,2,128,1024]{3,2,1,0:T(8,128)(2,1)} %fusion.18.refs_2_, ...), custom_call_target="tpu_custom_call" | custom-call | bytes 40000000 | tf_op jit(solution)/shard_map/pallas_call | solution.py:919
  682.5 3.1 constant_dynamic-update-slice_fusion
  685.6 8.4 bitcast_convert_fusion.3
  694.0 15.8 %shard_map.210 = (bf16[8,2,128,128]{3,2,1,0:T(8,128)(2,1)}, bf16[8,2,2,128,128]{4,3,2,1,0:T(8,128)(2,1)}) custom-call(s32[2]{0:T(128)} %broadcast_29_live_ref.2.live_ref, bf16[8,3,2,128,128]{4,3,2,1,0:T(8,128)(2,1)} %get-tuple-element.52.q_ref.k_ref.v_ref, bf16[8,3,2,128,128]{4,3,2,1,0:T(8,128)(2,1)} %get-tuple-element.52.q_ref.k_ref.v_ref, ...), custom_call_target="tpu_custom_call" | custom-call | flops 2684354560 | bytes 4194304 | tf_op jit(solution)/shard_map/pallas_call | solution.py:216
  709.8 56.1 %shard_map.211 = (bf16[3,32,1024]{2,1,0:T(8,128)(2,1)}, bf16[3,2,128,1024]{3,2,1,0:T(8,128)(2,1)}) custom-call(bf16[2,4,2,4,32,1024]{5,4,3,2,1,0:T(8,128)(2,1)} %bitcast.197, bf16[1,4,2,4,32,1024]{5,4,3,2,1,0:T(8,128)(2,1)} %bitcast.186, bf16[8,2,128,128]{3,2,1,0:T(8,128)(2,1)} %get-tuple-element.75.refs_2_, ...), custom_call_target="tpu_custom_call" | custom-call | bytes 60000000 | tf_op jit(solution)/shard_map/pallas_call | solution.py:919
  765.9 5.3 fusion.25
  771.2 4.7 bitcast_convert_fusion.2
  775.9 0.6 fusion.23
  776.7 0.7 fusion
  777.4 0.7 concatenate.25
  779.3 1.6 reshape.238.refs_1_
  780.9 43.4 %shard_map.212 = (bf16[6,16,1024]{2,1,0:T(8,128)(2,1)}, bf16[1,16,1024]{2,1,0:T(8,128)(2,1)}) custom-call(bf16[3,4,2,4,32,1024]{5,4,3,2,1,0:T(8,128)(2,1)} %bitcast.180, bf16[1,4,2,4,16,1024]{5,4,3,2,1,0:T(8,128)(2,1)} %reshape.238.refs_1_), custom_call_target="tpu_custom_call" | custom-call | bytes 120000000 | tf_op jit(solution)/shard_map/pallas_call | solution.py:919
  824.3 0.8 copy.110
  825.2 10.1 %convolution_bitcast_fusion = f32[2,512,1024]{2,1,0:T(8,128)} fusion(bf16[2,2,512,1024]{3,2,1,0:T(8,128)(2,1)} %constant_dynamic-update-slice_fusion, bf16[2,1024,1024,1]{2,1,3,0:T(8,128)(2,1)} %bitcast.195), kind=kOutput, calls=%fused_computation.23 | convolution fusion | flops 4294967296 | bytes 12582912 | tf_op jit(solution)/shard_map/koie,kde->oid/dot_general | solution.py:27
  835.3 1.4 add_add_fusion.3
  836.6 14.4 %shard_map.213 = bf16[4,4,32,1024]{3,2,1,0:T(8,128)(2,1)} custom-call(s32[16]{0:T(128)} %select_reduce_fusion.index_ref, bf16[3,32,1024]{2,1,0:T(8,128)(2,1)} %bitcast.201, bf16[3,32,1024]{2,1,0:T(8,128)(2,1)} %get-tuple-element.79.refs_1_, bf16[2,32,1024]{2,1,0:T(8,128)(2,1)} %get-tuple-element.80.refs_2_, bf16[4,32,1024]{2,1,0:T(8,128)(2,1)} %get-tuple-element.81.refs_3_, ...), custom_call_target="tpu_custom_call" | custom-call | bytes 50000000 | tf_op jit(solution)/shard_map/pallas_call | solution.py:971
  851.1 6.9 fusion.61
  858.0 0.7 multiply_subtract_fusion.1
  (123 shorter events, 6.9 us)
Async XLA Ops:
  0.6 88.4 %copy-start = (f32[2,16]{1,0:T(2,128)S(1)}, f32[2,16]{1,0:T(2,128)}, u32[]{:S(2)}) copy-start(f32[2,16]{1,0:T(2,128)} %param.14) | copy-start | bytes 388
  76.7 9.4 %copy-start.23 = (bf16[4,2,4,16,1024]{4,3,2,1,0:T(8,128)(2,1)S(1)}, bf16[4,2,4,16,1024]{4,3,2,1,0:T(8,128)(2,1)}, u32[]{:S(2)}) copy-start(bf16[4,2,4,16,1024]{4,3,2,1,0:T(8,128)(2,1)} %get-tuple-element.47) | copy-start | bytes 3145732
  76.7 267.2 %all-to-all-start = ((bf16[8,2,1,512,128]{4,3,2,1,0:T(8,128)(2,1)}), bf16[8,2,1,512,128]{4,3,2,1,0:T(8,128)(2,1)}, u32[]{:S(2)}, u32[]{:S(2)}) async-start(bf16[8,2,1,512,128]{4,3,2,1,0:T(8,128)(2,1)} %shard_map.196), calls=%async_computation | async-start | bytes 4194304 | tf_op jit(solution)/shard_map/all_to_all | solution.py:1074
  86.1 2.5 copy-start.1
  86.1 3.2 copy-start.30
  250.9 5.6 copy-start.14
  256.4 3.6 copy-start.2
  256.4 3.6 copy-start.7
  256.4 4.2 copy-start.11
  256.5 4.9 copy-start.17
  382.6 12.4 %slice-start = ((s8[8388608]{0:T(1024)(128)(4,1)}), s8[4194304]{0:T(1024)(128)(4,1)S(1)}, s32[]{:S(2)}) async-start(s8[8388608]{0:T(1024)(128)(4,1)} %bitcast.207), calls=%async_computation.1 | async-start | bytes 8388608
  382.8 6.0 copy-start.25
  382.8 12.1 %slice-start.1 = ((s8[8388608]{0:T(1024)(128)(4,1)}), s8[4194304]{0:T(1024)(128)(4,1)S(1)}, s32[]{:S(2)}) async-start(s8[8388608]{0:T(1024)(128)(4,1)} %bitcast.207), calls=%async_computation.2 | async-start | bytes 8388608
  388.8 6.1 copy-start.31
  412.2 2.0 copy-start.9
  412.6 1.0 copy-start.12
  414.1 1.5 copy-start.19
  505.7 84.1 %copy-start.8 = (bf16[1,4,2,4,32,1024]{5,4,3,2,1,0:T(8,128)(2,1)S(1)}, bf16[1,4,2,4,32,1024]{5,4,3,2,1,0:T(8,128)(2,1)}, u32[]{:S(2)}) copy-start(bf16[1,4,2,4,32,1024]{5,4,3,2,1,0:T(8,128)(2,1)} %copy-done.7) | copy-start | bytes 6291460
  589.8 2.1 copy-start.15
  589.9 4.4 copy-start.10
  589.9 4.4 copy-start.20
  592.0 5.0 copy-start.13
  592.0 5.0 copy-start.22
  592.0 5.0 copy-start.24
  592.0 5.0 copy-start.26
  592.0 5.0 copy-start.32
  597.0 7.7 copy-start.3
  604.7 5.3 copy-start.4
  604.8 3.7 copy-start.16
  610.0 75.5 %copy-start.18 = (bf16[2,512,1024]{2,1,0:T(8,128)(2,1)S(1)}, bf16[2,512,1024]{2,1,0:T(8,128)(2,1)}, u32[]{:S(2)}) copy-start(bf16[2,512,1024]{2,1,0:T(8,128)(2,1)} %x_ref.1) | copy-start | bytes 6291460
  765.9 5.3 copy-start.21
  825.2 10.1 %copy-start.5 = (f32[2,128,1024]{2,1,0:T(8,128)S(1)}, f32[2,128,1024]{2,1,0:T(8,128)}, u32[]{:S(2)}) copy-start(f32[2,128,1024]{2,1,0:T(8,128)} %copy-done.4) | copy-start | bytes 3145732
  835.2 15.8 %copy-start.6 = (f32[4,128,1024]{2,1,0:T(8,128)S(1)}, f32[4,128,1024]{2,1,0:T(8,128)}, u32[]{:S(2)}) copy-start(f32[4,128,1024]{2,1,0:T(8,128)} %param.16) | copy-start | bytes 6291460
  851.1 6.9 copy-start.27
  851.1 6.9 copy-start.28
  851.1 6.9 copy-start.29
